TPU v7x, 128 devices: a whole 4x4x4 slice. The times are simulated.
128 devices in a mesh: horiz: 32 (over x_lo, y, z), tracer: 2 (over core), level: 2 (over x_hi).
Axes of the slice: x: 4 (x_hi: 2, x_lo: 2; x = x_hi * 2 + x_lo), y: 4, z: 4, core: 2. Of those that a mesh axis runs over, the one named last changes fastest.
Arguments:
- forward_init: float32 [32, 64, 128, 128], P('tracer', 'level', 'horiz'), may hold values from -6 to 6
- adjoint_init: float32 [32, 64, 128, 128], P('tracer', 'level', 'horiz'), may hold values from -6 to 6
- east_flow: float32 [64, 128, 128], P('level', 'horiz'), may hold values from -0.24 to 0.24
- north_flow: float32 [64, 128, 128], P('level', 'horiz'), may hold values from -0.24 to 0.24
- mixing: float32 [63, 128, 128], P(None, 'horiz'), may hold values from 0.05 to 5
- depth: int32 [128, 128], P('horiz'), may hold values from 32 to 64
- color: int32 [128, 128], P('horiz'), may hold values from 0 to 31
- fold: int32 [128], replicated, may hold values from 0 to 127, each once
Outputs:
- forward_final: float32 [32, 64, 128, 128], P('tracer', 'level', 'horiz')
- adjoint_final: float32 [32, 64, 128, 128], P('tracer', 'level', 'horiz')
- sensitivity: float32 [64, 128, 128], P('level', 'horiz')
Inputs may be any that keep to these rules, and one draw needn't show every extreme that they name: `fold`: each column number appears exactly once.
All inputs are finite; a program needn't handle non-finite values.
Results may differ from a plain program's by a relative error of at most 0.0003.
Values sent between devices are 32-bit elements; how exact they have to be, the bound alone decides.
No kernel may reach another device: no remote copies, remote signals or barrier semaphores. Data moves between devices by JAX's collectives and lax.ppermute only.
A program may use at most 256 MiB of HBM per device.

v0:
```python
import jax
import jax.numpy as jnp
from jax import lax
from jax.sharding import PartitionSpec as P

STEPS = 4


def padded_2(cells, sides, width):
    for axis, dim in sides:
        count = lax.axis_size(axis)
        ends = count - 1
        head = lax.slice_in_dim(cells, 0, width, axis=dim)
        tail = lax.slice_in_dim(cells, cells.shape[dim] - width, cells.shape[dim], axis=dim)
        cells = jnp.concatenate(
            [
                lax.ppermute(tail, axis, [(i, (i + 1) % count) for i in range(ends)]),
                cells,
                lax.ppermute(head, axis, [((i + 1) % count, i) for i in range(ends)]),
            ],
            axis=dim,
        )
    return cells


def from_behind(array, axis, by):
    size = lax.axis_size(axis)
    pairs = [(i, i + by) for i in range(size) if 0 <= i + by < size]
    return lax.ppermute(array, axis, pairs)


def swapped(value, axis, apart):
    mask = 2**apart
    pairs = [(source, source ^ mask) for source in range(lax.axis_size(axis))]
    return lax.ppermute(value, axis, pairs)


def tri_solve(inside, diagonal, rhs):
    n_levels = diagonal.shape[0]
    factors = []
    partials = []
    prev_factor = None
    prev_partial = None
    for lev_no in range(n_levels):
        if lev_no == 0:
            inverse = 1.0 / diagonal[0]
            partial_value = rhs[0] * inverse
        else:
            inverse = 1.0 / (diagonal[lev_no] - inside[lev_no - 1] * prev_factor)
            partial_value = (rhs[lev_no] + inside[lev_no - 1] * prev_partial) * inverse
        if lev_no < n_levels - 1:
            prev_factor = inside[lev_no] * inverse
            factors.append(prev_factor)
        partials.append(partial_value)
        prev_partial = partial_value
    solved = partials[-1]
    result = [solved]
    for lev_no in range(n_levels - 2, -1, -1):
        solved = partials[lev_no] + factors[lev_no] * solved
        result.append(solved)
    return jnp.stack(result[::-1], axis=0)


def per_device(forward_init, adjoint_init, east_flow, north_flow, mixing, depth, color, fold):
    n_trc = forward_init.shape[0]
    n_rows = forward_init.shape[2]
    total_levels = mixing.shape[0] + 1
    is_top = lax.axis_index("horiz") == lax.axis_size("horiz") - 1
    lvl_index = lax.axis_index("level")
    first_id = lax.axis_index("tracer") * n_trc
    flows = jnp.stack([east_flow, north_flow])
    fwd_part, adj_part = (forward_init, adjoint_init)
    level_start = lvl_index * forward_init.shape[1]
    n_pairs = fwd_part.shape[0]
    n_levels = fwd_part.shape[1]
    tracers = jnp.transpose(jnp.concatenate([fwd_part, adj_part], 0), (1, 0, 2, 3))
    flow_sign = jnp.concatenate(
        [jnp.ones((n_pairs,), jnp.float32), -jnp.ones((n_pairs,), jnp.float32)]
    ).reshape(1, -1, 1, 1)
    tracer_ids = first_id + jnp.arange(n_pairs, dtype=jnp.int32)
    tracer_ids = jnp.concatenate([tracer_ids, tracer_ids])
    rim_width = 1
    depth_ext = padded_2(depth, (("horiz", 0),), 1)
    color_ext = jnp.pad(color, ((1, 1), (0, 0)))
    flow_south = from_behind(flows[1][:, n_rows - 1 : n_rows], "horiz", 1)
    east_ext = jnp.pad(flows[0], ((0, 0), (1, 1), (0, 0)))
    north_ext = jnp.concatenate([flow_south, flows[1], jnp.zeros_like(flow_south)], 1)
    flow_ext = jnp.stack([east_ext, north_ext])
    mixing_ext = jnp.pad(mixing, ((0, 0), (1, 1), (0, 0)))
    top_row = rim_width + n_rows
    folded_depth = jnp.take(depth[n_rows - 1], fold, axis=0)
    depth_ext = depth_ext.at[top_row].set(jnp.where(is_top, folded_depth, depth_ext[top_row]))
    level_ids = jnp.arange(total_levels, dtype=jnp.int32)[:, None, None]
    wet_all_ext = (level_ids < depth_ext[None]).astype(jnp.float32)
    wet_local_ext = lax.dynamic_slice_in_dim(wet_all_ext, level_start, n_levels, 0)
    tracers = tracers * wet_local_ext[:, None, rim_width : rim_width + n_rows]
    local_ids = jnp.arange(n_levels, dtype=jnp.int32)[:, None, None]
    not_first = (local_ids > 0).astype(jnp.float32)
    not_last = (local_ids < n_levels - 1).astype(jnp.float32)
    totals = jnp.zeros((n_levels, n_rows, east_flow.shape[2]), jnp.float32)
    for step_no in range(STEPS):
        padded = padded_2(tracers, (("horiz", 2),), 1)
        row_at = 1 + n_rows
        folded = jnp.take(padded[:, :, row_at - 1], fold, axis=2)
        padded = padded.at[:, :, row_at].set(jnp.where(is_top, folded, padded[:, :, row_at]))
        east_rows = flow_ext[0][:, 0 + 1 : 0 + 1 + n_rows]
        north_rows = flow_ext[1][:, 0 : 0 + n_rows + 1]
        wet_here = wet_local_ext[:, 1 : n_rows + 1]
        centre = padded[:, :, 1 : n_rows + 1]
        north_cell = padded[:, :, 2 : n_rows + 2]
        south_cell = padded[:, :, 0:n_rows]
        east_cell = jnp.roll(centre, -1, 3)
        west_cell = jnp.roll(centre, 1, 3)
        east_face = flow_sign * (east_rows * wet_here * jnp.roll(wet_here, -1, 2))[:, None]
        west_face = jnp.roll(east_face, 1, 3)
        vert_face = (
            flow_sign
            * (north_rows * wet_local_ext[:, 0 : n_rows + 1] * wet_local_ext[:, 1 : n_rows + 2])[
                :, None
            ]
        )
        north_face = vert_face[:, :, 1:]
        south_face = vert_face[:, :, :-1]
        source = (color_ext[0 + 1 : 0 + 1 + n_rows][None] == tracer_ids[:, None, None]).astype(
            jnp.float32
        )[None]
        explicit = (
            centre
            + jnp.maximum(west_face, 0.0) * west_cell
            + jnp.minimum(west_face, 0.0) * centre
            - jnp.maximum(east_face, 0.0) * centre
            - jnp.minimum(east_face, 0.0) * east_cell
            + jnp.maximum(south_face, 0.0) * south_cell
            + jnp.minimum(south_face, 0.0) * centre
            - jnp.maximum(north_face, 0.0) * centre
            - jnp.minimum(north_face, 0.0) * north_cell
            + source
        ) * wet_here[:, None]
        wet_all = wet_all_ext[:, 0 + 1 : 0 + 1 + n_rows]
        coupling = mixing_ext[:, 0 + 1 : 0 + 1 + n_rows] * wet_all[:-1] * wet_all[1:]
        zero_row = jnp.zeros_like(coupling[:1])
        coup_pad = jnp.concatenate([zero_row, coupling, zero_row], 0)
        coup_above = lax.dynamic_slice_in_dim(coup_pad, level_start, n_levels, 0)
        coup_below = lax.dynamic_slice_in_dim(coup_pad, level_start + 1, n_levels, 0)
        diagonal = 1.0 + coup_above * not_first + coup_below * not_last
        inside = coup_below[:-1]
        edge_index = jnp.where(lvl_index == 0, n_levels - 1, 0)
        unit_rhs = jnp.broadcast_to(
            (local_ids == edge_index).astype(jnp.float32)[:, None],
            (n_levels, 1, n_rows, east_rows.shape[2]),
        )
        solved = tri_solve(inside, diagonal, jnp.concatenate([explicit, unit_rhs], 1))
        own_edge = jnp.where(lvl_index == 0, solved[n_levels - 1], solved[0])
        far_edge = swapped(own_edge, "level", 0)
        cross_coup = jnp.where(lvl_index == 0, coup_below[n_levels - 1], coup_above[0])
        denominator = 1.0 + cross_coup * (own_edge[-1] + far_edge[-1])
        flux_q = cross_coup * (own_edge[:-1] - far_edge[:-1]) / denominator
        result = solved[:, :-1] - flux_q[None] * solved[:, -1:]
        next_row = jnp.where(lvl_index == 0, far_edge[:-1] + flux_q * far_edge[-1], 0.0)
        wet_pad = jnp.concatenate([wet_all, zero_row], 0)
        wet_next = lax.dynamic_slice_in_dim(wet_pad, level_start + 1, n_levels, 0)
        if_mask = wet_here * wet_next
        below_vals = jnp.concatenate([result[1:], next_row[None]], 0)
        differ = (below_vals - result) * if_mask[:, None]
        terms = jnp.sum(differ[:, :n_pairs] * differ[:, n_pairs:], axis=1)
        tracers, terms = (result, terms)
        totals = totals + terms
    tracers = jnp.transpose(tracers, (1, 0, 2, 3))
    fwd_out = tracers[:n_pairs]
    adj_out = tracers[n_pairs:]
    sens = lax.psum(totals, "tracer")
    return (fwd_out, adj_out, sens / STEPS)


def solution(mesh):
    placed = (
        P("tracer", "level", "horiz", None),
        P("tracer", "level", "horiz", None),
        P("level", "horiz", None),
        P("level", "horiz", None),
        P(None, "horiz", None),
        P("horiz", None),
        P("horiz", None),
        P(),
    )
    return jax.shard_map(
        per_device,
        mesh=mesh,
        in_specs=placed,
        out_specs=(
            P("tracer", "level", "horiz", None),
            P("tracer", "level", "horiz", None),
            P("level", "horiz", None),
        ),
        check_vma=False,
    )
```

profile of v0, /device:TPU:1, one launch (start us, length us, event | category | flops | bytes accessed | tf_op | source)
XLA Modules:
  0.0 248.2 jit_solution(12684039592056919300)
XLA Ops:
  8.0 4.4 %collective-permute-start = (s32[1,128]{1,0:T(1,128)S(1)}, s32[1,128]{1,0:T(1,128)S(1)}, u32[]{:S(2)}, u32[]{:S(2)}) collective-permute-start(s32[1,128]{1,0:T(1,128)S(1)} %get-tuple-element.359), channel_id=1, source_target_pairs={{0,4},{4,8},{8,12},{12,16},{16,20},{20,24},{24,28},{28,32},{32,36}... | collective-permute-start | bytes 1544 | tf_op jit(solution)/shard_map/ppermute | solution.py:17
  15.2 4.8 %collective-permute-start.4 = (f32[32,1,128]{2,0,1:T(8,128)}, f32[32,1,128]{2,0,1:T(8,128)}, u32[]{:S(2)}, u32[]{:S(2)}) collective-permute-start(f32[32,1,128]{2,0,1:T(8,128)} %slice.1833), channel_id=1, source_target_pairs={{0,4},{4,8},{8,12},{12,16},{16,20},{20,24},{24,28},{28,32},{32,36}... | collective-permute-start | bytes 49160 | tf_op jit(solution)/shard_map/ppermute | solution.py:29
  32.1 5.3 %collective-permute-start.2 = (f32[32,32,1,128]{3,1,2,0:T(8,128)}, f32[32,32,1,128]{3,1,2,0:T(8,128)}, u32[]{:S(2)}, u32[]{:S(2)}) collective-permute-start(f32[32,32,1,128]{3,1,2,0:T(8,128)} %get-tuple-element.346), channel_id=1, source_target_pairs={{0,4},{4,8},{8,12},{12,16},{16,20},{20,24},{24,28},{28,32},{32,36}... | collective-permute-start | bytes 1572872 | tf_op jit(solution)/shard_map/ppermute | solution.py:17
  39.4 2.8 %copy.990 = f32[32,32,128]{1,0,2:T(8,128)} copy(f32[32,32,128]{2,1,0:T(8,128)S(1)} %get-tuple-element.344) | data formatting | bytes 1048576 | tf_op jit(solution)/shard_map/squeeze | solution.py:104
  42.2 3.8 %gather_fusion.1 = f32[128,32,32]{2,1,0:T(8,128)} fusion(f32[32,32,128]{1,0,2:T(8,128)} %copy.990, s32[1024]{0:T(1024)} %copy-done.201), kind=kCustom, calls=%fused_computation.clone | custom fusion | bytes 1049088 | tf_op jit(solution)/shard_map/jit(_take)/gather | solution.py:104
  46.0 3.5 %copy.991 = f32[128,32,32]{0,2,1:T(8,128)} copy(f32[128,32,32]{2,1,0:T(8,128)} %gather_fusion.1) | data formatting | bytes 1048576 | tf_op jit(solution)/shard_map/jit(_take)/gather | solution.py:104
  56.2 4.3 %fusion.20 = (f32[32,32,4,128]{3,1,2,0:T(8,128)S(1)}, f32[32,32,4,128]{3,1,2,0:T(8,128)}) fusion(f32[32,32,6,128]{3,1,2,0:T(8,128)S(1)} %bitcast_dynamic-update-slice_fusion.3, f32[32,32,4,127]{3,1,2,0:T(8,128)S(1)} %get-tuple-element.330, f32[32,32,4,1]{3,1,2,0:T(8,128)S(1)} %get-tuple-element.332, f32[32,32,4,1]{3,1,2,0:T(8,128)S(1)} %get-tuple-element.331, ...), kind=kLoop, calls=%fused_computation.195 | loop fusion | flops 15728640 | bytes 21168256 | tf_op jit(solution)/shard_map/mul | solution.py:127
  63.6 2.8 %collective-permute-start.5 = (f32[33,4,128]{2,0,1:T(8,128)S(1)}, f32[33,4,128]{2,0,1:T(8,128)S(1)}, u32[]{:S(2)}, u32[]{:S(2)}) collective-permute-start(f32[33,4,128]{2,0,1:T(8,128)S(1)} %get-tuple-element.190), channel_id=1, source_target_pairs={{0,1},{1,0},{2,3},{3,2},{4,5},{5,4},{6,7},{7,6},{8,9},{9,8},{10,11... | collective-permute-start | bytes 202760 | tf_op jit(solution)/shard_map/ppermute | solution.py:35
  75.2 4.9 %collective-permute-start.6 = (f32[32,32,1,128]{3,1,2,0:T(8,128)}, f32[32,32,1,128]{3,1,2,0:T(8,128)}, u32[]{:S(2)}, u32[]{:S(2)}) collective-permute-start(f32[32,32,1,128]{3,1,2,0:T(8,128)} %get-tuple-element.343), channel_id=1, source_target_pairs={{0,4},{4,8},{8,12},{12,16},{16,20},{20,24},{24,28},{28,32},{32,36}... | collective-permute-start | bytes 1572872 | tf_op jit(solution)/shard_map/ppermute | solution.py:17
  80.2 2.8 %copy.1001 = f32[32,32,128]{1,0,2:T(8,128)} copy(f32[32,32,128]{2,1,0:T(8,128)S(1)} %get-tuple-element.341) | data formatting | bytes 1048576 | tf_op jit(solution)/shard_map/squeeze | solution.py:104
  83.0 3.7 %gather_fusion.2 = f32[128,32,32]{2,1,0:T(8,128)} fusion(f32[32,32,128]{1,0,2:T(8,128)} %copy.1001, s32[1024]{0:T(1024)} %copy-done.201), kind=kCustom, calls=%fused_computation.1.clone | custom fusion | bytes 1049088 | tf_op jit(solution)/shard_map/jit(_take)/gather | solution.py:104
  86.7 2.7 %copy.1002 = f32[128,32,32]{0,2,1:T(8,128)S(1)} copy(f32[128,32,32]{2,1,0:T(8,128)} %gather_fusion.2) | data formatting | bytes 1048576 | tf_op jit(solution)/shard_map/jit(_take)/gather | solution.py:104
  95.5 3.6 %fusion.14 = f32[32,32,4,128]{3,1,2,0:T(8,128)S(1)} fusion(f32[32,32,6,128]{3,1,2,0:T(8,128)S(1)} %bitcast_dynamic-update-slice_fusion.2, f32[32,32,4,127]{3,1,2,0:T(8,128)S(1)} %get-tuple-element.326, f32[32,32,4,1]{3,1,2,0:T(8,128)S(1)} %get-tuple-element.328, f32[32,32,4,1]{3,1,2,0:T(8,128)S(1)} %get-tuple-element.327, ...), kind=kLoop, calls=%fused_computation.186 | loop fusion | flops 15204352 | bytes 19071104 | tf_op jit(solution)/shard_map/mul | solution.py:127
  112.4 5.0 %collective-permute-start.9 = (f32[32,32,1,128]{3,1,2,0:T(8,128)}, f32[32,32,1,128]{3,1,2,0:T(8,128)}, u32[]{:S(2)}, u32[]{:S(2)}) collective-permute-start(f32[32,32,1,128]{3,1,2,0:T(8,128)} %get-tuple-element.340), channel_id=1, source_target_pairs={{0,4},{4,8},{8,12},{12,16},{16,20},{20,24},{24,28},{28,32},{32,36}... | collective-permute-start | bytes 1572872 | tf_op jit(solution)/shard_map/ppermute | solution.py:17
  117.4 2.8 %copy.1006 = f32[32,32,128]{1,0,2:T(8,128)} copy(f32[32,32,128]{2,1,0:T(8,128)S(1)} %get-tuple-element.338) | data formatting | bytes 1048576 | tf_op jit(solution)/shard_map/squeeze | solution.py:104
  120.2 3.8 %gather_fusion.3 = f32[128,32,32]{2,1,0:T(8,128)} fusion(f32[32,32,128]{1,0,2:T(8,128)} %copy.1006, s32[1024]{0:T(1024)} %copy-done.201), kind=kCustom, calls=%fused_computation.2.clone | custom fusion | bytes 1049088 | tf_op jit(solution)/shard_map/jit(_take)/gather | solution.py:104
  124.0 2.7 %copy.1007 = f32[128,32,32]{0,2,1:T(8,128)S(1)} copy(f32[128,32,32]{2,1,0:T(8,128)} %gather_fusion.3) | data formatting | bytes 1048576 | tf_op jit(solution)/shard_map/jit(_take)/gather | solution.py:104
  132.7 3.6 %fusion.8 = f32[32,32,4,128]{3,1,2,0:T(8,128)S(1)} fusion(f32[32,32,6,128]{3,1,2,0:T(8,128)S(1)} %bitcast_dynamic-update-slice_fusion.1, f32[32,32,4,127]{3,1,2,0:T(8,128)S(1)} %get-tuple-element.322, f32[32,32,4,1]{3,1,2,0:T(8,128)S(1)} %get-tuple-element.324, f32[32,32,4,1]{3,1,2,0:T(8,128)S(1)} %get-tuple-element.323, ...), kind=kLoop, calls=%fused_computation.177 | loop fusion | flops 15204352 | bytes 19071104 | tf_op jit(solution)/shard_map/mul | solution.py:127
  147.8 5.1 %collective-permute-start.12 = (f32[32,32,1,128]{3,1,2,0:T(8,128)}, f32[32,32,1,128]{3,1,2,0:T(8,128)}, u32[]{:S(2)}, u32[]{:S(2)}) collective-permute-start(f32[32,32,1,128]{3,1,2,0:T(8,128)} %get-tuple-element.337), channel_id=1, source_target_pairs={{0,4},{4,8},{8,12},{12,16},{16,20},{20,24},{24,28},{28,32},{32,36}... | collective-permute-start | bytes 1572872 | tf_op jit(solution)/shard_map/ppermute | solution.py:17
  153.6 2.9 %copy.1011 = f32[32,32,128]{1,0,2:T(8,128)} copy(f32[32,32,128]{2,1,0:T(8,128)S(1)} %get-tuple-element.335) | data formatting | bytes 1048576 | tf_op jit(solution)/shard_map/squeeze | solution.py:104
  156.5 3.7 %gather_fusion.4 = f32[128,32,32]{2,1,0:T(8,128)} fusion(f32[32,32,128]{1,0,2:T(8,128)} %copy.1011, s32[1024]{0:T(1024)} %copy-done.201), kind=kCustom, calls=%fused_computation.3.clone | custom fusion | bytes 1049088 | tf_op jit(solution)/shard_map/jit(_take)/gather | solution.py:104
  168.9 3.6 %fusion.2 = f32[32,32,4,128]{3,1,2,0:T(8,128)S(1)} fusion(f32[32,32,6,128]{3,1,2,0:T(8,128)S(1)} %bitcast_dynamic-update-slice_fusion, f32[32,32,4,127]{3,1,2,0:T(8,128)S(1)} %get-tuple-element.318, f32[32,32,4,1]{3,1,2,0:T(8,128)S(1)} %get-tuple-element.320, f32[32,32,4,1]{3,1,2,0:T(8,128)S(1)} %get-tuple-element.319, ...), kind=kLoop, calls=%fused_computation.168 | loop fusion | flops 15204352 | bytes 19071104 | tf_op jit(solution)/shard_map/mul | solution.py:127
  184.7 3.7 %fusion.42 = (f32[32,32,4,128]{3,1,2,0:T(8,128)S(1)}, f32[32,32,4,128]{3,1,2,0:T(8,128)S(1)}, f32[32,32,4,128]{3,1,2,0:T(8,128)S(1)}, f32[32,32,4,128]{3,1,2,0:T(8,128)S(1)}) fusion(f32[1,32,4,128]{3,1,2,0:T(8,128)S(1)} %copy-done.85, f32[31,32,4,128]{3,1,2,0:T(8,128)S(1)} %slice-done.1, f32[32,4,128]{2,1,0:T(4,128)S(1)} %copy-done.83, ...), kind=kLoop, calls=%fused_computation.230 | loop fusion | flops 10485760 | bytes 25755648 | tf_op jit(solution)/shard_map/mul | solution.py:164
  193.9 45.2 %all-reduce.3.cloned.1.call-done = f32[32,4,128]{0,2,1:T(8,128)} async-done(((f32[32,4,128]{0,2,1:T(8,128)}), f32[32,4,128]{0,2,1:T(8,128)}) %all-reduce.3.cloned.1.call-update) | async-done | bytes 65552 | tf_op jit(solution)/shard_map/psum | solution.py:171
  (670 shorter events, 98.0 us)
Async XLA Ops:
  7.2 19.9 %copy-start.206 = (s32[4,128]{1,0:T(4,128)S(1)}, s32[4,128]{1,0:T(4,128)}, u32[]{:S(2)}) copy-start(s32[4,128]{1,0:T(4,128)} %param.25) | copy-start | bytes 6148
  7.2 19.9 %copy-start.207 = (s32[128]{0:T(128)S(1)}, s32[128]{0:T(128)}, u32[]{:S(2)}) copy-start(s32[128]{0:T(128)} %param.27) | copy-start | bytes 1540
  7.2 17.9 %copy-start.16 = (f32[16,32,4,128]{3,2,1,0:T(4,128)S(1)}, f32[16,32,4,128]{3,2,1,0:T(4,128)}, u32[]{:S(2)}) copy-start(f32[16,32,4,128]{3,2,1,0:T(4,128)} %param.21) | copy-start | bytes 3145732
  7.2 231.9 %all-reduce.3.cloned.1.call-start = ((), (), s32[]{:S(2)}) async-start(), calls=%async_computation | async-start | bytes 524288 | tf_op jit(solution)/shard_map/psum | solution.py:171
  8.0 19.0 %collective-permute-start = (s32[1,128]{1,0:T(1,128)S(1)}, s32[1,128]{1,0:T(1,128)S(1)}, u32[]{:S(2)}, u32[]{:S(2)}) collective-permute-start(s32[1,128]{1,0:T(1,128)S(1)} %get-tuple-element.359), channel_id=1, source_target_pairs={{0,4},{4,8},{8,12},{12,16},{16,20},{20,24},{24,28},{28,32},{32,36}... | collective-permute-start | bytes 1544 | tf_op jit(solution)/shard_map/ppermute | solution.py:17
  12.4 14.6 %collective-permute-start.1 = (s32[1,128]{1,0:T(1,128)S(1)}, s32[1,128]{1,0:T(1,128)S(1)}, u32[]{:S(2)}, u32[]{:S(2)}) collective-permute-start(s32[1,128]{1,0:T(1,128)S(1)} %get-tuple-element.360), channel_id=1, source_target_pairs={{4,0},{8,4},{12,8},{16,12},{20,16},{24,20},{28,24},{32,28},{36,32}... | collective-permute-start | bytes 1544 | tf_op jit(solution)/shard_map/ppermute | solution.py:19
  14.5 8.8 %copy-start.81 = (f32[32,4,128]{2,0,1:T(8,128)}, f32[32,4,128]{2,0,1:T(8,128)S(1)}, u32[]{:S(2)}) copy-start(f32[32,4,128]{2,0,1:T(8,128)S(1)} %copy.994) | copy-start | bytes 196612
  15.2 34.9 %collective-permute-start.4 = (f32[32,1,128]{2,0,1:T(8,128)}, f32[32,1,128]{2,0,1:T(8,128)}, u32[]{:S(2)}, u32[]{:S(2)}) collective-permute-start(f32[32,1,128]{2,0,1:T(8,128)} %slice.1833), channel_id=1, source_target_pairs={{0,4},{4,8},{8,12},{12,16},{16,20},{20,24},{24,28},{28,32},{32,36}... | collective-permute-start | bytes 49160 | tf_op jit(solution)/shard_map/ppermute | solution.py:29
  28.3 9.6 %copy-start.18 = (f32[65,4,128]{2,0,1:T(8,128)}, f32[65,4,128]{2,0,1:T(8,128)S(1)}, u32[]{:S(2)}) copy-start(f32[65,4,128]{2,0,1:T(8,128)S(1)} %pad_maximum_fusion.9) | copy-start | bytes 399364
  30.8 20.9 %collective-permute-start.3 = (f32[32,32,1,128]{3,1,2,0:T(8,128)}, f32[32,32,1,128]{3,1,2,0:T(8,128)S(1)}, u32[]{:S(2)}, u32[]{:S(2)}) collective-permute-start(f32[32,32,1,128]{3,1,2,0:T(8,128)} %get-tuple-element.345), channel_id=1, source_target_pairs={{4,0},{8,4},{12,8},{16,12},{20,16},{24,20},{28,24},{32,28},{36,32}... | collective-permute-start | bytes 1572872 | tf_op jit(solution)/shard_map/ppermute | solution.py:19
  32.1 19.6 %collective-permute-start.2 = (f32[32,32,1,128]{3,1,2,0:T(8,128)}, f32[32,32,1,128]{3,1,2,0:T(8,128)}, u32[]{:S(2)}, u32[]{:S(2)}) collective-permute-start(f32[32,32,1,128]{3,1,2,0:T(8,128)} %get-tuple-element.346), channel_id=1, source_target_pairs={{0,4},{4,8},{8,12},{12,16},{16,20},{20,24},{24,28},{28,32},{32,36}... | collective-permute-start | bytes 1572872 | tf_op jit(solution)/shard_map/ppermute | solution.py:17
  37.8 11.6 %copy-start.6 = (f32[32,32,4,128]{3,1,2,0:T(8,128)}, f32[32,32,4,128]{3,1,2,0:T(8,128)S(1)}, u32[]{:S(2)}) copy-start(f32[32,32,4,128]{3,1,2,0:T(8,128)S(1)} %broadcast_multiply_fusion.1) | copy-start | bytes 6291460
  63.6 5.3 %collective-permute-start.5 = (f32[33,4,128]{2,0,1:T(8,128)S(1)}, f32[33,4,128]{2,0,1:T(8,128)S(1)}, u32[]{:S(2)}, u32[]{:S(2)}) collective-permute-start(f32[33,4,128]{2,0,1:T(8,128)S(1)} %get-tuple-element.190), channel_id=1, source_target_pairs={{0,1},{1,0},{2,3},{3,2},{4,5},{5,4},{6,7},{7,6},{8,9},{9,8},{10,11... | collective-permute-start | bytes 202760 | tf_op jit(solution)/shard_map/ppermute | solution.py:35
  69.7 21.8 %copy-start.194 = (f32[1,4,128]{2,0,1:T(1,128)}, f32[1,4,128]{2,0,1:T(1,128)S(1)}, u32[]{:S(2)}) copy-start(f32[1,4,128]{2,0,1:T(1,128)S(1)} %get-tuple-element.189) | copy-start | bytes 6148
  74.0 15.5 %collective-permute-start.7 = (f32[32,32,1,128]{3,1,2,0:T(8,128)}, f32[32,32,1,128]{3,1,2,0:T(8,128)}, u32[]{:S(2)}, u32[]{:S(2)}) collective-permute-start(f32[32,32,1,128]{3,1,2,0:T(8,128)} %get-tuple-element.342), channel_id=1, source_target_pairs={{4,0},{8,4},{12,8},{16,12},{20,16},{24,20},{28,24},{32,28},{36,32}... | collective-permute-start | bytes 1572872 | tf_op jit(solution)/shard_map/ppermute | solution.py:19
  75.2 14.2 %collective-permute-start.6 = (f32[32,32,1,128]{3,1,2,0:T(8,128)}, f32[32,32,1,128]{3,1,2,0:T(8,128)}, u32[]{:S(2)}, u32[]{:S(2)}) collective-permute-start(f32[32,32,1,128]{3,1,2,0:T(8,128)} %get-tuple-element.343), channel_id=1, source_target_pairs={{0,4},{4,8},{8,12},{12,16},{16,20},{20,24},{24,28},{28,32},{32,36}... | collective-permute-start | bytes 1572872 | tf_op jit(solution)/shard_map/ppermute | solution.py:17
  101.4 4.9 %collective-permute-start.8 = (f32[33,4,128]{2,0,1:T(8,128)S(1)}, f32[33,4,128]{2,0,1:T(8,128)S(1)}, u32[]{:S(2)}, u32[]{:S(2)}) collective-permute-start(f32[33,4,128]{2,0,1:T(8,128)S(1)} %get-tuple-element.157), channel_id=1, source_target_pairs={{0,1},{1,0},{2,3},{3,2},{4,5},{5,4},{6,7},{7,6},{8,9},{9,8},{10,11... | collective-permute-start | bytes 202760 | tf_op jit(solution)/shard_map/ppermute | solution.py:35
  111.1 15.6 %collective-permute-start.10 = (f32[32,32,1,128]{3,1,2,0:T(8,128)}, f32[32,32,1,128]{3,1,2,0:T(8,128)}, u32[]{:S(2)}, u32[]{:S(2)}) collective-permute-start(f32[32,32,1,128]{3,1,2,0:T(8,128)} %get-tuple-element.339), channel_id=1, source_target_pairs={{4,0},{8,4},{12,8},{16,12},{20,16},{24,20},{28,24},{32,28},{36,32}... | collective-permute-start | bytes 1572872 | tf_op jit(solution)/shard_map/ppermute | solution.py:19
  112.4 14.3 %collective-permute-start.9 = (f32[32,32,1,128]{3,1,2,0:T(8,128)}, f32[32,32,1,128]{3,1,2,0:T(8,128)}, u32[]{:S(2)}, u32[]{:S(2)}) collective-permute-start(f32[32,32,1,128]{3,1,2,0:T(8,128)} %get-tuple-element.340), channel_id=1, source_target_pairs={{0,4},{4,8},{8,12},{12,16},{16,20},{20,24},{24,28},{28,32},{32,36}... | collective-permute-start | bytes 1572872 | tf_op jit(solution)/shard_map/ppermute | solution.py:17
  138.6 4.9 %collective-permute-start.11 = (f32[33,4,128]{2,0,1:T(8,128)S(1)}, f32[33,4,128]{2,0,1:T(8,128)S(1)}, u32[]{:S(2)}, u32[]{:S(2)}) collective-permute-start(f32[33,4,128]{2,0,1:T(8,128)S(1)} %get-tuple-element.126), channel_id=1, source_target_pairs={{0,1},{1,0},{2,3},{3,2},{4,5},{5,4},{6,7},{7,6},{8,9},{9,8},{10,11... | collective-permute-start | bytes 202760 | tf_op jit(solution)/shard_map/ppermute | solution.py:35
  145.2 8.4 %copy-start.5 = (f32[32,32,4,128]{3,1,2,0:T(8,128)}, f32[32,32,4,128]{3,1,2,0:T(8,128)S(1)}, u32[]{:S(2)}) copy-start(f32[32,32,4,128]{3,1,2,0:T(8,128)S(1)} %slice_subtract_fusion.1) | copy-start | bytes 6291460
  146.5 16.3 %collective-permute-start.13 = (f32[32,32,1,128]{3,1,2,0:T(8,128)}, f32[32,32,1,128]{3,1,2,0:T(8,128)}, u32[]{:S(2)}, u32[]{:S(2)}) collective-permute-start(f32[32,32,1,128]{3,1,2,0:T(8,128)} %get-tuple-element.336), channel_id=1, source_target_pairs={{4,0},{8,4},{12,8},{16,12},{20,16},{24,20},{28,24},{32,28},{36,32}... | collective-permute-start | bytes 1572872 | tf_op jit(solution)/shard_map/ppermute | solution.py:19
  147.8 15.0 %collective-permute-start.12 = (f32[32,32,1,128]{3,1,2,0:T(8,128)}, f32[32,32,1,128]{3,1,2,0:T(8,128)}, u32[]{:S(2)}, u32[]{:S(2)}) collective-permute-start(f32[32,32,1,128]{3,1,2,0:T(8,128)} %get-tuple-element.337), channel_id=1, source_target_pairs={{0,4},{4,8},{8,12},{12,16},{16,20},{20,24},{24,28},{28,32},{32,36}... | collective-permute-start | bytes 1572872 | tf_op jit(solution)/shard_map/ppermute | solution.py:17
  174.8 5.2 %collective-permute-start.14 = (f32[33,4,128]{2,0,1:T(8,128)S(1)}, f32[33,4,128]{2,0,1:T(8,128)S(1)}, u32[]{:S(2)}, u32[]{:S(2)}) collective-permute-start(f32[33,4,128]{2,0,1:T(8,128)S(1)} %get-tuple-element.95), channel_id=1, source_target_pairs={{0,1},{1,0},{2,3},{3,2},{4,5},{5,4},{6,7},{7,6},{8,9},{9,8},{10,11... | collective-permute-start | bytes 202760 | tf_op jit(solution)/shard_map/ppermute | solution.py:35
  (203 other events, 852.7 us)
Sparse Core Ops, SparseCore 0:
  191.0 48.0 all-reduce.2
where the time goes:
time: 253 us; the launch traced here: 248 us
  local copies, waits for them, and re-layouts  75.2 us (30%)
  other arithmetic  63 us (25%)
  waiting for transfers between devices  46.8 us (18%)
  starting transfers between devices  44.4 us (18%)
  between operations  18.9 us (7%)
    psum x1, waiting for transfers between devices, per_device(): sens = lax.psum(totals, 'tracer')  45.2 us
    gather x8, local copies, waits for them, and re-layouts, per_device(): folded = jnp.take(padded[:, :, row_at - 1], fold, axis=2)  26.4 us
    ppermute x5, starting transfers between devices, padded_2(): lax.ppermute(tail, axis, [(i, (i + 1) % count) for i in range(ends)])  24.7 us
    unnamed x478, local copies, waits for them, and re-layouts  18.5 us
    squeeze x8, local copies, waits for them, and re-layouts, per_device(): folded = jnp.take(padded[:, :, row_at - 1], fold, axis=2)  16.3 us
    mul x4, other arithmetic, per_device(): (centre + jnp.maximum(west_face, 0.0) * west_cell + jnp.minimum(west_face...  15.1 us
    ppermute x4, starting transfers between devices, swapped(): return lax.ppermute(value, axis, pairs)  8.52 us
    unnamed x72, other arithmetic  8.5 us
  transfers between devices with their start and end apart: 16, of which 4 were waited for; matrix products, arithmetic and copies ran while one was open for 27% of the time, Pallas kernels for 0%

commit v1 on v0

v1 whole, which is shorter than its diff:
```python
import functools
import jax
import jax.numpy as jnp
from jax import lax
from jax.experimental import pallas as pl
from jax.experimental.pallas import tpu as pltpu
from jax.sharding import PartitionSpec as P

STEPS = 4
LANES = 128
C0F, C0A, CWF, CWA, CEF, CEA, CSF, CSA, CNF, CNA, UP, WI, BACK = range(13)
E0F, E0A, ESF, ESA, T0F, T0A, TNF, TNA = range(8)
F32 = jnp.float32
UNROLL = 2


def order(flags_ref, n_lev):
    bottom = flags_ref[0]
    return bottom * (n_lev - 1), 1 - 2 * bottom


def west(v):
    return pltpu.roll(v, 1, 1)


def east(v):
    return pltpu.roll(v, LANES - 1, 1)


def spread(v):
    return jnp.broadcast_to(v, (8, LANES))


def pick(c_ref, which, lev, row):
    return spread(c_ref[which, lev, row : row + 1, :])


def sweep(flags_ref, n_lev, n_pair, rows, put, last):
    k0, dk = order(flags_ref, n_lev)
    halves = n_pair // 8
    zero = jnp.zeros((8, LANES), F32)

    def body(s, carry):
        lev = k0 + dk * s
        out = []
        at = 0
        for i, (coef, src, center, south, north) in enumerate(rows):
            up = coef(UP, lev)
            wi = coef(WI, lev)
            srcs = [src(g) * wi for g in range(halves)]
            for kind in range(2):
                c0, cw, ce, cs, cn = (coef(base + kind, lev) for base in (C0F, CWF, CEF, CSF, CNF))
                for g in range(halves):
                    c = center(lev, kind, g)
                    v = c0 * c + cw * west(c)
                    v = v + (ce * east(c) + cs * south(lev, kind, g))
                    v = v + (cn * north(lev, kind, g) + srcs[g])
                    v = v + up * carry[at]
                    put(lev, i, kind, g, v)
                    out.append(v)
                    at += 1
        return tuple(out)

    final = lax.fori_loop(0, n_lev, body, (zero,) * (len(rows) * 2 * halves), unroll=UNROLL)
    at = 0
    for i in range(len(rows)):
        for kind in range(2):
            for g in range(halves):
                last(i, kind, g, final[at])
                at += 1


def back(flags_ref, n_lev, n_pair, rows, wx_ref, far_ref, c_ref, part, put, acc_in, acc_out):
    bottom = flags_ref[0]
    k0, dk = order(flags_ref, n_lev)
    halves = n_pair // 8
    mid = k0 + dk * (n_lev - 1)
    own, far = [], []
    for i, row in enumerate(rows):
        wa, wb, ff = (spread(wx_ref[j, row : row + 1, :]) for j in range(3))
        for kind in range(2):
            for g in range(halves):
                p_far = far_ref[row, pl.ds((kind * halves + g) * 8, 8), :]
                x = wa * part(mid, i, kind, g) + wb * p_far
                own.append(x)
                far.append(p_far + ff * x)

    def tally(s, now, nxt):
        at = jnp.where(bottom == 0, s + 1, n_lev - 1 - s)
        for i in range(len(rows)):
            b = i * 2 * halves
            total = acc_in(at, i)
            for g in range(halves):
                f, a = b + g, b + halves + g
                total = total + (nxt[f] - now[f]) * (nxt[a] - now[a])
            acc_out(at, i, total)

    def store(lev, xs):
        at = 0
        for i in range(len(rows)):
            for kind in range(2):
                for g in range(halves):
                    put(lev, i, kind, g, xs[at])
                    at += 1

    tally(n_lev - 1, own, far)
    store(mid, own)

    def body(q, nxt):
        s = n_lev - 2 - q
        lev = k0 + dk * s
        now = []
        at = 0
        for i, row in enumerate(rows):
            f = pick(c_ref, BACK, lev, row)
            for kind in range(2):
                for g in range(halves):
                    now.append(part(lev, i, kind, g) + f * nxt[at])
                    at += 1
        tally(s, now, nxt)
        store(lev, now)
        return tuple(now)

    lax.fori_loop(0, n_lev - 1, body, tuple(own), unroll=UNROLL)


def fold_rows(flags_ref, fold_ref, nf_ref, get, mf_ref, n_lev, n_pair):
    @pl.when(flags_ref[1] == 1)
    def _():
        where_to = spread(fold_ref[0:1, :])

        def body(lev, _):
            n3 = spread(nf_ref[lev, 3:4, :])
            for g in range(n_pair // 8):
                f = jnp.take_along_axis(get(lev, 0, g), where_to, axis=1)
                a = jnp.take_along_axis(get(lev, 1, g), where_to, axis=1)
                mf_ref[lev, pl.ds(g * 8, 8), :] = jnp.where(n3 < 0.0, f, a)
            return 0

        lax.fori_loop(0, n_lev, body, 0)


def rows_at(ref, row, lev, kind, g, halves):
    return ref[lev, row, pl.ds((kind * halves + g) * 8, 8), :]


def send_first(n_lev, n_pair, n_rows, flags_ref, f_ref, a_ref, nf_ref, depth_ref, north_ref, south_ref):
    stride = n_lev * n_rows
    first = flags_ref[0] * n_lev
    depth = depth_ref[...]

    def body(lev, _):
        wet = jnp.where(first + lev < depth, 1.0, 0.0)
        w0 = spread(wet[0:1])
        w3 = spread(wet[n_rows - 1 : n_rows])
        n3 = spread(nf_ref[lev, n_rows - 1 : n_rows, :])
        for g in range(n_pair // 8):
            at = g * 8 * stride + lev * n_rows
            low, high = pl.ds(at, 8, stride=stride), pl.ds(at + n_rows - 1, 8, stride=stride)
            to = pl.ds(g * 8, 8)
            north_ref[lev, to, :] = jnp.where(n3 > 0.0, f_ref[high, :], a_ref[high, :]) * w3
            south_ref[lev, to, :] = f_ref[low, :] * w0
            south_ref[n_lev + lev, to, :] = a_ref[low, :] * w0
        return 0

    lax.fori_loop(0, n_lev, body, 0, unroll=UNROLL)
    for lev in range(n_lev):
        page, line = n_lev + lev // n_pair, lev % n_pair
        north_ref[page, line : line + 1, :] = nf_ref[lev, n_rows - 1 : n_rows, :]
    high = depth[n_rows - 1 : n_rows].astype(F32)
    low = depth[0:1].astype(F32)
    north_ref[n_lev + n_lev // n_pair] = jnp.broadcast_to(high, (n_pair, LANES))
    south_ref[2 * n_lev] = jnp.broadcast_to(low, (n_pair, LANES))


def prepare(
    n_lev, n_pair, n_rows, flags_ref, f_ref, a_ref, ef_ref, nf_ref, mix_ref, depth_ref, color_ref, fold_ref,
    xe_ref, xi_ref, pi_ref, c_ref, wx_ref, hot_ref, mf_ref, inv_ref,
):
    halves = n_pair // 8
    stride = n_lev * n_rows
    bottom = flags_ref[0]
    first = bottom * n_lev
    k0, dk = order(flags_ref, n_lev)
    depth = depth_ref[...]

    def lay(lev, _):
        wet = jnp.where(first + lev < depth, 1.0, 0.0)
        for row in range(n_rows):
            w = spread(wet[row : row + 1])
            to_ref, line = (xe_ref, row // 3) if row in (0, 3) else (xi_ref, row - 1)
            for kind, from_ref in enumerate((f_ref, a_ref)):
                for g in range(halves):
                    v = from_ref[pl.ds(g * 8 * stride + lev * n_rows + row, 8, stride=stride), :]
                    to_ref[lev, line, pl.ds((kind * halves + g) * 8, 8), :] = v * w
        return 0

    lax.fori_loop(0, n_lev, lay, 0, unroll=UNROLL)

    def coupling(k):
        inner = jnp.where((k >= 0) & (k < 2 * n_lev - 1), 1.0, 0.0)
        m = mix_ref[jnp.clip(k, 0, 2 * n_lev - 2)]
        return m * jnp.where(k + 1 < depth, inner, 0.0)

    def eliminate(s, carry):
        own_f, far_f = carry
        k = bottom * (2 * n_lev - 1) + dk * s
        prev, nxt = coupling(k - 1 + bottom), coupling(k - bottom)
        inverse = 1.0 / (1.0 + nxt + prev * (1.0 - own_f))
        lev = k0 + dk * s
        inv_ref[lev] = inverse
        c_ref[UP, lev] = prev * inverse
        own_f = nxt * inverse
        c_ref[BACK, lev] = own_f
        k = (1 - bottom) * (2 * n_lev - 1) - dk * s
        prev, nxt = coupling(k - bottom), coupling(k - 1 + bottom)
        far_f = nxt / (1.0 + nxt + prev * (1.0 - far_f))
        return own_f, far_f

    one = jnp.zeros((n_rows, LANES), F32)
    own_f, far_f = lax.fori_loop(0, n_lev, eliminate, (one, one), unroll=UNROLL)
    meet = 1.0 / (1.0 - own_f * far_f)
    wx_ref[0] = meet
    wx_ref[1] = own_f * meet
    wx_ref[2] = far_f

    depth_east = east(depth)
    depth_north = jnp.concatenate([depth[1:], jnp.zeros((1, LANES), jnp.int32)], 0)

    def coefs(lev, _):
        k = first + lev
        wet = jnp.where(k < depth, 1.0, 0.0)
        inverse = inv_ref[lev]
        e = ef_ref[lev] * wet * jnp.where(k < depth_east, 1.0, 0.0)
        n = nf_ref[lev] * wet * jnp.where(k < depth_north, 1.0, 0.0)
        w = west(e)
        s = jnp.concatenate([jnp.zeros((1, LANES), F32), n[:-1]], 0)
        plus = [jnp.maximum(v, 0.0) for v in (w, e, s, n)]
        minus = [jnp.maximum(-v, 0.0) for v in (w, e, s, n)]
        c_ref[C0F, lev] = (1.0 - minus[0] - plus[1] - minus[2] - plus[3]) * inverse
        c_ref[C0A, lev] = (1.0 - plus[0] - minus[1] - plus[2] - minus[3]) * inverse
        c_ref[CWF, lev], c_ref[CWA, lev] = plus[0] * inverse, minus[0] * inverse
        c_ref[CEF, lev], c_ref[CEA, lev] = minus[1] * inverse, plus[1] * inverse
        c_ref[CSF, lev], c_ref[CSA, lev] = plus[2] * inverse, minus[2] * inverse
        c_ref[CNF, lev], c_ref[CNA, lev] = minus[3] * inverse, plus[3] * inverse
        c_ref[WI, lev] = wet * inverse
        return 0

    lax.fori_loop(0, n_lev, coefs, 0, unroll=UNROLL)

    ids = lax.broadcasted_iota(jnp.int32, (n_pair, LANES), 0) + flags_ref[3]
    for row in range(n_rows):
        hot_ref[row] = jnp.where(color_ref[row : row + 1, :] == ids, 1.0, 0.0)

    inner_sweep(n_lev, n_pair, flags_ref, xe_ref, xi_ref, c_ref, hot_ref, pi_ref)
    fold_rows(
        flags_ref, fold_ref, nf_ref, lambda lev, kind, g: rows_at(xe_ref, 1, lev, kind, g, halves), mf_ref, n_lev, n_pair
    )


def inner_sweep(n_lev, n_pair, flags_ref, xe_ref, xi_ref, c_ref, hot_ref, pi_ref):
    halves = n_pair // 8

    def row(number):
        line = number - 1

        def at(ref, which):
            return lambda lev, kind, g: rows_at(ref, which, lev, kind, g, halves)

        return (
            lambda which, lev: pick(c_ref, which, lev, number),
            lambda g: hot_ref[number, pl.ds(g * 8, 8), :],
            at(xi_ref, line),
            at(xe_ref, 0) if line == 0 else at(xi_ref, 0),
            at(xi_ref, 1) if line == 0 else at(xe_ref, 1),
        )

    def put(lev, i, kind, g, v):
        pi_ref[lev, i, pl.ds((kind * halves + g) * 8, 8), :] = v

    sweep(flags_ref, n_lev, n_pair, [row(1), row(2)], put, lambda *_: None)


def edge_sweep(
    is_first, n_lev, n_pair, flags_ref, xe_ref, xi_ref, pi_ref, c_ref, hot_ref, mf_ref, ms_ref, mn_ref, ec_in, *rest
):
    halves = n_pair // 8
    is_top = flags_ref[1] == 1
    if is_first:
        nf_ref, depth_ref, fold_ref = ec_in
        pe_ref, edge_ref, ec_ref, fs_ref = rest
        first = flags_ref[0] * n_lev
        depth = depth_ref[...]
        own0, own3 = depth[0:1], depth[3:4]
        page = n_lev + n_lev // n_pair
        south_depth = ms_ref[page, 0:1, :]
        folded = jnp.take_along_axis(spread(own3.astype(F32)), spread(fold_ref[0:1, :]), axis=1)[0:1]
        north_depth = jnp.where(is_top, folded, mn_ref[2 * n_lev, 0:1, :])
        open_south = jnp.where(flags_ref[2] == 1, 0.0, 1.0)
        for lev in range(n_lev):
            k = first + lev
            kf = k.astype(F32)
            raw = ms_ref[n_lev + lev // n_pair, lev % n_pair : lev % n_pair + 1, :]
            fs_ref[lev] = spread(raw)
            wi0, wi3 = c_ref[WI, lev, 0:1, :], c_ref[WI, lev, 3:4, :]
            s = raw * jnp.where(kf < south_depth, 1.0, 0.0) * open_south * wi0
            n = nf_ref[lev, 3:4, :] * jnp.where(kf < north_depth, 1.0, 0.0) * wi3
            sp, sm, np_, nm = (jnp.maximum(v, 0.0) for v in (s, -s, n, -n))
            ec_ref[E0F, lev] = spread(c_ref[C0F, lev, 0:1, :] - sm)
            ec_ref[E0A, lev] = spread(c_ref[C0A, lev, 0:1, :] - sp)
            ec_ref[ESF, lev] = spread(sp)
            ec_ref[ESA, lev] = spread(sm)
            ec_ref[T0F, lev] = spread(c_ref[C0F, lev, 3:4, :] - np_)
            ec_ref[T0A, lev] = spread(c_ref[C0A, lev, 3:4, :] - nm)
            ec_ref[TNF, lev] = spread(nm)
            ec_ref[TNA, lev] = spread(np_)
    else:
        ec_ref = ec_in
        pe_ref, edge_ref = rest

    low = {C0F: E0F, C0A: E0A, CSF: ESF, CSA: ESA}
    high = {C0F: T0F, C0A: T0A, CNF: TNF, CNA: TNA}

    def coef(number, table):
        def get(which, lev):
            return ec_ref[table[which], lev] if which in table else pick(c_ref, which, lev, number)

        return get

    def north_of_edge(lev, kind, g):
        to = pl.ds(g * 8, 8)
        if is_first:
            n3 = spread(nf_ref[lev, 3:4, :])
            come = jnp.where(n3 < 0.0, mn_ref[lev, to, :], mn_ref[n_lev + lev, to, :])
        else:
            come = mn_ref[lev, to, :]
        return jnp.where(is_top, mf_ref[lev, to, :], come)

    def at(ref, which):
        return lambda lev, kind, g: rows_at(ref, which, lev, kind, g, halves)

    rows = [
        (
            coef(0, low),
            lambda g: hot_ref[0, pl.ds(g * 8, 8), :],
            at(xe_ref, 0),
            lambda lev, kind, g: ms_ref[lev, pl.ds(g * 8, 8), :],
            at(xi_ref, 0),
        ),
        (
            coef(3, high),
            lambda g: hot_ref[3, pl.ds(g * 8, 8), :],
            at(xe_ref, 1),
            at(xi_ref, 1),
            north_of_edge,
        ),
    ]

    def put(lev, i, kind, g, v):
        pe_ref[lev, i, pl.ds((kind * halves + g) * 8, 8), :] = v

    def last(i, kind, g, v):
        edge_ref[3 * i, pl.ds((kind * halves + g) * 8, 8), :] = v

    sweep(flags_ref, n_lev, n_pair, rows, put, last)
    k0, dk = order(flags_ref, n_lev)
    mid = k0 + dk * (n_lev - 1)
    edge_ref[1] = pi_ref[mid, 0]
    edge_ref[2] = pi_ref[mid, 1]


def first_edge(n_lev, n_pair, *refs):
    edge_sweep(True, n_lev, n_pair, *refs[:9], refs[9:12], *refs[12:])


def next_edge(n_lev, n_pair, *refs):
    edge_sweep(False, n_lev, n_pair, *refs)


def tallies(is_first, in_ref, out_ref, n_lev):
    if is_first:
        out_ref[0] = jnp.zeros(out_ref.shape[1:], F32)
        out_ref[n_lev] = jnp.zeros(out_ref.shape[1:], F32)
    else:
        out_ref[0] = in_ref[0]
        out_ref[n_lev] = in_ref[n_lev]
    zero = jnp.zeros((8, LANES), F32)

    def put(at, i, v):
        out_ref[at, i] = v

    return (lambda at, i: zero) if is_first else (lambda at, i: in_ref[at, i]), put


def edge_back(is_first, n_lev, n_pair, flags_ref, pe_ref, far_ref, c_ref, wx_ref, nf_ref, fs_ref, *rest):
    halves = n_pair // 8
    acc_ref, (xe_ref, north_ref, south_ref, out_ref) = (None, rest) if is_first else (rest[0], rest[1:])
    acc_in, acc_out = tallies(is_first, acc_ref, out_ref, n_lev)
    held = {}

    def put(lev, i, kind, g, v):
        xe_ref[lev, i, pl.ds((kind * halves + g) * 8, 8), :] = v
        if kind == 0:
            held[i, g] = v
        elif i == 0:
            south_ref[lev, pl.ds(g * 8, 8), :] = jnp.where(fs_ref[lev] < 0.0, held[i, g], v)
        else:
            n3 = spread(nf_ref[lev, 3:4, :])
            north_ref[lev, pl.ds(g * 8, 8), :] = jnp.where(n3 > 0.0, held[i, g], v)

    back(
        flags_ref, n_lev, n_pair, (0, 3), wx_ref, far_ref, c_ref,
        lambda lev, i, kind, g: rows_at(pe_ref, i, lev, kind, g, halves), put, acc_in, acc_out,
    )


def inner(is_first, n_lev, n_pair, flags_ref, pi_ref, far_ref, c_ref, wx_ref, nf_ref, fold_ref, hot_ref, xe_ref, *rest):
    halves = n_pair // 8
    acc_ref, (xi_ref, pn_ref, mf_ref, out_ref) = (None, rest) if is_first else (rest[0], rest[1:])
    acc_in, acc_out = tallies(is_first, acc_ref, out_ref, n_lev)

    def put(lev, i, kind, g, v):
        xi_ref[lev, i, pl.ds((kind * halves + g) * 8, 8), :] = v

    back(
        flags_ref, n_lev, n_pair, (1, 2), wx_ref, far_ref, c_ref,
        lambda lev, i, kind, g: rows_at(pi_ref, i, lev, kind, g, halves), put, acc_in, acc_out,
    )
    inner_sweep(n_lev, n_pair, flags_ref, xe_ref, xi_ref, c_ref, hot_ref, pn_ref)
    fold_rows(
        flags_ref, fold_ref, nf_ref, lambda lev, kind, g: rows_at(xe_ref, 1, lev, kind, g, halves), mf_ref, n_lev, n_pair
    )


def finish(
    n_lev, n_pair, n_rows, flags_ref, pe_ref, pi_ref, far_ref, c_ref, wx_ref, depth_ref, acce_ref, acci_ref,
    f_ref, a_ref, sens_ref, te_ref, ti_ref,
):
    halves = n_pair // 8
    stride = n_lev * n_rows

    for rows, p_ref, acc_ref, t_ref in (((0, 3), pe_ref, acce_ref, te_ref), ((1, 2), pi_ref, acci_ref, ti_ref)):
        acc_in, acc_out = tallies(False, acc_ref, t_ref, n_lev)

        def put(lev, i, kind, g, v, rows=rows):
            to = f_ref if kind == 0 else a_ref
            to[pl.ds(g * 8 * stride + lev * n_rows + rows[i], 8, stride=stride), :] = v

        back(
            flags_ref, n_lev, n_pair, rows, wx_ref, far_ref, c_ref,
            lambda lev, i, kind, g, p_ref=p_ref: rows_at(p_ref, i, lev, kind, g, halves), put, acc_in, acc_out,
        )
    first = flags_ref[0] * n_lev
    depth = depth_ref[...]

    def reduce(lev, _):
        k = first + lev
        live = jnp.where((k + 1 < depth) & (k + 1 < 2 * n_lev), 1.0 / STEPS, 0.0)
        e0, e3 = (jnp.sum(te_ref[lev + 1, i], axis=0, keepdims=True) for i in range(2))
        i1, i2 = (jnp.sum(ti_ref[lev + 1, i], axis=0, keepdims=True) for i in range(2))
        sens_ref[lev] = jnp.concatenate([e0, i1, i2, e3], 0) * live
        return 0

    lax.fori_loop(0, n_lev, reduce, 0, unroll=UNROLL)


def vmem(*shape):
    return pltpu.VMEM(shape, F32)


def call(kernel, outs, args, flops, scratch=()):
    spec = pl.BlockSpec(memory_space=pltpu.VMEM)
    return pl.pallas_call(
        kernel,
        out_shape=tuple(outs),
        in_specs=[pl.BlockSpec(memory_space=pltpu.SMEM)] + [spec] * (len(args) - 1),
        out_specs=tuple([spec] * len(outs)),
        scratch_shapes=list(scratch),
        compiler_params=pltpu.CompilerParams(vmem_limit_bytes=24 * 2**20),
        cost_estimate=pl.CostEstimate(flops=flops, bytes_accessed=flops // 8, transcendentals=0),
    )(args[0], *[pltpu.with_memory_space_constraint(a, pltpu.VMEM) for a in args[1:]])


def per_device(forward_init, adjoint_init, east_flow, north_flow, mixing, depth, color, fold):
    n_pair, n_lev, n_rows, n_x = forward_init.shape
    n_all = 2 * n_pair
    count = lax.axis_size("horiz")
    place = lax.axis_index("horiz")
    flags = jnp.stack(
        [
            lax.axis_index("level"),
            (place == count - 1).astype(jnp.int32),
            (place == 0).astype(jnp.int32),
            lax.axis_index("tracer") * n_pair,
        ]
    ).astype(jnp.int32)
    northward = [(i, (i + 1) % count) for i in range(count)]
    southward = [((i + 1) % count, i) for i in range(count)]
    swap = [(0, 1), (1, 0)]
    f2 = forward_init.reshape(n_pair * n_lev * n_rows, n_x)
    a2 = adjoint_init.reshape(n_pair * n_lev * n_rows, n_x)
    fold2 = fold.reshape(1, n_x)
    work = n_lev * n_rows * n_all * n_x
    pages = n_lev // n_pair

    to_north, to_south = call(
        functools.partial(send_first, n_lev, n_pair, n_rows),
        [vmem(n_lev + pages + 1, n_pair, n_x), vmem(2 * n_lev + 1, n_pair, n_x)],
        [flags, f2, a2, north_flow, depth],
        work,
    )
    from_south = lax.ppermute(to_north, "horiz", northward)
    from_north = lax.ppermute(to_south, "horiz", southward)
    state = vmem(n_lev, 2, n_all, n_x)
    halo = vmem(n_lev, n_pair, n_x)
    acc = vmem(n_lev + 1, 2, 8, n_x)
    xe, xi, pi, c, wx, hot, mf = call(
        functools.partial(prepare, n_lev, n_pair, n_rows),
        [state, state, state, vmem(13, n_lev, n_rows, n_x), vmem(3, n_rows, n_x), vmem(n_rows, n_pair, n_x), halo],
        [flags, f2, a2, east_flow, north_flow, mixing, depth, color, fold2],
        work * 10,
        [vmem(n_lev, n_rows, n_x)],
    )
    edges = vmem(n_rows, n_all, n_x)
    acce = acci = None
    for step in range(STEPS):
        if step == 0:
            pe, edge, ec, fs = call(
                functools.partial(first_edge, n_lev, n_pair),
                [state, edges, vmem(8, n_lev, 8, n_x), vmem(n_lev, 8, n_x)],
                [flags, xe, xi, pi, c, hot, mf, from_south, from_north, north_flow, depth, fold2],
                work * 5,
            )
        else:
            pe, edge = call(
                functools.partial(next_edge, n_lev, n_pair),
                [state, edges],
                [flags, xe, xi, pi, c, hot, mf, from_south, from_north, ec],
                work * 5,
            )
        far = lax.ppermute(edge, "level", swap)
        if step == STEPS - 1:
            break
        more = [] if step == 0 else [acce]
        xe, to_north, to_south, acce = call(
            functools.partial(edge_back, step == 0, n_lev, n_pair),
            [state, halo, halo, acc],
            [flags, pe, far, c, wx, north_flow, fs] + more,
            work * 2,
        )
        from_south = lax.ppermute(to_north, "horiz", northward)
        from_north = lax.ppermute(to_south, "horiz", southward)
        more = [] if step == 0 else [acci]
        xi, pi, mf, acci = call(
            functools.partial(inner, step == 0, n_lev, n_pair),
            [state, state, halo, acc],
            [flags, pi, far, c, wx, north_flow, fold2, hot, xe] + more,
            work * 7,
        )
    flat = vmem(n_pair * n_lev * n_rows, n_x)
    f_out, a_out, sens = call(
        functools.partial(finish, n_lev, n_pair, n_rows),
        [flat, flat, vmem(n_lev, n_rows, n_x)],
        [flags, pe, pi, far, c, wx, depth, acce, acci],
        work * 4,
        [acc, acc],
    )
    sens = sens + lax.ppermute(sens, "tracer", swap)
    return f_out.reshape(forward_init.shape), a_out.reshape(adjoint_init.shape), sens


def solution(mesh):
    tracers, flows = P("tracer", "level", "horiz", None), P("level", "horiz", None)
    return jax.shard_map(
        per_device,
        mesh=mesh,
        in_specs=(tracers, tracers, flows, flows, P(None, "horiz", None), P("horiz", None), P("horiz", None), P()),
        out_specs=(tracers, tracers, flows),
        check_vma=False,
    )
```

time: 253 us -> 102 us (0.40)
  the two profiles are of different devices: /device:TPU:1 before, /device:TPU:3 now
where the time goes in v1:
time: 102 us; the launch traced here: 100 us
  starting transfers between devices  42.7 us (42%)
  Pallas kernels  29.5 us (29%)
  waiting for transfers between devices  20.3 us (20%)
  local copies, waits for them, and re-layouts  6.55 us (6%)
    pallas_call x13, Pallas kernels, call(): pl.pallas_call(kernel, out_shape=tuple(outs), in_specs=[pl.BlockSpec(memo...  29.5 us
    ppermute x4, starting transfers between devices, per_device(): from_north = lax.ppermute(to_south, 'horiz', southward)  23.3 us
    ppermute x4, waiting for transfers between devices, per_device(): far = lax.ppermute(edge, 'level', swap)  10.9 us
    ppermute x1, starting transfers between devices, per_device(): sens = sens + lax.ppermute(sens, 'tracer', swap)  10.2 us
    ppermute x4, waiting for transfers between devices, per_device(): from_south = lax.ppermute(to_north, 'horiz', northward)  9.36 us
    ppermute x4, starting transfers between devices, per_device(): far = lax.ppermute(edge, 'level', swap)  8.86 us
    unnamed x20, local copies, waits for them, and re-layouts  6.55 us
  transfers between devices with their start and end apart: 13, of which 8 were waited for; matrix products, arithmetic and copies ran while one was open for 2% of the time, Pallas kernels for 13%

profile of v1, /device:TPU:3, one launch (start us, length us, event | category | flops | bytes accessed | tf_op | source)
XLA Modules:
  0.0 100.5 jit_solution(5736942286011195386)
XLA Ops:
  6.0 6.2 %collective-permute-start.1 = (f32[65,16,128]{2,1,0:T(8,128)S(1)}, f32[65,16,128]{2,1,0:T(8,128)S(1)}, u32[]{:S(2)}, u32[]{:S(2)}) collective-permute-start(f32[65,16,128]{2,1,0:T(8,128)S(1)} %get-tuple-element.56), channel_id=1, source_target_pairs={{4,0},{8,4},{12,8},{16,12},{20,16},{24,20},{28,24},{32,28},{36,32}... | collective-permute-start | bytes 1597448 | tf_op jit(solution)/shard_map/ppermute | solution.py:513
  12.9 5.7 %shard_map.103 = (f32[32,2,32,128]{3,2,1,0:T(8,128)S(1)}, f32[32,2,32,128]{3,2,1,0:T(8,128)S(1)}, f32[32,2,32,128]{3,2,1,0:T(8,128)S(1)}, f32[13,32,4,128]{3,2,1...) custom-call(s32[4]{0:T(128)S(1)} %pad_add_fusion.flags_ref.refs_0_, ...), custom_call_target="tpu_custom_call" | custom-call | flops 5242880 | bytes 655360 | tf_op jit(solution)/shard_map/pallas_call | solution.py:473
  18.6 5.2 %collective-permute-done.refs_7_ = f32[35,16,128]{2,1,0:T(8,128)S(1)} collective-permute-done((f32[35,16,128]{2,1,0:T(8,128)S(1)}, f32[35,16,128]{2,1,0:T(8,128)S(1)}, u32[]{:S(2)}, u32[]{:S(2)}) %collective-permute-start) | collective-permute-done | bytes 286752 | tf_op jit(solution)/shard_map/ppermute | solution.py:512
  23.8 2.4 %shard_map.105 = (f32[32,2,32,128]{3,2,1,0:T(8,128)S(1)}, f32[4,32,128]{2,1,0:T(8,128)S(1)}, f32[8,32,8,128]{3,2,1,0:T(8,128)S(1)}, f32[32,8,128]{2,1,0:T(8,128)S(1)}) custom-call(s32[4]{0:T(128)S(1)} %pad_add_fusion.flags_ref.refs_0_, f32[32,2,32,128]{3,2,1,0:T(8,128)S(1)} %get-tuple-element.49.refs_1_, f32[32,2,32,128]{3,2,1,0:T(8,128)S(1)} %get-tuple-element.50.refs_2_, ...), custom_call_target="tpu_custom_call" | custom-call | flops 2621440 | bytes 327680 | tf_op jit(solution)/shard_map/pallas_call | solution.py:473
  26.3 2.2 %collective-permute-start.2 = (f32[4,32,128]{2,1,0:T(8,128)S(1)}, f32[4,32,128]{2,1,0:T(8,128)S(1)}, u32[]{:S(2)}, u32[]{:S(2)}) collective-permute-start(f32[4,32,128]{2,1,0:T(8,128)S(1)} %get-tuple-element.58), channel_id=1, source_target_pairs={{0,1},{1,0},{2,3},{3,2},{4,5},{5,4},{6,7},{7,6},{8,9},{9,8},{10,11... | collective-permute-start | bytes 196616 | tf_op jit(solution)/shard_map/ppermute | solution.py:541
  28.5 2.5 %collective-permute-done.2.far_ref = f32[4,32,128]{2,1,0:T(8,128)S(1)} collective-permute-done((f32[4,32,128]{2,1,0:T(8,128)S(1)}, f32[4,32,128]{2,1,0:T(8,128)S(1)}, u32[]{:S(2)}, u32[]{:S(2)}) %collective-permute-start.2) | collective-permute-done | bytes 65568 | tf_op jit(solution)/shard_map/ppermute | solution.py:541
  31.9 5.7 %collective-permute-start.4 = (f32[32,16,128]{2,1,0:T(8,128)S(1)}, f32[32,16,128]{2,1,0:T(8,128)S(1)}, u32[]{:S(2)}, u32[]{:S(2)}) collective-permute-start(f32[32,16,128]{2,1,0:T(8,128)S(1)} %get-tuple-element.66), channel_id=1, source_target_pairs={{4,0},{8,4},{12,8},{16,12},{20,16},{24,20},{28,24},{32,28},{36,32}... | collective-permute-start | bytes 786440 | tf_op jit(solution)/shard_map/ppermute | solution.py:552
  37.6 2.6 %shard_map.107 = (f32[32,2,32,128]{3,2,1,0:T(8,128)S(1)}, f32[32,2,32,128]{3,2,1,0:T(8,128)S(1)}, f32[32,16,128]{2,1,0:T(8,128)S(1)}, f32[33,2,8,128]{3,2,1,0:T(8,128)S(1)}) custom-call(s32[4]{0:T(128)S(1)} %pad_add_fusion.flags_ref.refs_0_, f32[32,2,32,128]{3,2,1,0:T(8,128)S(1)} %get-tuple-element.51.refs_3_.pi_ref, ...), custom_call_target="tpu_custom_call" | custom-call | flops 3670016 | bytes 458752 | tf_op jit(solution)/shard_map/pallas_call | solution.py:473
  41.3 2.3 %shard_map.108 = (f32[32,2,32,128]{3,2,1,0:T(8,128)S(1)}, f32[4,32,128]{2,1,0:T(8,128)S(1)}) custom-call(s32[4]{0:T(128)S(1)} %pad_add_fusion.flags_ref.refs_0_, f32[32,2,32,128]{3,2,1,0:T(8,128)S(1)} %get-tuple-element.61.xe_ref.refs_1_, f32[32,2,32,128]{3,2,1,0:T(8,128)S(1)} %get-tuple-element.62.refs_2_, ...), custom_call_target="tpu_custom_call" | custom-call | flops 2621440 | bytes 327680 | tf_op jit(solution)/shard_map/pallas_call | solution.py:473
  43.6 2.2 %collective-permute-start.5 = (f32[4,32,128]{2,1,0:T(8,128)S(1)}, f32[4,32,128]{2,1,0:T(8,128)S(1)}, u32[]{:S(2)}, u32[]{:S(2)}) collective-permute-start(f32[4,32,128]{2,1,0:T(8,128)S(1)} %get-tuple-element.69), channel_id=1, source_target_pairs={{0,1},{1,0},{2,3},{3,2},{4,5},{5,4},{6,7},{7,6},{8,9},{9,8},{10,11... | collective-permute-start | bytes 196616 | tf_op jit(solution)/shard_map/ppermute | solution.py:541
  45.9 2.5 %collective-permute-done.5.far_ref = f32[4,32,128]{2,1,0:T(8,128)S(1)} collective-permute-done((f32[4,32,128]{2,1,0:T(8,128)S(1)}, f32[4,32,128]{2,1,0:T(8,128)S(1)}, u32[]{:S(2)}, u32[]{:S(2)}) %collective-permute-start.5) | collective-permute-done | bytes 65568 | tf_op jit(solution)/shard_map/ppermute | solution.py:541
  49.3 5.7 %collective-permute-start.7 = (f32[32,16,128]{2,1,0:T(8,128)S(1)}, f32[32,16,128]{2,1,0:T(8,128)S(1)}, u32[]{:S(2)}, u32[]{:S(2)}) collective-permute-start(f32[32,16,128]{2,1,0:T(8,128)S(1)} %get-tuple-element.77), channel_id=1, source_target_pairs={{4,0},{8,4},{12,8},{16,12},{20,16},{24,20},{28,24},{32,28},{36,32}... | collective-permute-start | bytes 786440 | tf_op jit(solution)/shard_map/ppermute | solution.py:552
  55.0 2.6 %shard_map.110 = (f32[32,2,32,128]{3,2,1,0:T(8,128)S(1)}, f32[32,2,32,128]{3,2,1,0:T(8,128)S(1)}, f32[32,16,128]{2,1,0:T(8,128)S(1)}, f32[33,2,8,128]{3,2,1,0:T(8,128)S(1)}) custom-call(s32[4]{0:T(128)S(1)} %pad_add_fusion.flags_ref.refs_0_, f32[32,2,32,128]{3,2,1,0:T(8,128)S(1)} %get-tuple-element.63.refs_3_.pi_ref, ...), custom_call_target="tpu_custom_call" | custom-call | flops 3670016 | bytes 458752 | tf_op jit(solution)/shard_map/pallas_call | solution.py:473
  57.6 1.8 %collective-permute-done.6.refs_7_ = f32[32,16,128]{2,1,0:T(8,128)S(1)} collective-permute-done((f32[32,16,128]{2,1,0:T(8,128)S(1)}, f32[32,16,128]{2,1,0:T(8,128)S(1)}, u32[]{:S(2)}, u32[]{:S(2)}) %collective-permute-start.6) | collective-permute-done | bytes 262176 | tf_op jit(solution)/shard_map/ppermute | solution.py:551
  59.4 2.3 %shard_map.111 = (f32[32,2,32,128]{3,2,1,0:T(8,128)S(1)}, f32[4,32,128]{2,1,0:T(8,128)S(1)}) custom-call(s32[4]{0:T(128)S(1)} %pad_add_fusion.flags_ref.refs_0_, f32[32,2,32,128]{3,2,1,0:T(8,128)S(1)} %get-tuple-element.71.xe_ref.refs_1_, f32[32,2,32,128]{3,2,1,0:T(8,128)S(1)} %get-tuple-element.73.refs_2_, ...), custom_call_target="tpu_custom_call" | custom-call | flops 2621440 | bytes 327680 | tf_op jit(solution)/shard_map/pallas_call | solution.py:473
  61.7 1.8 %collective-permute-start.8 = (f32[4,32,128]{2,1,0:T(8,128)S(1)}, f32[4,32,128]{2,1,0:T(8,128)S(1)}, u32[]{:S(2)}, u32[]{:S(2)}) collective-permute-start(f32[4,32,128]{2,1,0:T(8,128)S(1)} %get-tuple-element.79), channel_id=1, source_target_pairs={{0,1},{1,0},{2,3},{3,2},{4,5},{5,4},{6,7},{7,6},{8,9},{9,8},{10,11... | collective-permute-start | bytes 196616 | tf_op jit(solution)/shard_map/ppermute | solution.py:541
  63.5 3.5 %collective-permute-done.8.far_ref = f32[4,32,128]{2,1,0:T(8,128)S(1)} collective-permute-done((f32[4,32,128]{2,1,0:T(8,128)S(1)}, f32[4,32,128]{2,1,0:T(8,128)S(1)}, u32[]{:S(2)}, u32[]{:S(2)}) %collective-permute-start.8) | collective-permute-done | bytes 65568 | tf_op jit(solution)/shard_map/ppermute | solution.py:541
  68.0 5.7 %collective-permute-start.10 = (f32[32,16,128]{2,1,0:T(8,128)S(1)}, f32[32,16,128]{2,1,0:T(8,128)S(1)}, u32[]{:S(2)}, u32[]{:S(2)}) collective-permute-start(f32[32,16,128]{2,1,0:T(8,128)S(1)} %get-tuple-element.87), channel_id=1, source_target_pairs={{4,0},{8,4},{12,8},{16,12},{20,16},{24,20},{28,24},{32,28},{36,32}... | collective-permute-start | bytes 786440 | tf_op jit(solution)/shard_map/ppermute | solution.py:552
  73.7 2.6 %shard_map.113 = (f32[32,2,32,128]{3,2,1,0:T(8,128)S(1)}, f32[32,2,32,128]{3,2,1,0:T(8,128)S(1)}, f32[32,16,128]{2,1,0:T(8,128)S(1)}, f32[33,2,8,128]{3,2,1,0:T(8,128)S(1)}) custom-call(s32[4]{0:T(128)S(1)} %pad_add_fusion.flags_ref.refs_0_, f32[32,2,32,128]{3,2,1,0:T(8,128)S(1)} %get-tuple-element.74.refs_3_.pi_ref, ...), custom_call_target="tpu_custom_call" | custom-call | flops 3670016 | bytes 458752 | tf_op jit(solution)/shard_map/pallas_call | solution.py:473
  77.4 2.3 %shard_map.114 = (f32[32,2,32,128]{3,2,1,0:T(8,128)S(1)}, f32[4,32,128]{2,1,0:T(8,128)S(1)}) custom-call(s32[4]{0:T(128)S(1)} %pad_add_fusion.flags_ref.refs_0_, f32[32,2,32,128]{3,2,1,0:T(8,128)S(1)} %get-tuple-element.81.xe_ref.refs_1_, f32[32,2,32,128]{3,2,1,0:T(8,128)S(1)} %get-tuple-element.83.refs_2_, ...), custom_call_target="tpu_custom_call" | custom-call | flops 2621440 | bytes 327680 | tf_op jit(solution)/shard_map/pallas_call | solution.py:473
  79.7 2.6 %collective-permute-start.11 = (f32[4,32,128]{2,1,0:T(8,128)S(1)}, f32[4,32,128]{2,1,0:T(8,128)S(1)}, u32[]{:S(2)}, u32[]{:S(2)}) collective-permute-start(f32[4,32,128]{2,1,0:T(8,128)S(1)} %get-tuple-element.89), channel_id=1, source_target_pairs={{0,1},{1,0},{2,3},{3,2},{4,5},{5,4},{6,7},{7,6},{8,9},{9,8},{10,11... | collective-permute-start | bytes 196616 | tf_op jit(solution)/shard_map/ppermute | solution.py:541
  82.3 2.4 %collective-permute-done.11.far_ref = f32[4,32,128]{2,1,0:T(8,128)S(1)} collective-permute-done((f32[4,32,128]{2,1,0:T(8,128)S(1)}, f32[4,32,128]{2,1,0:T(8,128)S(1)}, u32[]{:S(2)}, u32[]{:S(2)}) %collective-permute-start.11) | collective-permute-done | bytes 65568 | tf_op jit(solution)/shard_map/ppermute | solution.py:541
  84.7 2.9 %shard_map.115 = (f32[2048,128]{1,0:T(8,128)S(1)}, f32[2048,128]{1,0:T(8,128)S(1)}, f32[32,4,128]{2,1,0:T(4,128)S(1)}) custom-call(s32[4]{0:T(128)S(1)} %pad_add_fusion.flags_ref.refs_0_, f32[32,2,32,128]{3,2,1,0:T(8,128)S(1)} %get-tuple-element.88.pe_ref, f32[32,2,32,128]{3,2,1,0:T(8,128)S(1)} %get-tuple-element.84.refs_3_.pi_ref, ...), custom_call_target="tpu_custom_call" | custom-call | flops 2097152 | bytes 262144 | tf_op jit(solution)/shard_map/pallas_call | solution.py:473
  87.6 10.2 %collective-permute-start.12 = (f32[32,4,128]{2,1,0:T(4,128)S(1)}, f32[32,4,128]{2,1,0:T(4,128)S(1)}, u32[]{:S(2)}, u32[]{:S(2)}) collective-permute-start(f32[32,4,128]{2,1,0:T(4,128)S(1)} %get-tuple-element.94), channel_id=1, source_target_pairs={{0,2},{2,0},{1,3},{3,1},{4,6},{6,4},{5,7},{7,5},{8,10},{10,8},{9,1... | collective-permute-start | bytes 196616 | tf_op jit(solution)/shard_map/ppermute | solution.py:568
  (37 shorter events, 13.7 us)
Async XLA Ops:
  0.7 0.7 copy-start.6
  1.4 0.8 copy-start
  2.2 1.2 %copy-start.2 = (f32[16,32,4,128]{3,2,1,0:T(4,128)S(1)}, f32[16,32,4,128]{3,2,1,0:T(4,128)}, u32[]{:S(2)}) copy-start(f32[16,32,4,128]{3,2,1,0:T(4,128)} %param.8) | copy-start | bytes 3145732
  3.5 1.2 %copy-start.3 = (f32[16,32,4,128]{3,2,1,0:T(4,128)S(1)}, f32[16,32,4,128]{3,2,1,0:T(4,128)}, u32[]{:S(2)}) copy-start(f32[16,32,4,128]{3,2,1,0:T(4,128)} %param.9) | copy-start | bytes 3145732
  4.7 7.5 %copy-start.1 = (f32[32,4,128]{2,1,0:T(4,128)S(1)}, f32[32,4,128]{2,1,0:T(4,128)}, u32[]{:S(2)}) copy-start(f32[32,4,128]{2,1,0:T(4,128)} %nf_ref.15) | copy-start | bytes 196612
  4.7 7.5 %copy-start.4 = (f32[63,4,128]{2,1,0:T(4,128)S(1)}, f32[63,4,128]{2,1,0:T(4,128)}, u32[]{:S(2)}) copy-start(f32[63,4,128]{2,1,0:T(4,128)} %mix_ref.1) | copy-start | bytes 387076
  4.7 7.6 %copy-start.5 = (f32[32,4,128]{2,1,0:T(4,128)S(1)}, f32[32,4,128]{2,1,0:T(4,128)}, u32[]{:S(2)}) copy-start(f32[32,4,128]{2,1,0:T(4,128)} %ef_ref.1) | copy-start | bytes 196612
  6.0 6.3 %copy-start.8 = (s32[4,128]{1,0:T(4,128)S(1)}, s32[4,128]{1,0:T(4,128)}, u32[]{:S(2)}) copy-start(s32[4,128]{1,0:T(4,128)} %color_ref.1) | copy-start | bytes 6148
  6.0 17.9 %collective-permute-start.1 = (f32[65,16,128]{2,1,0:T(8,128)S(1)}, f32[65,16,128]{2,1,0:T(8,128)S(1)}, u32[]{:S(2)}, u32[]{:S(2)}) collective-permute-start(f32[65,16,128]{2,1,0:T(8,128)S(1)} %get-tuple-element.56), channel_id=1, source_target_pairs={{4,0},{8,4},{12,8},{16,12},{20,16},{24,20},{28,24},{32,28},{36,32}... | collective-permute-start | bytes 1597448 | tf_op jit(solution)/shard_map/ppermute | solution.py:513
  12.2 0.7 copy-start.7
  12.2 11.6 %collective-permute-start = (f32[35,16,128]{2,1,0:T(8,128)S(1)}, f32[35,16,128]{2,1,0:T(8,128)S(1)}, u32[]{:S(2)}, u32[]{:S(2)}) collective-permute-start(f32[35,16,128]{2,1,0:T(8,128)S(1)} %get-tuple-element.55), channel_id=1, source_target_pairs={{0,4},{4,8},{8,12},{12,16},{16,20},{20,24},{24,28},{28,32},{32,36}... | collective-permute-start | bytes 860168 | tf_op jit(solution)/shard_map/ppermute | solution.py:512
  26.3 4.7 %collective-permute-start.2 = (f32[4,32,128]{2,1,0:T(8,128)S(1)}, f32[4,32,128]{2,1,0:T(8,128)S(1)}, u32[]{:S(2)}, u32[]{:S(2)}) collective-permute-start(f32[4,32,128]{2,1,0:T(8,128)S(1)} %get-tuple-element.58), channel_id=1, source_target_pairs={{0,1},{1,0},{2,3},{3,2},{4,5},{5,4},{6,7},{7,6},{8,9},{9,8},{10,11... | collective-permute-start | bytes 196616 | tf_op jit(solution)/shard_map/ppermute | solution.py:541
  31.8 9.5 %collective-permute-start.3 = (f32[32,16,128]{2,1,0:T(8,128)S(1)}, f32[32,16,128]{2,1,0:T(8,128)S(1)}, u32[]{:S(2)}, u32[]{:S(2)}) collective-permute-start(f32[32,16,128]{2,1,0:T(8,128)S(1)} %get-tuple-element.65), channel_id=1, source_target_pairs={{0,4},{4,8},{8,12},{12,16},{16,20},{20,24},{24,28},{28,32},{32,36}... | collective-permute-start | bytes 786440 | tf_op jit(solution)/shard_map/ppermute | solution.py:551
  31.9 9.4 %collective-permute-start.4 = (f32[32,16,128]{2,1,0:T(8,128)S(1)}, f32[32,16,128]{2,1,0:T(8,128)S(1)}, u32[]{:S(2)}, u32[]{:S(2)}) collective-permute-start(f32[32,16,128]{2,1,0:T(8,128)S(1)} %get-tuple-element.66), channel_id=1, source_target_pairs={{4,0},{8,4},{12,8},{16,12},{20,16},{24,20},{28,24},{32,28},{36,32}... | collective-permute-start | bytes 786440 | tf_op jit(solution)/shard_map/ppermute | solution.py:552
  43.6 4.7 %collective-permute-start.5 = (f32[4,32,128]{2,1,0:T(8,128)S(1)}, f32[4,32,128]{2,1,0:T(8,128)S(1)}, u32[]{:S(2)}, u32[]{:S(2)}) collective-permute-start(f32[4,32,128]{2,1,0:T(8,128)S(1)} %get-tuple-element.69), channel_id=1, source_target_pairs={{0,1},{1,0},{2,3},{3,2},{4,5},{5,4},{6,7},{7,6},{8,9},{9,8},{10,11... | collective-permute-start | bytes 196616 | tf_op jit(solution)/shard_map/ppermute | solution.py:541
  49.2 10.2 %collective-permute-start.6 = (f32[32,16,128]{2,1,0:T(8,128)S(1)}, f32[32,16,128]{2,1,0:T(8,128)S(1)}, u32[]{:S(2)}, u32[]{:S(2)}) collective-permute-start(f32[32,16,128]{2,1,0:T(8,128)S(1)} %get-tuple-element.76), channel_id=1, source_target_pairs={{0,4},{4,8},{8,12},{12,16},{16,20},{20,24},{24,28},{28,32},{32,36}... | collective-permute-start | bytes 786440 | tf_op jit(solution)/shard_map/ppermute | solution.py:551
  49.3 10.1 %collective-permute-start.7 = (f32[32,16,128]{2,1,0:T(8,128)S(1)}, f32[32,16,128]{2,1,0:T(8,128)S(1)}, u32[]{:S(2)}, u32[]{:S(2)}) collective-permute-start(f32[32,16,128]{2,1,0:T(8,128)S(1)} %get-tuple-element.77), channel_id=1, source_target_pairs={{4,0},{8,4},{12,8},{16,12},{20,16},{24,20},{28,24},{32,28},{36,32}... | collective-permute-start | bytes 786440 | tf_op jit(solution)/shard_map/ppermute | solution.py:552
  61.7 5.4 %collective-permute-start.8 = (f32[4,32,128]{2,1,0:T(8,128)S(1)}, f32[4,32,128]{2,1,0:T(8,128)S(1)}, u32[]{:S(2)}, u32[]{:S(2)}) collective-permute-start(f32[4,32,128]{2,1,0:T(8,128)S(1)} %get-tuple-element.79), channel_id=1, source_target_pairs={{0,1},{1,0},{2,3},{3,2},{4,5},{5,4},{6,7},{7,6},{8,9},{9,8},{10,11... | collective-permute-start | bytes 196616 | tf_op jit(solution)/shard_map/ppermute | solution.py:541
  67.9 9.5 %collective-permute-start.9 = (f32[32,16,128]{2,1,0:T(8,128)S(1)}, f32[32,16,128]{2,1,0:T(8,128)S(1)}, u32[]{:S(2)}, u32[]{:S(2)}) collective-permute-start(f32[32,16,128]{2,1,0:T(8,128)S(1)} %get-tuple-element.86), channel_id=1, source_target_pairs={{0,4},{4,8},{8,12},{12,16},{16,20},{20,24},{24,28},{28,32},{32,36}... | collective-permute-start | bytes 786440 | tf_op jit(solution)/shard_map/ppermute | solution.py:551
  68.0 9.4 %collective-permute-start.10 = (f32[32,16,128]{2,1,0:T(8,128)S(1)}, f32[32,16,128]{2,1,0:T(8,128)S(1)}, u32[]{:S(2)}, u32[]{:S(2)}) collective-permute-start(f32[32,16,128]{2,1,0:T(8,128)S(1)} %get-tuple-element.87), channel_id=1, source_target_pairs={{4,0},{8,4},{12,8},{16,12},{20,16},{24,20},{28,24},{32,28},{36,32}... | collective-permute-start | bytes 786440 | tf_op jit(solution)/shard_map/ppermute | solution.py:552
  79.7 5.0 %collective-permute-start.11 = (f32[4,32,128]{2,1,0:T(8,128)S(1)}, f32[4,32,128]{2,1,0:T(8,128)S(1)}, u32[]{:S(2)}, u32[]{:S(2)}) collective-permute-start(f32[4,32,128]{2,1,0:T(8,128)S(1)} %get-tuple-element.89), channel_id=1, source_target_pairs={{0,1},{1,0},{2,3},{3,2},{4,5},{5,4},{6,7},{7,6},{8,9},{9,8},{10,11... | collective-permute-start | bytes 196616 | tf_op jit(solution)/shard_map/ppermute | solution.py:541
  87.6 12.2 %collective-permute-start.12 = (f32[32,4,128]{2,1,0:T(4,128)S(1)}, f32[32,4,128]{2,1,0:T(4,128)S(1)}, u32[]{:S(2)}, u32[]{:S(2)}) collective-permute-start(f32[32,4,128]{2,1,0:T(4,128)S(1)} %get-tuple-element.94), channel_id=1, source_target_pairs={{0,2},{2,0},{1,3},{3,1},{4,6},{6,4},{5,7},{7,5},{8,10},{10,8},{9,1... | collective-permute-start | bytes 196616 | tf_op jit(solution)/shard_map/ppermute | solution.py:568

commit v2 on v1

--- a/solution.py
+++ b/solution.py
@@ -11,7 +11,8 @@
 C0F, C0A, CWF, CWA, CEF, CEA, CSF, CSA, CNF, CNA, UP, WI, BACK = range(13)
 E0F, E0A, ESF, ESA, T0F, T0A, TNF, TNA = range(8)
 F32 = jnp.float32
-UNROLL = 2
+UNROLL = 8
+PIECE = 8
 
 
 def order(flags_ref, n_lev):
@@ -43,34 +44,48 @@
     def body(s, carry):
         lev = k0 + dk * s
         out = []
-        at = 0
-        for i, (coef, src, center, south, north) in enumerate(rows):
-            up = coef(UP, lev)
-            wi = coef(WI, lev)
-            srcs = [src(g) * wi for g in range(halves)]
+        for i, (up, explicit, swept) in enumerate(rows):
+            values = explicit(lev)
+            factor = up(lev) if swept else None
             for kind in range(2):
-                c0, cw, ce, cs, cn = (coef(base + kind, lev) for base in (C0F, CWF, CEF, CSF, CNF))
                 for g in range(halves):
-                    c = center(lev, kind, g)
-                    v = c0 * c + cw * west(c)
-                    v = v + (ce * east(c) + cs * south(lev, kind, g))
-                    v = v + (cn * north(lev, kind, g) + srcs[g])
-                    v = v + up * carry[at]
+                    v = values[kind][g]
+                    if swept:
+                        v = v + factor * carry[len(out)]
+                        out.append(v)
                     put(lev, i, kind, g, v)
-                    out.append(v)
-                    at += 1
         return tuple(out)
 
-    final = lax.fori_loop(0, n_lev, body, (zero,) * (len(rows) * 2 * halves), unroll=UNROLL)
-    at = 0
-    for i in range(len(rows)):
+    n_swept = sum(row[2] for row in rows)
+    final = lax.fori_loop(0, n_lev, body, (zero,) * (n_swept * 2 * halves), unroll=UNROLL)
+    for at, v in enumerate(final):
+        last(at // (2 * halves), at // halves % 2, at % halves, v)
+
+
+def own_part(n_pair, coef, src, center, sides):
+    halves = n_pair // 8
+
+    def explicit(lev):
+        wi = coef(WI, lev)
+        srcs = [src(g) * wi for g in range(halves)]
+        out = []
         for kind in range(2):
+            c0, cw, ce = (coef(base + kind, lev) for base in (C0F, CWF, CEF))
+            cs = [coef(base + kind, lev) for base, _ in sides]
+            vs = []
             for g in range(halves):
-                last(i, kind, g, final[at])
-                at += 1
-
-
-def back(flags_ref, n_lev, n_pair, rows, wx_ref, far_ref, c_ref, part, put, acc_in, acc_out):
+                c = center(lev, kind, g)
+                v = (c0 * c + srcs[g]) + (cw * west(c) + ce * east(c))
+                for k, (_, side) in zip(cs, sides):
+                    v = v + k * side(lev, kind, g)
+                vs.append(v)
+            out.append(vs)
+        return out
+
+    return explicit
+
+
+def back(flags_ref, n_lev, n_pair, rows, wx_ref, far_ref, c_ref, part, put, acc_in, acc_out, done=None):
     bottom = flags_ref[0]
     k0, dk = order(flags_ref, n_lev)
     halves = n_pair // 8
@@ -121,7 +136,14 @@
         store(lev, now)
         return tuple(now)
 
-    lax.fori_loop(0, n_lev - 1, body, tuple(own), unroll=UNROLL)
+    if done is None:
+        lax.fori_loop(0, n_lev - 1, body, tuple(own), unroll=UNROLL)
+        return
+    now = lax.fori_loop(0, PIECE - 1, body, tuple(own), unroll=PIECE - 1)
+    done(0)
+    for piece in range(1, n_lev // PIECE):
+        now = lax.fori_loop(piece * PIECE - 1, (piece + 1) * PIECE - 1, body, now, unroll=PIECE)
+        done(piece)
 
 
 def fold_rows(flags_ref, fold_ref, nf_ref, get, mf_ref, n_lev, n_pair):
@@ -137,33 +159,40 @@
                 mf_ref[lev, pl.ds(g * 8, 8), :] = jnp.where(n3 < 0.0, f, a)
             return 0
 
-        lax.fori_loop(0, n_lev, body, 0)
+        lax.fori_loop(0, n_lev, body, 0, unroll=4)
 
 
 def rows_at(ref, row, lev, kind, g, halves):
     return ref[lev, row, pl.ds((kind * halves + g) * 8, 8), :]
 
 
-def send_first(n_lev, n_pair, n_rows, flags_ref, f_ref, a_ref, nf_ref, depth_ref, north_ref, south_ref):
+def send_first(
+    n_lev, n_pair, n_rows, f_hbm, a_hbm, nf_hbm, depth_hbm, north_ref, south_ref, f_ref, a_ref, nf_ref, depth_ref, sems
+):
     stride = n_lev * n_rows
-    first = flags_ref[0] * n_lev
+    part = 4 * stride
+    first = lax.axis_index("level") * n_lev
+    small = [
+        pltpu.make_async_copy(nf_hbm, nf_ref, sems.at[0]),
+        pltpu.make_async_copy(depth_hbm, depth_ref, sems.at[1]),
+    ]
+    large = [
+        [
+            pltpu.make_async_copy(
+                hbm.at[pl.ds(j * part, part), :], to.at[pl.ds(j * part, part), :], sems.at[2 + 2 * j + i]
+            )
+            for i, (hbm, to) in enumerate(((f_hbm, f_ref), (a_hbm, a_ref)))
+        ]
+        for j in range(n_pair // 4)
+    ]
+    for copy in small:
+        copy.start()
+    for pair in large:
+        for copy in pair:
+            copy.start()
+    for copy in small:
+        copy.wait()
     depth = depth_ref[...]
-
-    def body(lev, _):
-        wet = jnp.where(first + lev < depth, 1.0, 0.0)
-        w0 = spread(wet[0:1])
-        w3 = spread(wet[n_rows - 1 : n_rows])
-        n3 = spread(nf_ref[lev, n_rows - 1 : n_rows, :])
-        for g in range(n_pair // 8):
-            at = g * 8 * stride + lev * n_rows
-            low, high = pl.ds(at, 8, stride=stride), pl.ds(at + n_rows - 1, 8, stride=stride)
-            to = pl.ds(g * 8, 8)
-            north_ref[lev, to, :] = jnp.where(n3 > 0.0, f_ref[high, :], a_ref[high, :]) * w3
-            south_ref[lev, to, :] = f_ref[low, :] * w0
-            south_ref[n_lev + lev, to, :] = a_ref[low, :] * w0
-        return 0
-
-    lax.fori_loop(0, n_lev, body, 0, unroll=UNROLL)
     for lev in range(n_lev):
         page, line = n_lev + lev // n_pair, lev % n_pair
         north_ref[page, line : line + 1, :] = nf_ref[lev, n_rows - 1 : n_rows, :]
@@ -171,11 +200,30 @@
     low = depth[0:1].astype(F32)
     north_ref[n_lev + n_lev // n_pair] = jnp.broadcast_to(high, (n_pair, LANES))
     south_ref[2 * n_lev] = jnp.broadcast_to(low, (n_pair, LANES))
+    for g in range(n_pair // 8):
+        for pair in large[2 * g : 2 * g + 2]:
+            for copy in pair:
+                copy.wait()
+
+        def body(lev, _, g=g):
+            wet = jnp.where(first + lev < depth, 1.0, 0.0)
+            w0 = spread(wet[0:1])
+            w3 = spread(wet[n_rows - 1 : n_rows])
+            n3 = spread(nf_ref[lev, n_rows - 1 : n_rows, :])
+            at = g * 8 * stride + lev * n_rows
+            low, high = pl.ds(at, 8, stride=stride), pl.ds(at + n_rows - 1, 8, stride=stride)
+            to = pl.ds(g * 8, 8)
+            north_ref[lev, to, :] = jnp.where(n3 > 0.0, f_ref[high, :], a_ref[high, :]) * w3
+            south_ref[lev, to, :] = f_ref[low, :] * w0
+            south_ref[n_lev + lev, to, :] = a_ref[low, :] * w0
+            return 0
+
+        lax.fori_loop(0, n_lev, body, 0, unroll=UNROLL)
 
 
 def prepare(
     n_lev, n_pair, n_rows, flags_ref, f_ref, a_ref, ef_ref, nf_ref, mix_ref, depth_ref, color_ref, fold_ref,
-    xe_ref, xi_ref, pi_ref, c_ref, wx_ref, hot_ref, mf_ref, inv_ref,
+    xe_ref, pi_ref, be_ref, c_ref, wx_ref, hot_ref, mf_ref, inv_ref, xi_ref,
 ):
     halves = n_pair // 8
     stride = n_lev * n_rows
@@ -252,46 +300,49 @@
     for row in range(n_rows):
         hot_ref[row] = jnp.where(color_ref[row : row + 1, :] == ids, 1.0, 0.0)
 
-    inner_sweep(n_lev, n_pair, flags_ref, xe_ref, xi_ref, c_ref, hot_ref, pi_ref)
+    inner_sweep(n_lev, n_pair, flags_ref, xe_ref, xi_ref, c_ref, None, hot_ref, pi_ref, be_ref)
     fold_rows(
         flags_ref, fold_ref, nf_ref, lambda lev, kind, g: rows_at(xe_ref, 1, lev, kind, g, halves), mf_ref, n_lev, n_pair
     )
 
 
-def inner_sweep(n_lev, n_pair, flags_ref, xe_ref, xi_ref, c_ref, hot_ref, pi_ref):
-    halves = n_pair // 8
+def inner_sweep(n_lev, n_pair, flags_ref, xe_ref, xi_ref, c_ref, ec_ref, hot_ref, pi_ref, be_ref):
+    halves = n_pair // 8
+
+    def at(ref, line):
+        return lambda lev, kind, g: rows_at(ref, line, lev, kind, g, halves)
+
+    x = [at(xe_ref, 0), at(xi_ref, 0), at(xi_ref, 1), at(xe_ref, 1)]
 
     def row(number):
-        line = number - 1
-
-        def at(ref, which):
-            return lambda lev, kind, g: rows_at(ref, which, lev, kind, g, halves)
-
-        return (
-            lambda which, lev: pick(c_ref, which, lev, number),
-            lambda g: hot_ref[number, pl.ds(g * 8, 8), :],
-            at(xi_ref, line),
-            at(xe_ref, 0) if line == 0 else at(xi_ref, 0),
-            at(xi_ref, 1) if line == 0 else at(xe_ref, 1),
-        )
+        edge = {0: {C0F: E0F, C0A: E0A}, 3: {C0F: T0F, C0A: T0A}}.get(number, {}) if ec_ref is not None else {}
+
+        def coef(which, lev):
+            return ec_ref[edge[which], lev] if which in edge else pick(c_ref, which, lev, number)
+
+        sides = []
+        if number > 0:
+            sides.append((CSF, x[number - 1]))
+        if number < 3:
+            sides.append((CNF, x[number + 1]))
+        explicit = own_part(n_pair, coef, lambda g: hot_ref[number, pl.ds(g * 8, 8), :], x[number], sides)
+        return lambda lev: coef(UP, lev), explicit, number in (1, 2)
 
     def put(lev, i, kind, g, v):
-        pi_ref[lev, i, pl.ds((kind * halves + g) * 8, 8), :] = v
-
-    sweep(flags_ref, n_lev, n_pair, [row(1), row(2)], put, lambda *_: None)
-
-
-def edge_sweep(
-    is_first, n_lev, n_pair, flags_ref, xe_ref, xi_ref, pi_ref, c_ref, hot_ref, mf_ref, ms_ref, mn_ref, ec_in, *rest
-):
+        to, line = (pi_ref, i) if i < 2 else (be_ref, i - 2)
+        to[lev, line, pl.ds((kind * halves + g) * 8, 8), :] = v
+
+    sweep(flags_ref, n_lev, n_pair, [row(1), row(2), row(0), row(3)], put, lambda *_: None)
+
+
+def edge_sweep(is_first, n_lev, n_pair, flags_ref, be_ref, pi_ref, c_ref, mf_ref, ms_ref, mn_ref, *rest):
     halves = n_pair // 8
     is_top = flags_ref[1] == 1
     if is_first:
-        nf_ref, depth_ref, fold_ref = ec_in
-        pe_ref, edge_ref, ec_ref, fs_ref = rest
+        xe_ref, nf_ref, depth_ref, fold_ref, pe_ref, edge_ref, ec_ref, fs_ref = rest
         first = flags_ref[0] * n_lev
         depth = depth_ref[...]
-        own0, own3 = depth[0:1], depth[3:4]
+        own3 = depth[3:4]
         page = n_lev + n_lev // n_pair
         south_depth = ms_ref[page, 0:1, :]
         folded = jnp.take_along_axis(spread(own3.astype(F32)), spread(fold_ref[0:1, :]), axis=1)[0:1]
@@ -315,19 +366,9 @@
             ec_ref[TNF, lev] = spread(nm)
             ec_ref[TNA, lev] = spread(np_)
     else:
-        ec_ref = ec_in
-        pe_ref, edge_ref = rest
-
-    low = {C0F: E0F, C0A: E0A, CSF: ESF, CSA: ESA}
-    high = {C0F: T0F, C0A: T0A, CNF: TNF, CNA: TNA}
-
-    def coef(number, table):
-        def get(which, lev):
-            return ec_ref[table[which], lev] if which in table else pick(c_ref, which, lev, number)
-
-        return get
-
-    def north_of_edge(lev, kind, g):
+        ec_ref, pe_ref, edge_ref = rest
+
+    def come_north(lev, g):
         to = pl.ds(g * 8, 8)
         if is_first:
             n3 = spread(nf_ref[lev, 3:4, :])
@@ -336,25 +377,22 @@
             come = mn_ref[lev, to, :]
         return jnp.where(is_top, mf_ref[lev, to, :], come)
 
-    def at(ref, which):
-        return lambda lev, kind, g: rows_at(ref, which, lev, kind, g, halves)
-
-    rows = [
-        (
-            coef(0, low),
-            lambda g: hot_ref[0, pl.ds(g * 8, 8), :],
-            at(xe_ref, 0),
-            lambda lev, kind, g: ms_ref[lev, pl.ds(g * 8, 8), :],
-            at(xi_ref, 0),
-        ),
-        (
-            coef(3, high),
-            lambda g: hot_ref[3, pl.ds(g * 8, 8), :],
-            at(xe_ref, 1),
-            at(xi_ref, 1),
-            north_of_edge,
-        ),
-    ]
+    def row(i, number, inflow, come):
+        def explicit(lev):
+            ks = [ec_ref[inflow + kind, lev] for kind in range(2)]
+            ms = [come(lev, g) for g in range(halves)]
+            out = []
+            for kind in range(2):
+                vs = []
+                for g in range(halves):
+                    v = rows_at(be_ref, i, lev, kind, g, halves) + ks[kind] * ms[g]
+                    if is_first:
+                        v = v - ks[1 - kind] * rows_at(xe_ref, i, lev, kind, g, halves)
+                    vs.append(v)
+                out.append(vs)
+            return out
+
+        return lambda lev: pick(c_ref, UP, lev, number), explicit, True
 
     def put(lev, i, kind, g, v):
         pe_ref[lev, i, pl.ds((kind * halves + g) * 8, 8), :] = v
@@ -362,19 +400,12 @@
     def last(i, kind, g, v):
         edge_ref[3 * i, pl.ds((kind * halves + g) * 8, 8), :] = v
 
+    rows = [row(0, 0, ESF, lambda lev, g: ms_ref[lev, pl.ds(g * 8, 8), :]), row(1, 3, TNF, come_north)]
     sweep(flags_ref, n_lev, n_pair, rows, put, last)
     k0, dk = order(flags_ref, n_lev)
     mid = k0 + dk * (n_lev - 1)
     edge_ref[1] = pi_ref[mid, 0]
     edge_ref[2] = pi_ref[mid, 1]
-
-
-def first_edge(n_lev, n_pair, *refs):
-    edge_sweep(True, n_lev, n_pair, *refs[:9], refs[9:12], *refs[12:])
-
-
-def next_edge(n_lev, n_pair, *refs):
-    edge_sweep(False, n_lev, n_pair, *refs)
 
 
 def tallies(is_first, in_ref, out_ref, n_lev):
@@ -414,9 +445,11 @@
     )
 
 
-def inner(is_first, n_lev, n_pair, flags_ref, pi_ref, far_ref, c_ref, wx_ref, nf_ref, fold_ref, hot_ref, xe_ref, *rest):
-    halves = n_pair // 8
-    acc_ref, (xi_ref, pn_ref, mf_ref, out_ref) = (None, rest) if is_first else (rest[0], rest[1:])
+def inner(
+    is_first, n_lev, n_pair, flags_ref, pi_ref, far_ref, c_ref, ec_ref, wx_ref, nf_ref, fold_ref, hot_ref, xe_ref, *rest
+):
+    halves = n_pair // 8
+    acc_ref, (pn_ref, be_ref, mf_ref, out_ref, xi_ref) = (None, rest) if is_first else (rest[0], rest[1:])
     acc_in, acc_out = tallies(is_first, acc_ref, out_ref, n_lev)
 
     def put(lev, i, kind, g, v):
@@ -426,7 +459,7 @@
         flags_ref, n_lev, n_pair, (1, 2), wx_ref, far_ref, c_ref,
         lambda lev, i, kind, g: rows_at(pi_ref, i, lev, kind, g, halves), put, acc_in, acc_out,
     )
-    inner_sweep(n_lev, n_pair, flags_ref, xe_ref, xi_ref, c_ref, hot_ref, pn_ref)
+    inner_sweep(n_lev, n_pair, flags_ref, xe_ref, xi_ref, c_ref, ec_ref, hot_ref, pn_ref, be_ref)
     fold_rows(
         flags_ref, fold_ref, nf_ref, lambda lev, kind, g: rows_at(xe_ref, 1, lev, kind, g, halves), mf_ref, n_lev, n_pair
     )
@@ -434,22 +467,37 @@
 
 def finish(
     n_lev, n_pair, n_rows, flags_ref, pe_ref, pi_ref, far_ref, c_ref, wx_ref, depth_ref, acce_ref, acci_ref,
-    f_ref, a_ref, sens_ref, te_ref, ti_ref,
+    f_hbm, a_hbm, sens_ref, te_ref, ti_ref, f_ref, a_ref, sems,
 ):
     halves = n_pair // 8
     stride = n_lev * n_rows
-
-    for rows, p_ref, acc_ref, t_ref in (((0, 3), pe_ref, acce_ref, te_ref), ((1, 2), pi_ref, acci_ref, ti_ref)):
-        acc_in, acc_out = tallies(False, acc_ref, t_ref, n_lev)
-
-        def put(lev, i, kind, g, v, rows=rows):
-            to = f_ref if kind == 0 else a_ref
-            to[pl.ds(g * 8 * stride + lev * n_rows + rows[i], 8, stride=stride), :] = v
-
-        back(
-            flags_ref, n_lev, n_pair, rows, wx_ref, far_ref, c_ref,
-            lambda lev, i, kind, g, p_ref=p_ref: rows_at(p_ref, i, lev, kind, g, halves), put, acc_in, acc_out,
-        )
+    bottom = lax.axis_index("level")
+    ps = [(pe_ref, 0), (pi_ref, 0), (pi_ref, 1), (pe_ref, 1)]
+    e_in, e_out = tallies(False, acce_ref, te_ref, n_lev)
+    i_in, i_out = tallies(False, acci_ref, ti_ref, n_lev)
+    copies = []
+
+    def put(lev, i, kind, g, v):
+        to = f_ref if kind == 0 else a_ref
+        to[pl.ds(g * 8 * stride + lev * n_rows + i, 8, stride=stride), :] = v
+
+    def done(piece):
+        low = jnp.where(bottom == 0, n_lev - (piece + 1) * PIECE, piece * PIECE)
+        at = pl.ds(pl.multiple_of(low * n_rows, PIECE * n_rows), PIECE * n_rows)
+        for kind, (ref, hbm) in enumerate(((f_ref, f_hbm), (a_ref, a_hbm))):
+            copy = pltpu.make_async_copy(
+                ref.reshape(n_pair, stride, LANES).at[:, at, :], hbm.at[:, at, :], sems.at[2 * piece + kind]
+            )
+            copy.start()
+            copies.append(copy)
+
+    back(
+        flags_ref, n_lev, n_pair, range(4), wx_ref, far_ref, c_ref,
+        lambda lev, i, kind, g: rows_at(ps[i][0], ps[i][1], lev, kind, g, halves), put,
+        lambda at, i: e_in(at, i // 3) if i in (0, 3) else i_in(at, i - 1),
+        lambda at, i, v: e_out(at, i // 3, v) if i in (0, 3) else i_out(at, i - 1, v),
+        done,
+    )
     first = flags_ref[0] * n_lev
     depth = depth_ref[...]
 
@@ -462,23 +510,34 @@
         return 0
 
     lax.fori_loop(0, n_lev, reduce, 0, unroll=UNROLL)
+    for copy in copies:
+        copy.wait()
 
 
 def vmem(*shape):
     return pltpu.VMEM(shape, F32)
 
 
-def call(kernel, outs, args, flops, scratch=()):
+def call(kernel, outs, args, flops, scratch=(), first=pltpu.SMEM, hbm=0):
     spec = pl.BlockSpec(memory_space=pltpu.VMEM)
+    far = pl.BlockSpec(memory_space=pltpu.HBM)
     return pl.pallas_call(
         kernel,
         out_shape=tuple(outs),
-        in_specs=[pl.BlockSpec(memory_space=pltpu.SMEM)] + [spec] * (len(args) - 1),
-        out_specs=tuple([spec] * len(outs)),
+        in_specs=[pl.BlockSpec(memory_space=pltpu.SMEM)] + [spec] * (len(args) - 1)
+        if first is pltpu.SMEM
+        else [far] * len(args),
+        out_specs=tuple([far] * hbm + [spec] * (len(outs) - hbm)),
         scratch_shapes=list(scratch),
         compiler_params=pltpu.CompilerParams(vmem_limit_bytes=24 * 2**20),
         cost_estimate=pl.CostEstimate(flops=flops, bytes_accessed=flops // 8, transcendentals=0),
-    )(args[0], *[pltpu.with_memory_space_constraint(a, pltpu.VMEM) for a in args[1:]])
+    )(
+        *(
+            args[:1] + [pltpu.with_memory_space_constraint(a, pltpu.VMEM) for a in args[1:]]
+            if first is pltpu.SMEM
+            else [pltpu.with_memory_space_constraint(a, pltpu.HBM) for a in args]
+        )
+    )
 
 
 def per_device(forward_init, adjoint_init, east_flow, north_flow, mixing, depth, color, fold):
@@ -503,40 +562,50 @@
     work = n_lev * n_rows * n_all * n_x
     pages = n_lev // n_pair
 
-    to_north, to_south = call(
+    flat = vmem(n_pair * n_lev * n_rows, n_x)
+    to_north, to_south, f2, a2, north_flow, depth = call(
         functools.partial(send_first, n_lev, n_pair, n_rows),
-        [vmem(n_lev + pages + 1, n_pair, n_x), vmem(2 * n_lev + 1, n_pair, n_x)],
-        [flags, f2, a2, north_flow, depth],
+        [
+            vmem(n_lev + pages + 1, n_pair, n_x),
+            vmem(2 * n_lev + 1, n_pair, n_x),
+            flat,
+            flat,
+            vmem(n_lev, n_rows, n_x),
+            pltpu.VMEM((n_rows, n_x), jnp.int32),
+        ],
+        [f2, a2, north_flow, depth],
         work,
-    )
+        [pltpu.SemaphoreType.DMA((2 + n_pair // 2,))],
+        first=pltpu.HBM,
+    )
+    from_north = lax.ppermute(to_south, "horiz", southward)
     from_south = lax.ppermute(to_north, "horiz", northward)
-    from_north = lax.ppermute(to_south, "horiz", southward)
     state = vmem(n_lev, 2, n_all, n_x)
     halo = vmem(n_lev, n_pair, n_x)
     acc = vmem(n_lev + 1, 2, 8, n_x)
-    xe, xi, pi, c, wx, hot, mf = call(
+    xe, pi, be, c, wx, hot, mf = call(
         functools.partial(prepare, n_lev, n_pair, n_rows),
-        [state, state, state, vmem(13, n_lev, n_rows, n_x), vmem(3, n_rows, n_x), vmem(n_rows, n_pair, n_x), halo],
+        [state] * 3 + [vmem(13, n_lev, n_rows, n_x), vmem(3, n_rows, n_x), vmem(n_rows, n_pair, n_x), halo],
         [flags, f2, a2, east_flow, north_flow, mixing, depth, color, fold2],
         work * 10,
-        [vmem(n_lev, n_rows, n_x)],
+        [vmem(n_lev, n_rows, n_x), state],
     )
     edges = vmem(n_rows, n_all, n_x)
     acce = acci = None
     for step in range(STEPS):
         if step == 0:
             pe, edge, ec, fs = call(
-                functools.partial(first_edge, n_lev, n_pair),
+                functools.partial(edge_sweep, True, n_lev, n_pair),
                 [state, edges, vmem(8, n_lev, 8, n_x), vmem(n_lev, 8, n_x)],
-                [flags, xe, xi, pi, c, hot, mf, from_south, from_north, north_flow, depth, fold2],
-                work * 5,
+                [flags, be, pi, c, mf, from_south, from_north, xe, north_flow, depth, fold2],
+                work * 3,
             )
         else:
             pe, edge = call(
-                functools.partial(next_edge, n_lev, n_pair),
+                functools.partial(edge_sweep, False, n_lev, n_pair),
                 [state, edges],
-                [flags, xe, xi, pi, c, hot, mf, from_south, from_north, ec],
-                work * 5,
+                [flags, be, pi, c, mf, from_south, from_north, ec],
+                work * 2,
             )
         far = lax.ppermute(edge, "level", swap)
         if step == STEPS - 1:
@@ -551,19 +620,21 @@
         from_south = lax.ppermute(to_north, "horiz", northward)
         from_north = lax.ppermute(to_south, "horiz", southward)
         more = [] if step == 0 else [acci]
-        xi, pi, mf, acci = call(
+        pi, be, mf, acci = call(
             functools.partial(inner, step == 0, n_lev, n_pair),
             [state, state, halo, acc],
-            [flags, pi, far, c, wx, north_flow, fold2, hot, xe] + more,
-            work * 7,
+            [flags, pi, far, c, ec, wx, north_flow, fold2, hot, xe] + more,
+            work * 9,
+            [state],
         )
-    flat = vmem(n_pair * n_lev * n_rows, n_x)
+    out = jax.ShapeDtypeStruct((n_pair, n_lev * n_rows, n_x), F32)
     f_out, a_out, sens = call(
         functools.partial(finish, n_lev, n_pair, n_rows),
-        [flat, flat, vmem(n_lev, n_rows, n_x)],
+        [out, out, vmem(n_lev, n_rows, n_x)],
         [flags, pe, pi, far, c, wx, depth, acce, acci],
         work * 4,
-        [acc, acc],
+        [acc, acc, flat, flat, pltpu.SemaphoreType.DMA((2 * n_lev // PIECE,))],
+        hbm=2,
     )
     sens = sens + lax.ppermute(sens, "tracer", swap)
     return f_out.reshape(forward_init.shape), a_out.reshape(adjoint_init.shape), sens

time: 102 us -> 93.7 us (0.919)
  Pallas kernels: 29.5 us -> 23.4 us
  local copies, waits for them, and re-layouts: 6.55 us -> 0.68 us
  waiting for transfers between devices: 20.3 us -> 24.3 us
    pallas_call x13, Pallas kernels: 29.5 us -> 23.4 us  [call(): pl.pallas_call(kernel, out_shape=tuple(outs), in_specs=[pl.BlockSpec(memo...]
    unnamed x20 -> x8, local copies, waits for them, and re-layouts: 6.55 us -> 0.68 us
    ppermute x4, waiting for transfers between devices: 9.36 us -> 11.6 us  [per_device(): from_south = lax.ppermute(to_north, 'horiz', northward)]
  transfers between devices with their start and end apart: 13 -> 13, of which waited for: 8 -> 9; matrix products, arithmetic and copies ran while one was open for 2% -> 0% of each run, Pallas kernels for 13% -> 12%
where the time goes in v2:
time: 93.7 us; the launch traced here: 91.9 us
  starting transfers between devices  42.1 us (45%)
  waiting for transfers between devices  24.3 us (26%)
  Pallas kernels  23.4 us (25%)
    ppermute x4, starting transfers between devices, per_device(): from_north = lax.ppermute(to_south, 'horiz', southward)  23.4 us
    pallas_call x13, Pallas kernels, call(): pl.pallas_call(kernel, out_shape=tuple(outs), in_specs=[pl.BlockSpec(memo...  23.4 us
    ppermute x4, waiting for transfers between devices, per_device(): far = lax.ppermute(edge, 'level', swap)  11.7 us
    ppermute x4, waiting for transfers between devices, per_device(): from_south = lax.ppermute(to_north, 'horiz', northward)  11.6 us
    ppermute x1, starting transfers between devices, per_device(): sens = sens + lax.ppermute(sens, 'tracer', swap)  10.3 us
    ppermute x4, starting transfers between devices, per_device(): far = lax.ppermute(edge, 'level', swap)  8.11 us
  transfers between devices with their start and end apart: 13, of which 9 were waited for; matrix products, arithmetic and copies ran while one was open for 0% of the time, Pallas kernels for 12%

profile of v2, /device:TPU:3, one launch (start us, length us, event | category | flops | bytes accessed | tf_op | source)
XLA Modules:
  0.0 91.9 jit_solution(7336639633148648809)
XLA Ops:
  0.7 2.8 %shard_map.103 = (f32[35,16,128]{2,1,0:T(8,128)S(1)}, f32[65,16,128]{2,1,0:T(8,128)}, f32[2048,128]{1,0:T(8,128)S(1)}, f32[2048,128]{1,0:T(8,128)S(1)}, f32[32,4,128]{2,1,0:T(4,128)S(1)}, /*index=5*/s32[4,128]{1,0:T(4,128)S(1)}) custom-call(f32[2048,128]{1,0:T(8,128)} %bitcast.14, f32[2048,128]{1,0:T(8,128)} %bitcast.15, f32[32,4,128]{2,1,0:T(4,128)} %nf_hbm.1, ...), custom_call_target="tpu_custom_call" | custom-call | flops 524288 | bytes 65536 | tf_op jit(solution)/shard_map/pallas_call | solution.py:524
  3.5 6.2 %collective-permute-start.1 = (f32[65,16,128]{2,1,0:T(8,128)}, f32[65,16,128]{2,1,0:T(8,128)S(1)}, u32[]{:S(2)}, u32[]{:S(2)}) collective-permute-start(f32[65,16,128]{2,1,0:T(8,128)} %get-tuple-element.62), channel_id=1, source_target_pairs={{4,0},{8,4},{12,8},{16,12},{20,16},{24,20},{28,24},{32,28},{36,32}... | collective-permute-start | bytes 1597448 | tf_op jit(solution)/shard_map/ppermute | solution.py:581
  10.5 4.3 %shard_map.104 = (f32[32,2,32,128]{3,2,1,0:T(8,128)S(1)}, f32[32,2,32,128]{3,2,1,0:T(8,128)S(1)}, f32[32,2,32,128]{3,2,1,0:T(8,128)S(1)}, f32[13,32,4,128]{3,2,1...) custom-call(s32[4]{0:T(128)S(1)} %pad_add_fusion.flags_ref, ...), custom_call_target="tpu_custom_call" | custom-call | flops 5242880 | bytes 655360 | tf_op jit(solution)/shard_map/pallas_call | solution.py:524
  14.8 6.5 %collective-permute-done.ms_ref = f32[35,16,128]{2,1,0:T(8,128)S(1)} collective-permute-done((f32[35,16,128]{2,1,0:T(8,128)S(1)}, f32[35,16,128]{2,1,0:T(8,128)S(1)}, u32[]{:S(2)}, u32[]{:S(2)}) %collective-permute-start) | collective-permute-done | bytes 286752 | tf_op jit(solution)/shard_map/ppermute | solution.py:582
  21.4 1.2 %shard_map.105 = (f32[32,2,32,128]{3,2,1,0:T(8,128)S(1)}, f32[4,32,128]{2,1,0:T(8,128)S(1)}, f32[8,32,8,128]{3,2,1,0:T(8,128)S(1)}, f32[32,8,128]{2,1,0:T(8,128)S(1)}) custom-call(s32[4]{0:T(128)S(1)} %pad_add_fusion.flags_ref, f32[32,2,32,128]{3,2,1,0:T(8,128)S(1)} %get-tuple-element.58.be_ref, f32[32,2,32,128]{3,2,1,0:T(8,128)S(1)} %get-tuple-element.57.pi_ref, ...), custom_call_target="tpu_custom_call" | custom-call | flops 1572864 | bytes 196608 | tf_op jit(solution)/shard_map/pallas_call | solution.py:524
  22.5 2.2 %collective-permute-start.2 = (f32[4,32,128]{2,1,0:T(8,128)S(1)}, f32[4,32,128]{2,1,0:T(8,128)S(1)}, u32[]{:S(2)}, u32[]{:S(2)}) collective-permute-start(f32[4,32,128]{2,1,0:T(8,128)S(1)} %get-tuple-element.64), channel_id=1, source_target_pairs={{0,1},{1,0},{2,3},{3,2},{4,5},{5,4},{6,7},{7,6},{8,9},{9,8},{10,11... | collective-permute-start | bytes 196616 | tf_op jit(solution)/shard_map/ppermute | solution.py:610
  24.7 2.5 %collective-permute-done.2.far_ref = f32[4,32,128]{2,1,0:T(8,128)S(1)} collective-permute-done((f32[4,32,128]{2,1,0:T(8,128)S(1)}, f32[4,32,128]{2,1,0:T(8,128)S(1)}, u32[]{:S(2)}, u32[]{:S(2)}) %collective-permute-start.2) | collective-permute-done | bytes 65568 | tf_op jit(solution)/shard_map/ppermute | solution.py:610
  28.1 5.9 %collective-permute-start.4 = (f32[32,16,128]{2,1,0:T(8,128)S(1)}, f32[32,16,128]{2,1,0:T(8,128)S(1)}, u32[]{:S(2)}, u32[]{:S(2)}) collective-permute-start(f32[32,16,128]{2,1,0:T(8,128)S(1)} %get-tuple-element.75), channel_id=1, source_target_pairs={{4,0},{8,4},{12,8},{16,12},{20,16},{24,20},{28,24},{32,28},{36,32}... | collective-permute-start | bytes 786440 | tf_op jit(solution)/shard_map/ppermute | solution.py:621
  34.0 2.2 %shard_map.107 = (f32[32,2,32,128]{3,2,1,0:T(8,128)S(1)}, f32[32,2,32,128]{3,2,1,0:T(8,128)S(1)}, f32[32,16,128]{2,1,0:T(8,128)S(1)}, f32[33,2,8,128]{3,2,1,0:T(8,128)S(1)}) custom-call(s32[4]{0:T(128)S(1)} %pad_add_fusion.flags_ref, f32[32,2,32,128]{3,2,1,0:T(8,128)S(1)} %get-tuple-element.57.pi_ref, f32[4,32,128]{2,1,0:T(8,128)S(1)} %collective-permute-done.2.far_ref, ...), custom_call_target="tpu_custom_call" | custom-call | flops 4718592 | bytes 589824 | tf_op jit(solution)/shard_map/pallas_call | solution.py:524
  36.2 1.4 %collective-permute-done.3.ms_ref = f32[32,16,128]{2,1,0:T(8,128)S(1)} collective-permute-done((f32[32,16,128]{2,1,0:T(8,128)S(1)}, f32[32,16,128]{2,1,0:T(8,128)S(1)}, u32[]{:S(2)}, u32[]{:S(2)}) %collective-permute-start.3) | collective-permute-done | bytes 262176 | tf_op jit(solution)/shard_map/ppermute | solution.py:620
  38.5 2.2 %collective-permute-start.5 = (f32[4,32,128]{2,1,0:T(8,128)S(1)}, f32[4,32,128]{2,1,0:T(8,128)S(1)}, u32[]{:S(2)}, u32[]{:S(2)}) collective-permute-start(f32[4,32,128]{2,1,0:T(8,128)S(1)} %get-tuple-element.76), channel_id=1, source_target_pairs={{0,1},{1,0},{2,3},{3,2},{4,5},{5,4},{6,7},{7,6},{8,9},{9,8},{10,11... | collective-permute-start | bytes 196616 | tf_op jit(solution)/shard_map/ppermute | solution.py:610
  40.7 3.2 %collective-permute-done.5.far_ref = f32[4,32,128]{2,1,0:T(8,128)S(1)} collective-permute-done((f32[4,32,128]{2,1,0:T(8,128)S(1)}, f32[4,32,128]{2,1,0:T(8,128)S(1)}, u32[]{:S(2)}, u32[]{:S(2)}) %collective-permute-start.5) | collective-permute-done | bytes 65568 | tf_op jit(solution)/shard_map/ppermute | solution.py:610
  44.9 5.7 %collective-permute-start.7 = (f32[32,16,128]{2,1,0:T(8,128)S(1)}, f32[32,16,128]{2,1,0:T(8,128)S(1)}, u32[]{:S(2)}, u32[]{:S(2)}) collective-permute-start(f32[32,16,128]{2,1,0:T(8,128)S(1)} %get-tuple-element.85), channel_id=1, source_target_pairs={{4,0},{8,4},{12,8},{16,12},{20,16},{24,20},{28,24},{32,28},{36,32}... | collective-permute-start | bytes 786440 | tf_op jit(solution)/shard_map/ppermute | solution.py:621
  50.6 2.3 %shard_map.110 = (f32[32,2,32,128]{3,2,1,0:T(8,128)S(1)}, f32[32,2,32,128]{3,2,1,0:T(8,128)S(1)}, f32[32,16,128]{2,1,0:T(8,128)S(1)}, f32[33,2,8,128]{3,2,1,0:T(8,128)S(1)}) custom-call(s32[4]{0:T(128)S(1)} %pad_add_fusion.flags_ref, f32[32,2,32,128]{3,2,1,0:T(8,128)S(1)} %get-tuple-element.71.pi_ref, f32[4,32,128]{2,1,0:T(8,128)S(1)} %collective-permute-done.5.far_ref, ...), custom_call_target="tpu_custom_call" | custom-call | flops 4718592 | bytes 589824 | tf_op jit(solution)/shard_map/pallas_call | solution.py:524
  52.8 2.2 %collective-permute-done.6.ms_ref = f32[32,16,128]{2,1,0:T(8,128)S(1)} collective-permute-done((f32[32,16,128]{2,1,0:T(8,128)S(1)}, f32[32,16,128]{2,1,0:T(8,128)S(1)}, u32[]{:S(2)}, u32[]{:S(2)}) %collective-permute-start.6) | collective-permute-done | bytes 262176 | tf_op jit(solution)/shard_map/ppermute | solution.py:620
  55.9 1.1 %collective-permute-start.8 = (f32[4,32,128]{2,1,0:T(8,128)S(1)}, f32[4,32,128]{2,1,0:T(8,128)S(1)}, u32[]{:S(2)}, u32[]{:S(2)}) collective-permute-start(f32[4,32,128]{2,1,0:T(8,128)S(1)} %get-tuple-element.86), channel_id=1, source_target_pairs={{0,1},{1,0},{2,3},{3,2},{4,5},{5,4},{6,7},{7,6},{8,9},{9,8},{10,11... | collective-permute-start | bytes 196616 | tf_op jit(solution)/shard_map/ppermute | solution.py:610
  57.0 3.8 %collective-permute-done.8.far_ref = f32[4,32,128]{2,1,0:T(8,128)S(1)} collective-permute-done((f32[4,32,128]{2,1,0:T(8,128)S(1)}, f32[4,32,128]{2,1,0:T(8,128)S(1)}, u32[]{:S(2)}, u32[]{:S(2)}) %collective-permute-start.8) | collective-permute-done | bytes 65568 | tf_op jit(solution)/shard_map/ppermute | solution.py:610
  61.8 5.7 %collective-permute-start.10 = (f32[32,16,128]{2,1,0:T(8,128)S(1)}, f32[32,16,128]{2,1,0:T(8,128)S(1)}, u32[]{:S(2)}, u32[]{:S(2)}) collective-permute-start(f32[32,16,128]{2,1,0:T(8,128)S(1)} %get-tuple-element.95), channel_id=1, source_target_pairs={{4,0},{8,4},{12,8},{16,12},{20,16},{24,20},{28,24},{32,28},{36,32}... | collective-permute-start | bytes 786440 | tf_op jit(solution)/shard_map/ppermute | solution.py:621
  67.4 2.3 %shard_map.113 = (f32[32,2,32,128]{3,2,1,0:T(8,128)S(1)}, f32[32,2,32,128]{3,2,1,0:T(8,128)S(1)}, f32[32,16,128]{2,1,0:T(8,128)S(1)}, f32[33,2,8,128]{3,2,1,0:T(8,128)S(1)}) custom-call(s32[4]{0:T(128)S(1)} %pad_add_fusion.flags_ref, f32[32,2,32,128]{3,2,1,0:T(8,128)S(1)} %get-tuple-element.81.pi_ref, f32[4,32,128]{2,1,0:T(8,128)S(1)} %collective-permute-done.8.far_ref, ...), custom_call_target="tpu_custom_call" | custom-call | flops 4718592 | bytes 589824 | tf_op jit(solution)/shard_map/pallas_call | solution.py:524
  69.7 1.5 %collective-permute-done.9.ms_ref = f32[32,16,128]{2,1,0:T(8,128)S(1)} collective-permute-done((f32[32,16,128]{2,1,0:T(8,128)S(1)}, f32[32,16,128]{2,1,0:T(8,128)S(1)}, u32[]{:S(2)}, u32[]{:S(2)}) %collective-permute-start.9) | collective-permute-done | bytes 262176 | tf_op jit(solution)/shard_map/ppermute | solution.py:620
  72.0 2.5 %collective-permute-start.11 = (f32[4,32,128]{2,1,0:T(8,128)S(1)}, f32[4,32,128]{2,1,0:T(8,128)S(1)}, u32[]{:S(2)}, u32[]{:S(2)}) collective-permute-start(f32[4,32,128]{2,1,0:T(8,128)S(1)} %get-tuple-element.97), channel_id=1, source_target_pairs={{0,1},{1,0},{2,3},{3,2},{4,5},{5,4},{6,7},{7,6},{8,9},{9,8},{10,11... | collective-permute-start | bytes 196616 | tf_op jit(solution)/shard_map/ppermute | solution.py:610
  74.6 2.2 %collective-permute-done.11.far_ref = f32[4,32,128]{2,1,0:T(8,128)S(1)} collective-permute-done((f32[4,32,128]{2,1,0:T(8,128)S(1)}, f32[4,32,128]{2,1,0:T(8,128)S(1)}, u32[]{:S(2)}, u32[]{:S(2)}) %collective-permute-start.11) | collective-permute-done | bytes 65568 | tf_op jit(solution)/shard_map/ppermute | solution.py:610
  76.7 3.3 %shard_map.115 = (f32[16,128,128]{2,1,0:T(8,128)}, f32[16,128,128]{2,1,0:T(8,128)}, f32[32,4,128]{2,1,0:T(4,128)S(1)}) custom-call(s32[4]{0:T(128)S(1)} %pad_add_fusion.flags_ref, f32[32,2,32,128]{3,2,1,0:T(8,128)S(1)} %get-tuple-element.96.pe_ref, f32[32,2,32,128]{3,2,1,0:T(8,128)S(1)} %get-tuple-element.92.pi_ref, ...), custom_call_target="tpu_custom_call" | custom-call | flops 2097152 | bytes 262144 | tf_op jit(solution)/shard_map/pallas_call | solution.py:524
  80.1 10.3 %collective-permute-start.12 = (f32[32,4,128]{2,1,0:T(4,128)S(1)}, f32[32,4,128]{2,1,0:T(4,128)S(1)}, u32[]{:S(2)}, u32[]{:S(2)}) collective-permute-start(f32[32,4,128]{2,1,0:T(4,128)S(1)} %get-tuple-element.102), channel_id=1, source_target_pairs={{0,2},{2,0},{1,3},{3,1},{4,6},{6,4},{5,7},{7,5},{8,10},{10,8},{9,1... | collective-permute-start | bytes 196616 | tf_op jit(solution)/shard_map/ppermute | solution.py:639
  (25 shorter events, 7.5 us)
Async XLA Ops:
  0.6 9.2 %copy-start = (f32[63,4,128]{2,1,0:T(4,128)S(1)}, f32[63,4,128]{2,1,0:T(4,128)}, u32[]{:S(2)}) copy-start(f32[63,4,128]{2,1,0:T(4,128)} %mix_ref.1) | copy-start | bytes 387076
  0.6 9.2 %copy-start.1 = (f32[32,4,128]{2,1,0:T(4,128)S(1)}, f32[32,4,128]{2,1,0:T(4,128)}, u32[]{:S(2)}) copy-start(f32[32,4,128]{2,1,0:T(4,128)} %ef_ref.1) | copy-start | bytes 196612
  3.5 17.9 %collective-permute-start.1 = (f32[65,16,128]{2,1,0:T(8,128)}, f32[65,16,128]{2,1,0:T(8,128)S(1)}, u32[]{:S(2)}, u32[]{:S(2)}) collective-permute-start(f32[65,16,128]{2,1,0:T(8,128)} %get-tuple-element.62), channel_id=1, source_target_pairs={{4,0},{8,4},{12,8},{16,12},{20,16},{24,20},{28,24},{32,28},{36,32}... | collective-permute-start | bytes 1597448 | tf_op jit(solution)/shard_map/ppermute | solution.py:581
  9.8 11.6 %collective-permute-start = (f32[35,16,128]{2,1,0:T(8,128)S(1)}, f32[35,16,128]{2,1,0:T(8,128)S(1)}, u32[]{:S(2)}, u32[]{:S(2)}) collective-permute-start(f32[35,16,128]{2,1,0:T(8,128)S(1)} %get-tuple-element.61), channel_id=1, source_target_pairs={{0,4},{4,8},{8,12},{12,16},{16,20},{20,24},{24,28},{28,32},{32,36}... | collective-permute-start | bytes 860168 | tf_op jit(solution)/shard_map/ppermute | solution.py:582
  9.8 0.7 copy-start.3
  9.8 0.7 copy-start.2
  22.5 4.7 %collective-permute-start.2 = (f32[4,32,128]{2,1,0:T(8,128)S(1)}, f32[4,32,128]{2,1,0:T(8,128)S(1)}, u32[]{:S(2)}, u32[]{:S(2)}) collective-permute-start(f32[4,32,128]{2,1,0:T(8,128)S(1)} %get-tuple-element.64), channel_id=1, source_target_pairs={{0,1},{1,0},{2,3},{3,2},{4,5},{5,4},{6,7},{7,6},{8,9},{9,8},{10,11... | collective-permute-start | bytes 196616 | tf_op jit(solution)/shard_map/ppermute | solution.py:610
  28.0 9.6 %collective-permute-start.3 = (f32[32,16,128]{2,1,0:T(8,128)S(1)}, f32[32,16,128]{2,1,0:T(8,128)S(1)}, u32[]{:S(2)}, u32[]{:S(2)}) collective-permute-start(f32[32,16,128]{2,1,0:T(8,128)S(1)} %get-tuple-element.74), channel_id=1, source_target_pairs={{0,4},{4,8},{8,12},{12,16},{16,20},{20,24},{24,28},{28,32},{32,36}... | collective-permute-start | bytes 786440 | tf_op jit(solution)/shard_map/ppermute | solution.py:620
  28.1 9.5 %collective-permute-start.4 = (f32[32,16,128]{2,1,0:T(8,128)S(1)}, f32[32,16,128]{2,1,0:T(8,128)S(1)}, u32[]{:S(2)}, u32[]{:S(2)}) collective-permute-start(f32[32,16,128]{2,1,0:T(8,128)S(1)} %get-tuple-element.75), channel_id=1, source_target_pairs={{4,0},{8,4},{12,8},{16,12},{20,16},{24,20},{28,24},{32,28},{36,32}... | collective-permute-start | bytes 786440 | tf_op jit(solution)/shard_map/ppermute | solution.py:621
  38.5 5.5 %collective-permute-start.5 = (f32[4,32,128]{2,1,0:T(8,128)S(1)}, f32[4,32,128]{2,1,0:T(8,128)S(1)}, u32[]{:S(2)}, u32[]{:S(2)}) collective-permute-start(f32[4,32,128]{2,1,0:T(8,128)S(1)} %get-tuple-element.76), channel_id=1, source_target_pairs={{0,1},{1,0},{2,3},{3,2},{4,5},{5,4},{6,7},{7,6},{8,9},{9,8},{10,11... | collective-permute-start | bytes 196616 | tf_op jit(solution)/shard_map/ppermute | solution.py:610
  44.8 10.2 %collective-permute-start.6 = (f32[32,16,128]{2,1,0:T(8,128)S(1)}, f32[32,16,128]{2,1,0:T(8,128)S(1)}, u32[]{:S(2)}, u32[]{:S(2)}) collective-permute-start(f32[32,16,128]{2,1,0:T(8,128)S(1)} %get-tuple-element.84), channel_id=1, source_target_pairs={{0,4},{4,8},{8,12},{12,16},{16,20},{20,24},{24,28},{28,32},{32,36}... | collective-permute-start | bytes 786440 | tf_op jit(solution)/shard_map/ppermute | solution.py:620
  44.9 10.1 %collective-permute-start.7 = (f32[32,16,128]{2,1,0:T(8,128)S(1)}, f32[32,16,128]{2,1,0:T(8,128)S(1)}, u32[]{:S(2)}, u32[]{:S(2)}) collective-permute-start(f32[32,16,128]{2,1,0:T(8,128)S(1)} %get-tuple-element.85), channel_id=1, source_target_pairs={{4,0},{8,4},{12,8},{16,12},{20,16},{24,20},{28,24},{32,28},{36,32}... | collective-permute-start | bytes 786440 | tf_op jit(solution)/shard_map/ppermute | solution.py:621
  55.9 5.0 %collective-permute-start.8 = (f32[4,32,128]{2,1,0:T(8,128)S(1)}, f32[4,32,128]{2,1,0:T(8,128)S(1)}, u32[]{:S(2)}, u32[]{:S(2)}) collective-permute-start(f32[4,32,128]{2,1,0:T(8,128)S(1)} %get-tuple-element.86), channel_id=1, source_target_pairs={{0,1},{1,0},{2,3},{3,2},{4,5},{5,4},{6,7},{7,6},{8,9},{9,8},{10,11... | collective-permute-start | bytes 196616 | tf_op jit(solution)/shard_map/ppermute | solution.py:610
  61.7 9.5 %collective-permute-start.9 = (f32[32,16,128]{2,1,0:T(8,128)S(1)}, f32[32,16,128]{2,1,0:T(8,128)S(1)}, u32[]{:S(2)}, u32[]{:S(2)}) collective-permute-start(f32[32,16,128]{2,1,0:T(8,128)S(1)} %get-tuple-element.94), channel_id=1, source_target_pairs={{0,4},{4,8},{8,12},{12,16},{16,20},{20,24},{24,28},{28,32},{32,36}... | collective-permute-start | bytes 786440 | tf_op jit(solution)/shard_map/ppermute | solution.py:620
  61.8 9.4 %collective-permute-start.10 = (f32[32,16,128]{2,1,0:T(8,128)S(1)}, f32[32,16,128]{2,1,0:T(8,128)S(1)}, u32[]{:S(2)}, u32[]{:S(2)}) collective-permute-start(f32[32,16,128]{2,1,0:T(8,128)S(1)} %get-tuple-element.95), channel_id=1, source_target_pairs={{4,0},{8,4},{12,8},{16,12},{20,16},{24,20},{28,24},{32,28},{36,32}... | collective-permute-start | bytes 786440 | tf_op jit(solution)/shard_map/ppermute | solution.py:621
  72.0 4.7 %collective-permute-start.11 = (f32[4,32,128]{2,1,0:T(8,128)S(1)}, f32[4,32,128]{2,1,0:T(8,128)S(1)}, u32[]{:S(2)}, u32[]{:S(2)}) collective-permute-start(f32[4,32,128]{2,1,0:T(8,128)S(1)} %get-tuple-element.97), channel_id=1, source_target_pairs={{0,1},{1,0},{2,3},{3,2},{4,5},{5,4},{6,7},{7,6},{8,9},{9,8},{10,11... | collective-permute-start | bytes 196616 | tf_op jit(solution)/shard_map/ppermute | solution.py:610
  80.1 11.2 %collective-permute-start.12 = (f32[32,4,128]{2,1,0:T(4,128)S(1)}, f32[32,4,128]{2,1,0:T(4,128)S(1)}, u32[]{:S(2)}, u32[]{:S(2)}) collective-permute-start(f32[32,4,128]{2,1,0:T(4,128)S(1)} %get-tuple-element.102), channel_id=1, source_target_pairs={{0,2},{2,0},{1,3},{3,1},{4,6},{6,4},{5,7},{7,5},{8,10},{10,8},{9,1... | collective-permute-start | bytes 196616 | tf_op jit(solution)/shard_map/ppermute | solution.py:639

commit v3 on v2

--- a/solution.py
+++ b/solution.py
@@ -12,11 +12,11 @@
 E0F, E0A, ESF, ESA, T0F, T0A, TNF, TNA = range(8)
 F32 = jnp.float32
 UNROLL = 8
-PIECE = 8
-
-
-def order(flags_ref, n_lev):
-    bottom = flags_ref[0]
+PIECES = 4
+
+
+def order(flags, n_lev):
+    bottom = flags[0]
     return bottom * (n_lev - 1), 1 - 2 * bottom
 
 
@@ -36,8 +36,8 @@
     return spread(c_ref[which, lev, row : row + 1, :])
 
 
-def sweep(flags_ref, n_lev, n_pair, rows, put, last):
-    k0, dk = order(flags_ref, n_lev)
+def sweep(flags, n_lev, n_pair, rows, put, last):
+    k0, dk = order(flags, n_lev)
     halves = n_pair // 8
     zero = jnp.zeros((8, LANES), F32)
 
@@ -85,9 +85,9 @@
     return explicit
 
 
-def back(flags_ref, n_lev, n_pair, rows, wx_ref, far_ref, c_ref, part, put, acc_in, acc_out, done=None):
-    bottom = flags_ref[0]
-    k0, dk = order(flags_ref, n_lev)
+def back(flags, n_lev, n_pair, rows, wx_ref, far_ref, c_ref, part, put, acc_in, acc_out):
+    bottom = flags[0]
+    k0, dk = order(flags, n_lev)
     halves = n_pair // 8
     mid = k0 + dk * (n_lev - 1)
     own, far = [], []
@@ -136,18 +136,11 @@
         store(lev, now)
         return tuple(now)
 
-    if done is None:
-        lax.fori_loop(0, n_lev - 1, body, tuple(own), unroll=UNROLL)
-        return
-    now = lax.fori_loop(0, PIECE - 1, body, tuple(own), unroll=PIECE - 1)
-    done(0)
-    for piece in range(1, n_lev // PIECE):
-        now = lax.fori_loop(piece * PIECE - 1, (piece + 1) * PIECE - 1, body, now, unroll=PIECE)
-        done(piece)
-
-
-def fold_rows(flags_ref, fold_ref, nf_ref, get, mf_ref, n_lev, n_pair):
-    @pl.when(flags_ref[1] == 1)
+    lax.fori_loop(0, n_lev - 1, body, tuple(own), unroll=UNROLL)
+
+
+def fold_rows(flags, fold_ref, nf_ref, get, mf_ref, n_lev, n_pair):
+    @pl.when(flags[1] == 1)
     def _():
         where_to = spread(fold_ref[0:1, :])
 
@@ -167,7 +160,7 @@
 
 
 def send_first(
-    n_lev, n_pair, n_rows, f_hbm, a_hbm, nf_hbm, depth_hbm, north_ref, south_ref, f_ref, a_ref, nf_ref, depth_ref, sems
+    n_lev, n_pair, n_rows, f_hbm, a_hbm, nf_hbm, depth_hbm, even_ref, odd_ref, f_ref, a_ref, nf_ref, depth_ref, sems
 ):
     stride = n_lev * n_rows
     part = 4 * stride
@@ -193,13 +186,11 @@
     for copy in small:
         copy.wait()
     depth = depth_ref[...]
-    for lev in range(n_lev):
-        page, line = n_lev + lev // n_pair, lev % n_pair
-        north_ref[page, line : line + 1, :] = nf_ref[lev, n_rows - 1 : n_rows, :]
+    up_even = lax.rem(lax.axis_index("horiz"), 2) == 0
     high = depth[n_rows - 1 : n_rows].astype(F32)
     low = depth[0:1].astype(F32)
-    north_ref[n_lev + n_lev // n_pair] = jnp.broadcast_to(high, (n_pair, LANES))
-    south_ref[2 * n_lev] = jnp.broadcast_to(low, (n_pair, LANES))
+    even_ref[2 * n_lev] = jnp.broadcast_to(jnp.where(up_even, high, low), (n_pair, LANES))
+    odd_ref[2 * n_lev] = jnp.broadcast_to(jnp.where(up_even, low, high), (n_pair, LANES))
     for g in range(n_pair // 8):
         for pair in large[2 * g : 2 * g + 2]:
             for copy in pair:
@@ -213,23 +204,36 @@
             at = g * 8 * stride + lev * n_rows
             low, high = pl.ds(at, 8, stride=stride), pl.ds(at + n_rows - 1, 8, stride=stride)
             to = pl.ds(g * 8, 8)
-            north_ref[lev, to, :] = jnp.where(n3 > 0.0, f_ref[high, :], a_ref[high, :]) * w3
-            south_ref[lev, to, :] = f_ref[low, :] * w0
-            south_ref[n_lev + lev, to, :] = a_ref[low, :] * w0
+            north = jnp.where(n3 > 0.0, f_ref[high, :], a_ref[high, :]) * w3
+            south = f_ref[low, :] * w0
+            even_ref[lev, to, :] = jnp.where(up_even, north, south)
+            odd_ref[lev, to, :] = jnp.where(up_even, south, north)
+            south = a_ref[low, :] * w0
+            even_ref[n_lev + lev, to, :] = south
+            odd_ref[n_lev + lev, to, :] = south
             return 0
 
         lax.fori_loop(0, n_lev, body, 0, unroll=UNROLL)
 
+    def flow(ref):
+        for lev in range(n_lev):
+            page, line = n_lev + lev // n_pair, lev % n_pair
+            ref[page, line : line + 1, :] = nf_ref[lev, n_rows - 1 : n_rows, :]
+
+    pl.when(up_even)(lambda: flow(even_ref))
+    pl.when(jnp.logical_not(up_even))(lambda: flow(odd_ref))
+
 
 def prepare(
-    n_lev, n_pair, n_rows, flags_ref, f_ref, a_ref, ef_ref, nf_ref, mix_ref, depth_ref, color_ref, fold_ref,
+    n_lev, n_pair, n_rows, f_ref, a_ref, ef_ref, nf_ref, mix_ref, depth_ref, color_ref, fold_ref,
     xe_ref, pi_ref, be_ref, c_ref, wx_ref, hot_ref, mf_ref, inv_ref, xi_ref,
 ):
+    flags = where_am_i(n_pair)
     halves = n_pair // 8
     stride = n_lev * n_rows
-    bottom = flags_ref[0]
+    bottom = flags[0]
     first = bottom * n_lev
-    k0, dk = order(flags_ref, n_lev)
+    k0, dk = order(flags, n_lev)
     depth = depth_ref[...]
 
     def lay(lev, _):
@@ -296,17 +300,17 @@
 
     lax.fori_loop(0, n_lev, coefs, 0, unroll=UNROLL)
 
-    ids = lax.broadcasted_iota(jnp.int32, (n_pair, LANES), 0) + flags_ref[3]
+    ids = lax.broadcasted_iota(jnp.int32, (n_pair, LANES), 0) + flags[3]
     for row in range(n_rows):
         hot_ref[row] = jnp.where(color_ref[row : row + 1, :] == ids, 1.0, 0.0)
 
-    inner_sweep(n_lev, n_pair, flags_ref, xe_ref, xi_ref, c_ref, None, hot_ref, pi_ref, be_ref)
+    inner_sweep(n_lev, n_pair, flags, xe_ref, xi_ref, c_ref, None, hot_ref, pi_ref, be_ref)
     fold_rows(
-        flags_ref, fold_ref, nf_ref, lambda lev, kind, g: rows_at(xe_ref, 1, lev, kind, g, halves), mf_ref, n_lev, n_pair
-    )
-
-
-def inner_sweep(n_lev, n_pair, flags_ref, xe_ref, xi_ref, c_ref, ec_ref, hot_ref, pi_ref, be_ref):
+        flags, fold_ref, nf_ref, lambda lev, kind, g: rows_at(xe_ref, 1, lev, kind, g, halves), mf_ref, n_lev, n_pair
+    )
+
+
+def inner_sweep(n_lev, n_pair, flags, xe_ref, xi_ref, c_ref, ec_ref, hot_ref, pi_ref, be_ref):
     halves = n_pair // 8
 
     def at(ref, line):
@@ -332,26 +336,35 @@
         to, line = (pi_ref, i) if i < 2 else (be_ref, i - 2)
         to[lev, line, pl.ds((kind * halves + g) * 8, 8), :] = v
 
-    sweep(flags_ref, n_lev, n_pair, [row(1), row(2), row(0), row(3)], put, lambda *_: None)
-
-
-def edge_sweep(is_first, n_lev, n_pair, flags_ref, be_ref, pi_ref, c_ref, mf_ref, ms_ref, mn_ref, *rest):
-    halves = n_pair // 8
-    is_top = flags_ref[1] == 1
+    sweep(flags, n_lev, n_pair, [row(1), row(2), row(0), row(3)], put, lambda *_: None)
+
+
+def edge_sweep(is_first, n_lev, n_pair, be_ref, pi_ref, c_ref, mf_ref, even_ref, odd_ref, *rest):
+    flags = where_am_i(n_pair)
+    halves = n_pair // 8
+    is_top = flags[1] == 1
+    up_even = flags[4] == 0
+
+    def from_south(*at):
+        return jnp.where(up_even, odd_ref[at], even_ref[at])
+
+    def from_north(*at):
+        return jnp.where(up_even, even_ref[at], odd_ref[at])
+
     if is_first:
         xe_ref, nf_ref, depth_ref, fold_ref, pe_ref, edge_ref, ec_ref, fs_ref = rest
-        first = flags_ref[0] * n_lev
+        first = flags[0] * n_lev
         depth = depth_ref[...]
         own3 = depth[3:4]
-        page = n_lev + n_lev // n_pair
-        south_depth = ms_ref[page, 0:1, :]
+        south_depth = from_south(2 * n_lev, slice(0, 1), slice(None))
         folded = jnp.take_along_axis(spread(own3.astype(F32)), spread(fold_ref[0:1, :]), axis=1)[0:1]
-        north_depth = jnp.where(is_top, folded, mn_ref[2 * n_lev, 0:1, :])
-        open_south = jnp.where(flags_ref[2] == 1, 0.0, 1.0)
+        north_depth = jnp.where(is_top, folded, from_north(2 * n_lev, slice(0, 1), slice(None)))
+        open_south = jnp.where(flags[2] == 1, 0.0, 1.0)
         for lev in range(n_lev):
             k = first + lev
             kf = k.astype(F32)
-            raw = ms_ref[n_lev + lev // n_pair, lev % n_pair : lev % n_pair + 1, :]
+            line = lev % n_pair
+            raw = from_south(n_lev + lev // n_pair, slice(line, line + 1), slice(None))
             fs_ref[lev] = spread(raw)
             wi0, wi3 = c_ref[WI, lev, 0:1, :], c_ref[WI, lev, 3:4, :]
             s = raw * jnp.where(kf < south_depth, 1.0, 0.0) * open_south * wi0
@@ -372,9 +385,9 @@
         to = pl.ds(g * 8, 8)
         if is_first:
             n3 = spread(nf_ref[lev, 3:4, :])
-            come = jnp.where(n3 < 0.0, mn_ref[lev, to, :], mn_ref[n_lev + lev, to, :])
+            come = jnp.where(n3 < 0.0, from_north(lev, to, slice(None)), from_north(n_lev + lev, to, slice(None)))
         else:
-            come = mn_ref[lev, to, :]
+            come = from_north(lev, to, slice(None))
         return jnp.where(is_top, mf_ref[lev, to, :], come)
 
     def row(i, number, inflow, come):
@@ -400,9 +413,9 @@
     def last(i, kind, g, v):
         edge_ref[3 * i, pl.ds((kind * halves + g) * 8, 8), :] = v
 
-    rows = [row(0, 0, ESF, lambda lev, g: ms_ref[lev, pl.ds(g * 8, 8), :]), row(1, 3, TNF, come_north)]
-    sweep(flags_ref, n_lev, n_pair, rows, put, last)
-    k0, dk = order(flags_ref, n_lev)
+    rows = [row(0, 0, ESF, lambda lev, g: from_south(lev, pl.ds(g * 8, 8), slice(None))), row(1, 3, TNF, come_north)]
+    sweep(flags, n_lev, n_pair, rows, put, last)
+    k0, dk = order(flags, n_lev)
     mid = k0 + dk * (n_lev - 1)
     edge_ref[1] = pi_ref[mid, 0]
     edge_ref[2] = pi_ref[mid, 1]
@@ -423,31 +436,36 @@
     return (lambda at, i: zero) if is_first else (lambda at, i: in_ref[at, i]), put
 
 
-def edge_back(is_first, n_lev, n_pair, flags_ref, pe_ref, far_ref, c_ref, wx_ref, nf_ref, fs_ref, *rest):
-    halves = n_pair // 8
-    acc_ref, (xe_ref, north_ref, south_ref, out_ref) = (None, rest) if is_first else (rest[0], rest[1:])
+def edge_back(is_first, n_lev, n_pair, pe_ref, far_ref, c_ref, wx_ref, nf_ref, fs_ref, *rest):
+    flags = where_am_i(n_pair)
+    halves = n_pair // 8
+    acc_ref, (xe_ref, even_ref, odd_ref, out_ref) = (None, rest) if is_first else (rest[0], rest[1:])
     acc_in, acc_out = tallies(is_first, acc_ref, out_ref, n_lev)
-    held = {}
+    held, south = {}, {}
+    up_even = flags[4] == 0
 
     def put(lev, i, kind, g, v):
         xe_ref[lev, i, pl.ds((kind * halves + g) * 8, 8), :] = v
         if kind == 0:
             held[i, g] = v
         elif i == 0:
-            south_ref[lev, pl.ds(g * 8, 8), :] = jnp.where(fs_ref[lev] < 0.0, held[i, g], v)
+            south[g] = jnp.where(fs_ref[lev] < 0.0, held[i, g], v)
         else:
             n3 = spread(nf_ref[lev, 3:4, :])
-            north_ref[lev, pl.ds(g * 8, 8), :] = jnp.where(n3 > 0.0, held[i, g], v)
+            north = jnp.where(n3 > 0.0, held[i, g], v)
+            even_ref[lev, pl.ds(g * 8, 8), :] = jnp.where(up_even, north, south[g])
+            odd_ref[lev, pl.ds(g * 8, 8), :] = jnp.where(up_even, south[g], north)
 
     back(
-        flags_ref, n_lev, n_pair, (0, 3), wx_ref, far_ref, c_ref,
+        flags, n_lev, n_pair, (0, 3), wx_ref, far_ref, c_ref,
         lambda lev, i, kind, g: rows_at(pe_ref, i, lev, kind, g, halves), put, acc_in, acc_out,
     )
 
 
 def inner(
-    is_first, n_lev, n_pair, flags_ref, pi_ref, far_ref, c_ref, ec_ref, wx_ref, nf_ref, fold_ref, hot_ref, xe_ref, *rest
+    is_first, n_lev, n_pair, pi_ref, far_ref, c_ref, ec_ref, wx_ref, nf_ref, fold_ref, hot_ref, xe_ref, *rest
 ):
+    flags = where_am_i(n_pair)
     halves = n_pair // 8
     acc_ref, (pn_ref, be_ref, mf_ref, out_ref, xi_ref) = (None, rest) if is_first else (rest[0], rest[1:])
     acc_in, acc_out = tallies(is_first, acc_ref, out_ref, n_lev)
@@ -456,49 +474,37 @@
         xi_ref[lev, i, pl.ds((kind * halves + g) * 8, 8), :] = v
 
     back(
-        flags_ref, n_lev, n_pair, (1, 2), wx_ref, far_ref, c_ref,
+        flags, n_lev, n_pair, (1, 2), wx_ref, far_ref, c_ref,
         lambda lev, i, kind, g: rows_at(pi_ref, i, lev, kind, g, halves), put, acc_in, acc_out,
     )
-    inner_sweep(n_lev, n_pair, flags_ref, xe_ref, xi_ref, c_ref, ec_ref, hot_ref, pn_ref, be_ref)
+    inner_sweep(n_lev, n_pair, flags, xe_ref, xi_ref, c_ref, ec_ref, hot_ref, pn_ref, be_ref)
     fold_rows(
-        flags_ref, fold_ref, nf_ref, lambda lev, kind, g: rows_at(xe_ref, 1, lev, kind, g, halves), mf_ref, n_lev, n_pair
+        flags, fold_ref, nf_ref, lambda lev, kind, g: rows_at(xe_ref, 1, lev, kind, g, halves), mf_ref, n_lev, n_pair
     )
 
 
 def finish(
-    n_lev, n_pair, n_rows, flags_ref, pe_ref, pi_ref, far_ref, c_ref, wx_ref, depth_ref, acce_ref, acci_ref,
-    f_hbm, a_hbm, sens_ref, te_ref, ti_ref, f_ref, a_ref, sems,
+    n_lev, n_pair, n_rows, pe_ref, pi_ref, far_ref, c_ref, wx_ref, depth_ref, acce_ref, acci_ref,
+    f_ref, a_ref, sens_ref, te_ref, ti_ref,
 ):
+    flags = where_am_i(n_pair)
     halves = n_pair // 8
     stride = n_lev * n_rows
-    bottom = lax.axis_index("level")
     ps = [(pe_ref, 0), (pi_ref, 0), (pi_ref, 1), (pe_ref, 1)]
     e_in, e_out = tallies(False, acce_ref, te_ref, n_lev)
     i_in, i_out = tallies(False, acci_ref, ti_ref, n_lev)
-    copies = []
 
     def put(lev, i, kind, g, v):
         to = f_ref if kind == 0 else a_ref
         to[pl.ds(g * 8 * stride + lev * n_rows + i, 8, stride=stride), :] = v
 
-    def done(piece):
-        low = jnp.where(bottom == 0, n_lev - (piece + 1) * PIECE, piece * PIECE)
-        at = pl.ds(pl.multiple_of(low * n_rows, PIECE * n_rows), PIECE * n_rows)
-        for kind, (ref, hbm) in enumerate(((f_ref, f_hbm), (a_ref, a_hbm))):
-            copy = pltpu.make_async_copy(
-                ref.reshape(n_pair, stride, LANES).at[:, at, :], hbm.at[:, at, :], sems.at[2 * piece + kind]
-            )
-            copy.start()
-            copies.append(copy)
-
     back(
-        flags_ref, n_lev, n_pair, range(4), wx_ref, far_ref, c_ref,
+        flags, n_lev, n_pair, range(4), wx_ref, far_ref, c_ref,
         lambda lev, i, kind, g: rows_at(ps[i][0], ps[i][1], lev, kind, g, halves), put,
         lambda at, i: e_in(at, i // 3) if i in (0, 3) else i_in(at, i - 1),
         lambda at, i, v: e_out(at, i // 3, v) if i in (0, 3) else i_out(at, i - 1, v),
-        done,
-    )
-    first = flags_ref[0] * n_lev
+    )
+    first = flags[0] * n_lev
     depth = depth_ref[...]
 
     def reduce(lev, _):
@@ -510,6 +516,17 @@
         return 0
 
     lax.fori_loop(0, n_lev, reduce, 0, unroll=UNROLL)
+
+
+def hand_out(pieces, f_ref, a_ref, f_hbm, a_hbm, sems):
+    size = f_ref.shape[0] // pieces
+    copies = [
+        pltpu.make_async_copy(ref.at[pl.ds(j * size, size), :], hbm.at[pl.ds(j * size, size), :], sems.at[2 * j + k])
+        for j in range(pieces)
+        for k, (ref, hbm) in enumerate(((f_ref, f_hbm), (a_ref, a_hbm)))
+    ]
+    for copy in copies:
+        copy.start()
     for copy in copies:
         copy.wait()
 
@@ -518,55 +535,51 @@
     return pltpu.VMEM(shape, F32)
 
 
-def call(kernel, outs, args, flops, scratch=(), first=pltpu.SMEM, hbm=0):
-    spec = pl.BlockSpec(memory_space=pltpu.VMEM)
-    far = pl.BlockSpec(memory_space=pltpu.HBM)
+def where_am_i(n_pair):
+    place, count = lax.axis_index("horiz"), lax.axis_size("horiz")
+    return (
+        lax.axis_index("level"),
+        jnp.where(place == count - 1, 1, 0),
+        jnp.where(place == 0, 1, 0),
+        lax.axis_index("tracer") * n_pair,
+        lax.rem(place, 2),
+    )
+
+
+def call(kernel, outs, args, flops, scratch=(), hbm_in=False, hbm_out=0):
+    near, far = pl.BlockSpec(memory_space=pltpu.VMEM), pl.BlockSpec(memory_space=pltpu.HBM)
     return pl.pallas_call(
         kernel,
         out_shape=tuple(outs),
-        in_specs=[pl.BlockSpec(memory_space=pltpu.SMEM)] + [spec] * (len(args) - 1)
-        if first is pltpu.SMEM
-        else [far] * len(args),
-        out_specs=tuple([far] * hbm + [spec] * (len(outs) - hbm)),
+        in_specs=[far if hbm_in else near] * len(args),
+        out_specs=tuple([far] * hbm_out + [near] * (len(outs) - hbm_out)),
         scratch_shapes=list(scratch),
         compiler_params=pltpu.CompilerParams(vmem_limit_bytes=24 * 2**20),
         cost_estimate=pl.CostEstimate(flops=flops, bytes_accessed=flops // 8, transcendentals=0),
-    )(
-        *(
-            args[:1] + [pltpu.with_memory_space_constraint(a, pltpu.VMEM) for a in args[1:]]
-            if first is pltpu.SMEM
-            else [pltpu.with_memory_space_constraint(a, pltpu.HBM) for a in args]
-        )
-    )
+    )(*[pltpu.with_memory_space_constraint(a, pltpu.HBM if hbm_in else pltpu.VMEM) for a in args])
 
 
 def per_device(forward_init, adjoint_init, east_flow, north_flow, mixing, depth, color, fold):
     n_pair, n_lev, n_rows, n_x = forward_init.shape
     n_all = 2 * n_pair
     count = lax.axis_size("horiz")
-    place = lax.axis_index("horiz")
-    flags = jnp.stack(
-        [
-            lax.axis_index("level"),
-            (place == count - 1).astype(jnp.int32),
-            (place == 0).astype(jnp.int32),
-            lax.axis_index("tracer") * n_pair,
-        ]
-    ).astype(jnp.int32)
-    northward = [(i, (i + 1) % count) for i in range(count)]
-    southward = [((i + 1) % count, i) for i in range(count)]
+    even = [(2 * i + t, 2 * (i ^ 1) + t) for i in range(count) for t in range(2)]
+    odd = []
+    for i in range(count):
+        partner = ((i - 1) ^ 1) + 1 if i > 0 else count
+        odd += [(2 * i + t, 2 * partner + t if partner < count else 2 * i + 1 - t) for t in range(2)]
+    pairs = ("horiz", "tracer")
     swap = [(0, 1), (1, 0)]
     f2 = forward_init.reshape(n_pair * n_lev * n_rows, n_x)
     a2 = adjoint_init.reshape(n_pair * n_lev * n_rows, n_x)
     fold2 = fold.reshape(1, n_x)
     work = n_lev * n_rows * n_all * n_x
-    pages = n_lev // n_pair
 
     flat = vmem(n_pair * n_lev * n_rows, n_x)
-    to_north, to_south, f2, a2, north_flow, depth = call(
+    to_even, to_odd, f2, a2, north_flow, depth = call(
         functools.partial(send_first, n_lev, n_pair, n_rows),
         [
-            vmem(n_lev + pages + 1, n_pair, n_x),
+            vmem(2 * n_lev + 1, n_pair, n_x),
             vmem(2 * n_lev + 1, n_pair, n_x),
             flat,
             flat,
@@ -576,17 +589,17 @@
         [f2, a2, north_flow, depth],
         work,
         [pltpu.SemaphoreType.DMA((2 + n_pair // 2,))],
-        first=pltpu.HBM,
-    )
-    from_north = lax.ppermute(to_south, "horiz", southward)
-    from_south = lax.ppermute(to_north, "horiz", northward)
+        hbm_in=True,
+    )
+    from_odd = lax.ppermute(to_odd, pairs, odd)
+    from_even = lax.ppermute(to_even, pairs, even)
     state = vmem(n_lev, 2, n_all, n_x)
     halo = vmem(n_lev, n_pair, n_x)
     acc = vmem(n_lev + 1, 2, 8, n_x)
     xe, pi, be, c, wx, hot, mf = call(
         functools.partial(prepare, n_lev, n_pair, n_rows),
         [state] * 3 + [vmem(13, n_lev, n_rows, n_x), vmem(3, n_rows, n_x), vmem(n_rows, n_pair, n_x), halo],
-        [flags, f2, a2, east_flow, north_flow, mixing, depth, color, fold2],
+        [f2, a2, east_flow, north_flow, mixing, depth, color, fold2],
         work * 10,
         [vmem(n_lev, n_rows, n_x), state],
     )
@@ -597,44 +610,51 @@
             pe, edge, ec, fs = call(
                 functools.partial(edge_sweep, True, n_lev, n_pair),
                 [state, edges, vmem(8, n_lev, 8, n_x), vmem(n_lev, 8, n_x)],
-                [flags, be, pi, c, mf, from_south, from_north, xe, north_flow, depth, fold2],
+                [be, pi, c, mf, from_even, from_odd, xe, north_flow, depth, fold2],
                 work * 3,
             )
         else:
             pe, edge = call(
                 functools.partial(edge_sweep, False, n_lev, n_pair),
                 [state, edges],
-                [flags, be, pi, c, mf, from_south, from_north, ec],
+                [be, pi, c, mf, from_even, from_odd, ec],
                 work * 2,
             )
         far = lax.ppermute(edge, "level", swap)
         if step == STEPS - 1:
             break
         more = [] if step == 0 else [acce]
-        xe, to_north, to_south, acce = call(
+        xe, to_even, to_odd, acce = call(
             functools.partial(edge_back, step == 0, n_lev, n_pair),
             [state, halo, halo, acc],
-            [flags, pe, far, c, wx, north_flow, fs] + more,
+            [pe, far, c, wx, north_flow, fs] + more,
             work * 2,
         )
-        from_south = lax.ppermute(to_north, "horiz", northward)
-        from_north = lax.ppermute(to_south, "horiz", southward)
+        from_odd = lax.ppermute(to_odd, pairs, odd)
+        from_even = lax.ppermute(to_even, pairs, even)
         more = [] if step == 0 else [acci]
         pi, be, mf, acci = call(
             functools.partial(inner, step == 0, n_lev, n_pair),
             [state, state, halo, acc],
-            [flags, pi, far, c, ec, wx, north_flow, fold2, hot, xe] + more,
+            [pi, far, c, ec, wx, north_flow, fold2, hot, xe] + more,
             work * 9,
             [state],
         )
-    out = jax.ShapeDtypeStruct((n_pair, n_lev * n_rows, n_x), F32)
-    f_out, a_out, sens = call(
+    f_flat, a_flat, sens = call(
         functools.partial(finish, n_lev, n_pair, n_rows),
-        [out, out, vmem(n_lev, n_rows, n_x)],
-        [flags, pe, pi, far, c, wx, depth, acce, acci],
+        [flat, flat, vmem(n_lev, n_rows, n_x)],
+        [pe, pi, far, c, wx, depth, acce, acci],
         work * 4,
-        [acc, acc, flat, flat, pltpu.SemaphoreType.DMA((2 * n_lev // PIECE,))],
-        hbm=2,
+        [acc, acc],
+    )
+    out = jax.ShapeDtypeStruct(f_flat.shape, F32)
+    f_out, a_out = call(
+        functools.partial(hand_out, PIECES),
+        [out, out],
+        [f_flat, a_flat],
+        work * 4,
+        [pltpu.SemaphoreType.DMA((2 * PIECES,))],
+        hbm_out=2,
     )
     sens = sens + lax.ppermute(sens, "tracer", swap)
     return f_out.reshape(forward_init.shape), a_out.reshape(adjoint_init.shape), sens

time: 93.7 us -> 87.3 us (0.932)
  waiting for transfers between devices: 24.3 us -> 32.7 us
  starting transfers between devices: 42.1 us -> 34.6 us
  Pallas kernels: 23.4 us -> 16.9 us
    ppermute x8, waiting for transfers between devices: 11.7 us -> 19.4 us  [the longest x4 16.6 us: per_device(): from_odd = lax.ppermute(to_odd, pairs, odd)]
    pallas_call x13 -> x14, Pallas kernels: 23.4 us -> 16.9 us  [call(): pl.pallas_call(kernel, out_shape=tuple(outs), in_specs=[far if hbm_in els...]
    ppermute x8, starting transfers between devices: 23.7 us -> 19.1 us  [the longest x4 17.2 us: per_device(): from_odd = lax.ppermute(to_odd, pairs, odd)]
    ppermute x1, starting transfers between devices: 10.3 us -> 8.65 us  [per_device(): sens = sens + lax.ppermute(sens, 'tracer', swap)]
    ppermute x4, waiting for transfers between devices: 11.7 us -> 13.2 us  [per_device(): far = lax.ppermute(edge, 'level', swap)]
    ppermute x4, starting transfers between devices: 8.11 us -> 6.86 us  [per_device(): far = lax.ppermute(edge, 'level', swap)]
  transfers between devices with their start and end apart: 13 -> 13, of which waited for: 9 -> 10; matrix products, arithmetic and copies ran while one was open for 0% -> 0% of each run, Pallas kernels for 12% -> 12%
where the time goes in v3:
time: 87.3 us; the launch traced here: 86.4 us
  starting transfers between devices  34.6 us (40%)
  waiting for transfers between devices  32.7 us (37%)
  Pallas kernels  16.9 us (19%)
    ppermute x4, starting transfers between devices, per_device(): from_odd = lax.ppermute(to_odd, pairs, odd)  17.2 us
    pallas_call x14, Pallas kernels, call(): pl.pallas_call(kernel, out_shape=tuple(outs), in_specs=[far if hbm_in els...  16.9 us
    ppermute x4, waiting for transfers between devices, per_device(): from_odd = lax.ppermute(to_odd, pairs, odd)  16.6 us
    ppermute x4, waiting for transfers between devices, per_device(): far = lax.ppermute(edge, 'level', swap)  13.2 us
    ppermute x1, starting transfers between devices, per_device(): sens = sens + lax.ppermute(sens, 'tracer', swap)  8.65 us
    ppermute x4, starting transfers between devices, per_device(): far = lax.ppermute(edge, 'level', swap)  6.86 us
    ppermute x4, waiting for transfers between devices, per_device(): from_even = lax.ppermute(to_even, pairs, even)  2.79 us
    ppermute x4, starting transfers between devices, per_device(): from_even = lax.ppermute(to_even, pairs, even)  1.97 us
  transfers between devices with their start and end apart: 13, of which 10 were waited for; matrix products, arithmetic and copies ran while one was open for 0% of the time, Pallas kernels for 12%

profile of v3, /device:TPU:3, one launch (start us, length us, event | category | flops | bytes accessed | tf_op | source)
XLA Modules:
  0.0 86.4 jit_solution(14009799452860390742)
XLA Ops:
  0.7 2.1 %shard_map.103 = (f32[65,16,128]{2,1,0:T(8,128)S(1)}, f32[65,16,128]{2,1,0:T(8,128)S(1)}, f32[2048,128]{1,0:T(8,128)S(1)}, f32[2048,128]{1,0:T(8,128)S(1)}, f32[...) custom-call(f32[2048,128]{1,0:T(8,128)} %bitcast.10, f32[2048,128]{1,0:T(8,128)} %bitcast.11, f32[32,4,128]{2,1,0:T(4,128)} %nf_hbm.1, ...), custom_call_target="tpu_custom_call" | custom-call | flops 524288 | bytes 65536 | tf_op jit(solution)/shard_map/pallas_call | solution.py:551
  2.7 1.7 %collective-permute-start = (f32[65,16,128]{2,1,0:T(8,128)S(1)}, f32[65,16,128]{2,1,0:T(8,128)S(1)}, u32[]{:S(2)}, u32[]{:S(2)}) collective-permute-start(f32[65,16,128]{2,1,0:T(8,128)S(1)} %get-tuple-element.63), channel_id=1, source_target_pairs={{0,4},{2,6},{4,0},{6,2},{8,12},{10,14},{12,8},{14,10},{16,20},{18,... | collective-permute-start | bytes 1597448 | tf_op jit(solution)/shard_map/ppermute | solution.py:595
  4.4 4.7 %collective-permute-start.1 = (f32[65,16,128]{2,1,0:T(8,128)S(1)}, f32[65,16,128]{2,1,0:T(8,128)S(1)}, u32[]{:S(2)}, u32[]{:S(2)}) collective-permute-start(f32[65,16,128]{2,1,0:T(8,128)S(1)} %get-tuple-element.64), channel_id=1, source_target_pairs={{0,2},{2,0},{4,8},{6,10},{8,4},{10,6},{12,16},{14,18},{16,12},{18,... | collective-permute-start | bytes 1597448 | tf_op jit(solution)/shard_map/ppermute | solution.py:594
  9.8 3.7 %shard_map.104 = (f32[32,2,32,128]{3,2,1,0:T(8,128)S(1)}, f32[32,2,32,128]{3,2,1,0:T(8,128)S(1)}, f32[32,2,32,128]{3,2,1,0:T(8,128)S(1)}, f32[13,32,4,128]{3,2,1...) custom-call(f32[2048,128]{1,0:T(8,128)S(1)} %get-tuple-element.55.f_ref, ...), custom_call_target="tpu_custom_call" | custom-call | flops 5242880 | bytes 655360 | tf_op jit(solution)/shard_map/pallas_call | solution.py:551
  13.5 2.6 %collective-permute-done.even_ref = f32[65,16,128]{2,1,0:T(8,128)S(1)} collective-permute-done((f32[65,16,128]{2,1,0:T(8,128)S(1)}, f32[65,16,128]{2,1,0:T(8,128)S(1)}, u32[]{:S(2)}, u32[]{:S(2)}) %collective-permute-start) | collective-permute-done | bytes 532512 | tf_op jit(solution)/shard_map/ppermute | solution.py:595
  16.1 5.2 %collective-permute-done.1.odd_ref = f32[65,16,128]{2,1,0:T(8,128)S(1)} collective-permute-done((f32[65,16,128]{2,1,0:T(8,128)S(1)}, f32[65,16,128]{2,1,0:T(8,128)S(1)}, u32[]{:S(2)}, u32[]{:S(2)}) %collective-permute-start.1) | collective-permute-done | bytes 532512 | tf_op jit(solution)/shard_map/ppermute | solution.py:594
  22.0 2.0 %collective-permute-start.2 = (f32[4,32,128]{2,1,0:T(8,128)S(1)}, f32[4,32,128]{2,1,0:T(8,128)S(1)}, u32[]{:S(2)}, u32[]{:S(2)}) collective-permute-start(f32[4,32,128]{2,1,0:T(8,128)S(1)} %get-tuple-element.66), channel_id=1, source_target_pairs={{0,1},{1,0},{2,3},{3,2},{4,5},{5,4},{6,7},{7,6},{8,9},{9,8},{10,11... | collective-permute-start | bytes 196616 | tf_op jit(solution)/shard_map/ppermute | solution.py:623
  23.9 2.7 %collective-permute-done.2.far_ref = f32[4,32,128]{2,1,0:T(8,128)S(1)} collective-permute-done((f32[4,32,128]{2,1,0:T(8,128)S(1)}, f32[4,32,128]{2,1,0:T(8,128)S(1)}, u32[]{:S(2)}, u32[]{:S(2)}) %collective-permute-start.2) | collective-permute-done | bytes 65568 | tf_op jit(solution)/shard_map/ppermute | solution.py:623
  27.1 4.7 %collective-permute-start.4 = (f32[32,16,128]{2,1,0:T(8,128)S(1)}, f32[32,16,128]{2,1,0:T(8,128)S(1)}, u32[]{:S(2)}, u32[]{:S(2)}) collective-permute-start(f32[32,16,128]{2,1,0:T(8,128)S(1)} %get-tuple-element.77), channel_id=1, source_target_pairs={{0,2},{2,0},{4,8},{6,10},{8,4},{10,6},{12,16},{14,18},{16,12},{18,... | collective-permute-start | bytes 786440 | tf_op jit(solution)/shard_map/ppermute | solution.py:633
  31.8 1.7 %shard_map.107 = (f32[32,2,32,128]{3,2,1,0:T(8,128)S(1)}, f32[32,2,32,128]{3,2,1,0:T(8,128)S(1)}, f32[32,16,128]{2,1,0:T(8,128)S(1)}, f32[33,2,8,128]{3,2,1,0:T(8,128)S(1)}) custom-call(f32[32,2,32,128]{3,2,1,0:T(8,128)S(1)} %get-tuple-element.59.pi_ref, f32[4,32,128]{2,1,0:T(8,128)S(1)} %collective-permute-done.2.far_ref, ...), custom_call_target="tpu_custom_call" | custom-call | flops 4718592 | bytes 589824 | tf_op jit(solution)/shard_map/pallas_call | solution.py:551
  33.5 3.1 %collective-permute-done.4.odd_ref = f32[32,16,128]{2,1,0:T(8,128)S(1)} collective-permute-done((f32[32,16,128]{2,1,0:T(8,128)S(1)}, f32[32,16,128]{2,1,0:T(8,128)S(1)}, u32[]{:S(2)}, u32[]{:S(2)}) %collective-permute-start.4) | collective-permute-done | bytes 262176 | tf_op jit(solution)/shard_map/ppermute | solution.py:633
  36.9 2.0 %collective-permute-start.5 = (f32[4,32,128]{2,1,0:T(8,128)S(1)}, f32[4,32,128]{2,1,0:T(8,128)S(1)}, u32[]{:S(2)}, u32[]{:S(2)}) collective-permute-start(f32[4,32,128]{2,1,0:T(8,128)S(1)} %get-tuple-element.78), channel_id=1, source_target_pairs={{0,1},{1,0},{2,3},{3,2},{4,5},{5,4},{6,7},{7,6},{8,9},{9,8},{10,11... | collective-permute-start | bytes 196616 | tf_op jit(solution)/shard_map/ppermute | solution.py:623
  38.9 3.1 %collective-permute-done.5.far_ref = f32[4,32,128]{2,1,0:T(8,128)S(1)} collective-permute-done((f32[4,32,128]{2,1,0:T(8,128)S(1)}, f32[4,32,128]{2,1,0:T(8,128)S(1)}, u32[]{:S(2)}, u32[]{:S(2)}) %collective-permute-start.5) | collective-permute-done | bytes 65568 | tf_op jit(solution)/shard_map/ppermute | solution.py:623
  42.3 4.4 %collective-permute-start.7 = (f32[32,16,128]{2,1,0:T(8,128)S(1)}, f32[32,16,128]{2,1,0:T(8,128)S(1)}, u32[]{:S(2)}, u32[]{:S(2)}) collective-permute-start(f32[32,16,128]{2,1,0:T(8,128)S(1)} %get-tuple-element.87), channel_id=1, source_target_pairs={{0,2},{2,0},{4,8},{6,10},{8,4},{10,6},{12,16},{14,18},{16,12},{18,... | collective-permute-start | bytes 786440 | tf_op jit(solution)/shard_map/ppermute | solution.py:633
  46.7 1.7 %shard_map.110 = (f32[32,2,32,128]{3,2,1,0:T(8,128)S(1)}, f32[32,2,32,128]{3,2,1,0:T(8,128)S(1)}, f32[32,16,128]{2,1,0:T(8,128)S(1)}, f32[33,2,8,128]{3,2,1,0:T(8,128)S(1)}) custom-call(f32[32,2,32,128]{3,2,1,0:T(8,128)S(1)} %get-tuple-element.73.pi_ref, f32[4,32,128]{2,1,0:T(8,128)S(1)} %collective-permute-done.5.far_ref, ...), custom_call_target="tpu_custom_call" | custom-call | flops 4718592 | bytes 589824 | tf_op jit(solution)/shard_map/pallas_call | solution.py:551
  48.5 4.1 %collective-permute-done.7.odd_ref = f32[32,16,128]{2,1,0:T(8,128)S(1)} collective-permute-done((f32[32,16,128]{2,1,0:T(8,128)S(1)}, f32[32,16,128]{2,1,0:T(8,128)S(1)}, u32[]{:S(2)}, u32[]{:S(2)}) %collective-permute-start.7) | collective-permute-done | bytes 262176 | tf_op jit(solution)/shard_map/ppermute | solution.py:633
  53.8 4.4 %collective-permute-done.8.far_ref = f32[4,32,128]{2,1,0:T(8,128)S(1)} collective-permute-done((f32[4,32,128]{2,1,0:T(8,128)S(1)}, f32[4,32,128]{2,1,0:T(8,128)S(1)}, u32[]{:S(2)}, u32[]{:S(2)}) %collective-permute-start.8) | collective-permute-done | bytes 65568 | tf_op jit(solution)/shard_map/ppermute | solution.py:623
  58.6 3.3 %collective-permute-start.10 = (f32[32,16,128]{2,1,0:T(8,128)S(1)}, f32[32,16,128]{2,1,0:T(8,128)S(1)}, u32[]{:S(2)}, u32[]{:S(2)}) collective-permute-start(f32[32,16,128]{2,1,0:T(8,128)S(1)} %get-tuple-element.97), channel_id=1, source_target_pairs={{0,2},{2,0},{4,8},{6,10},{8,4},{10,6},{12,16},{14,18},{16,12},{18,... | collective-permute-start | bytes 786440 | tf_op jit(solution)/shard_map/ppermute | solution.py:633
  62.0 1.7 %shard_map.113 = (f32[32,2,32,128]{3,2,1,0:T(8,128)S(1)}, f32[32,2,32,128]{3,2,1,0:T(8,128)S(1)}, f32[32,16,128]{2,1,0:T(8,128)S(1)}, f32[33,2,8,128]{3,2,1,0:T(8,128)S(1)}) custom-call(f32[32,2,32,128]{3,2,1,0:T(8,128)S(1)} %get-tuple-element.83.pi_ref, f32[4,32,128]{2,1,0:T(8,128)S(1)} %collective-permute-done.8.far_ref, ...), custom_call_target="tpu_custom_call" | custom-call | flops 4718592 | bytes 589824 | tf_op jit(solution)/shard_map/pallas_call | solution.py:551
  63.8 4.3 %collective-permute-done.10.odd_ref = f32[32,16,128]{2,1,0:T(8,128)S(1)} collective-permute-done((f32[32,16,128]{2,1,0:T(8,128)S(1)}, f32[32,16,128]{2,1,0:T(8,128)S(1)}, u32[]{:S(2)}, u32[]{:S(2)}) %collective-permute-start.10) | collective-permute-done | bytes 262176 | tf_op jit(solution)/shard_map/ppermute | solution.py:633
  68.5 2.0 %collective-permute-start.11 = (f32[4,32,128]{2,1,0:T(8,128)S(1)}, f32[4,32,128]{2,1,0:T(8,128)S(1)}, u32[]{:S(2)}, u32[]{:S(2)}) collective-permute-start(f32[4,32,128]{2,1,0:T(8,128)S(1)} %get-tuple-element.99), channel_id=1, source_target_pairs={{0,1},{1,0},{2,3},{3,2},{4,5},{5,4},{6,7},{7,6},{8,9},{9,8},{10,11... | collective-permute-start | bytes 196616 | tf_op jit(solution)/shard_map/ppermute | solution.py:623
  70.5 3.0 %collective-permute-done.11.far_ref = f32[4,32,128]{2,1,0:T(8,128)S(1)} collective-permute-done((f32[4,32,128]{2,1,0:T(8,128)S(1)}, f32[4,32,128]{2,1,0:T(8,128)S(1)}, u32[]{:S(2)}, u32[]{:S(2)}) %collective-permute-start.11) | collective-permute-done | bytes 65568 | tf_op jit(solution)/shard_map/ppermute | solution.py:623
  73.5 2.2 %shard_map.115 = (f32[2048,128]{1,0:T(8,128)S(1)}, f32[2048,128]{1,0:T(8,128)S(1)}, f32[32,4,128]{2,1,0:T(4,128)S(1)}) custom-call(f32[32,2,32,128]{3,2,1,0:T(8,128)S(1)} %get-tuple-element.98.pe_ref, f32[32,2,32,128]{3,2,1,0:T(8,128)S(1)} %get-tuple-element.94.pi_ref, f32[4,32,128]{2,1,0:T(8,128)S(1)} %collective-permute-done.11.far_ref, ...), custom_call_target="tpu_custom_call" | custom-call | flops 2097152 | bytes 262144 | tf_op jit(solution)/shard_map/pallas_call | solution.py:551
  75.7 8.7 %collective-permute-start.12 = (f32[32,4,128]{2,1,0:T(4,128)S(1)}, f32[32,4,128]{2,1,0:T(4,128)S(1)}, u32[]{:S(2)}, u32[]{:S(2)}) collective-permute-start(f32[32,4,128]{2,1,0:T(4,128)S(1)} %get-tuple-element.106), channel_id=1, source_target_pairs={{0,2},{2,0},{1,3},{3,1},{4,6},{6,4},{5,7},{7,5},{8,10},{10,8},{9,1... | collective-permute-start | bytes 196616 | tf_op jit(solution)/shard_map/ppermute | solution.py:659
  (25 shorter events, 6.5 us)
Async XLA Ops:
  0.6 8.5 %copy-start = (f32[63,4,128]{2,1,0:T(4,128)S(1)}, f32[63,4,128]{2,1,0:T(4,128)}, u32[]{:S(2)}) copy-start(f32[63,4,128]{2,1,0:T(4,128)} %mix_ref.1) | copy-start | bytes 387076
  0.6 8.5 %copy-start.1 = (f32[32,4,128]{2,1,0:T(4,128)S(1)}, f32[32,4,128]{2,1,0:T(4,128)}, u32[]{:S(2)}) copy-start(f32[32,4,128]{2,1,0:T(4,128)} %ef_ref.1) | copy-start | bytes 196612
  2.7 13.4 %collective-permute-start = (f32[65,16,128]{2,1,0:T(8,128)S(1)}, f32[65,16,128]{2,1,0:T(8,128)S(1)}, u32[]{:S(2)}, u32[]{:S(2)}) collective-permute-start(f32[65,16,128]{2,1,0:T(8,128)S(1)} %get-tuple-element.63), channel_id=1, source_target_pairs={{0,4},{2,6},{4,0},{6,2},{8,12},{10,14},{12,8},{14,10},{16,20},{18,... | collective-permute-start | bytes 1597448 | tf_op jit(solution)/shard_map/ppermute | solution.py:595
  4.4 16.9 %collective-permute-start.1 = (f32[65,16,128]{2,1,0:T(8,128)S(1)}, f32[65,16,128]{2,1,0:T(8,128)S(1)}, u32[]{:S(2)}, u32[]{:S(2)}) collective-permute-start(f32[65,16,128]{2,1,0:T(8,128)S(1)} %get-tuple-element.64), channel_id=1, source_target_pairs={{0,2},{2,0},{4,8},{6,10},{8,4},{10,6},{12,16},{14,18},{16,12},{18,... | collective-permute-start | bytes 1597448 | tf_op jit(solution)/shard_map/ppermute | solution.py:594
  9.1 0.7 copy-start.3
  9.1 0.7 copy-start.2
  22.0 4.7 %collective-permute-start.2 = (f32[4,32,128]{2,1,0:T(8,128)S(1)}, f32[4,32,128]{2,1,0:T(8,128)S(1)}, u32[]{:S(2)}, u32[]{:S(2)}) collective-permute-start(f32[4,32,128]{2,1,0:T(8,128)S(1)} %get-tuple-element.66), channel_id=1, source_target_pairs={{0,1},{1,0},{2,3},{3,2},{4,5},{5,4},{6,7},{7,6},{8,9},{9,8},{10,11... | collective-permute-start | bytes 196616 | tf_op jit(solution)/shard_map/ppermute | solution.py:623
  27.0 6.5 %collective-permute-start.3 = (f32[32,16,128]{2,1,0:T(8,128)S(1)}, f32[32,16,128]{2,1,0:T(8,128)S(1)}, u32[]{:S(2)}, u32[]{:S(2)}) collective-permute-start(f32[32,16,128]{2,1,0:T(8,128)S(1)} %get-tuple-element.76), channel_id=1, source_target_pairs={{0,4},{2,6},{4,0},{6,2},{8,12},{10,14},{12,8},{14,10},{16,20},{18,... | collective-permute-start | bytes 786440 | tf_op jit(solution)/shard_map/ppermute | solution.py:634
  27.1 9.5 %collective-permute-start.4 = (f32[32,16,128]{2,1,0:T(8,128)S(1)}, f32[32,16,128]{2,1,0:T(8,128)S(1)}, u32[]{:S(2)}, u32[]{:S(2)}) collective-permute-start(f32[32,16,128]{2,1,0:T(8,128)S(1)} %get-tuple-element.77), channel_id=1, source_target_pairs={{0,2},{2,0},{4,8},{6,10},{8,4},{10,6},{12,16},{14,18},{16,12},{18,... | collective-permute-start | bytes 786440 | tf_op jit(solution)/shard_map/ppermute | solution.py:633
  36.9 5.0 %collective-permute-start.5 = (f32[4,32,128]{2,1,0:T(8,128)S(1)}, f32[4,32,128]{2,1,0:T(8,128)S(1)}, u32[]{:S(2)}, u32[]{:S(2)}) collective-permute-start(f32[4,32,128]{2,1,0:T(8,128)S(1)} %get-tuple-element.78), channel_id=1, source_target_pairs={{0,1},{1,0},{2,3},{3,2},{4,5},{5,4},{6,7},{7,6},{8,9},{9,8},{10,11... | collective-permute-start | bytes 196616 | tf_op jit(solution)/shard_map/ppermute | solution.py:623
  42.2 6.2 %collective-permute-start.6 = (f32[32,16,128]{2,1,0:T(8,128)S(1)}, f32[32,16,128]{2,1,0:T(8,128)S(1)}, u32[]{:S(2)}, u32[]{:S(2)}) collective-permute-start(f32[32,16,128]{2,1,0:T(8,128)S(1)} %get-tuple-element.86), channel_id=1, source_target_pairs={{0,4},{2,6},{4,0},{6,2},{8,12},{10,14},{12,8},{14,10},{16,20},{18,... | collective-permute-start | bytes 786440 | tf_op jit(solution)/shard_map/ppermute | solution.py:634
  42.3 10.2 %collective-permute-start.7 = (f32[32,16,128]{2,1,0:T(8,128)S(1)}, f32[32,16,128]{2,1,0:T(8,128)S(1)}, u32[]{:S(2)}, u32[]{:S(2)}) collective-permute-start(f32[32,16,128]{2,1,0:T(8,128)S(1)} %get-tuple-element.87), channel_id=1, source_target_pairs={{0,2},{2,0},{4,8},{6,10},{8,4},{10,6},{12,16},{14,18},{16,12},{18,... | collective-permute-start | bytes 786440 | tf_op jit(solution)/shard_map/ppermute | solution.py:633
  52.8 5.4 %collective-permute-start.8 = (f32[4,32,128]{2,1,0:T(8,128)S(1)}, f32[4,32,128]{2,1,0:T(8,128)S(1)}, u32[]{:S(2)}, u32[]{:S(2)}) collective-permute-start(f32[4,32,128]{2,1,0:T(8,128)S(1)} %get-tuple-element.88), channel_id=1, source_target_pairs={{0,1},{1,0},{2,3},{3,2},{4,5},{5,4},{6,7},{7,6},{8,9},{9,8},{10,11... | collective-permute-start | bytes 196616 | tf_op jit(solution)/shard_map/ppermute | solution.py:623
  58.5 5.3 %collective-permute-start.9 = (f32[32,16,128]{2,1,0:T(8,128)S(1)}, f32[32,16,128]{2,1,0:T(8,128)S(1)}, u32[]{:S(2)}, u32[]{:S(2)}) collective-permute-start(f32[32,16,128]{2,1,0:T(8,128)S(1)} %get-tuple-element.96), channel_id=1, source_target_pairs={{0,4},{2,6},{4,0},{6,2},{8,12},{10,14},{12,8},{14,10},{16,20},{18,... | collective-permute-start | bytes 786440 | tf_op jit(solution)/shard_map/ppermute | solution.py:634
  58.6 9.5 %collective-permute-start.10 = (f32[32,16,128]{2,1,0:T(8,128)S(1)}, f32[32,16,128]{2,1,0:T(8,128)S(1)}, u32[]{:S(2)}, u32[]{:S(2)}) collective-permute-start(f32[32,16,128]{2,1,0:T(8,128)S(1)} %get-tuple-element.97), channel_id=1, source_target_pairs={{0,2},{2,0},{4,8},{6,10},{8,4},{10,6},{12,16},{14,18},{16,12},{18,... | collective-permute-start | bytes 786440 | tf_op jit(solution)/shard_map/ppermute | solution.py:633
  68.5 5.0 %collective-permute-start.11 = (f32[4,32,128]{2,1,0:T(8,128)S(1)}, f32[4,32,128]{2,1,0:T(8,128)S(1)}, u32[]{:S(2)}, u32[]{:S(2)}) collective-permute-start(f32[4,32,128]{2,1,0:T(8,128)S(1)} %get-tuple-element.99), channel_id=1, source_target_pairs={{0,1},{1,0},{2,3},{3,2},{4,5},{5,4},{6,7},{7,6},{8,9},{9,8},{10,11... | collective-permute-start | bytes 196616 | tf_op jit(solution)/shard_map/ppermute | solution.py:623
  75.7 10.0 %collective-permute-start.12 = (f32[32,4,128]{2,1,0:T(4,128)S(1)}, f32[32,4,128]{2,1,0:T(4,128)S(1)}, u32[]{:S(2)}, u32[]{:S(2)}) collective-permute-start(f32[32,4,128]{2,1,0:T(4,128)S(1)} %get-tuple-element.106), channel_id=1, source_target_pairs={{0,2},{2,0},{1,3},{3,1},{4,6},{6,4},{5,7},{7,5},{8,10},{10,8},{9,1... | collective-permute-start | bytes 196616 | tf_op jit(solution)/shard_map/ppermute | solution.py:659

commit v4 on v3

--- a/solution.py
+++ b/solution.py
@@ -12,7 +12,6 @@
 E0F, E0A, ESF, ESA, T0F, T0A, TNF, TNA = range(8)
 F32 = jnp.float32
 UNROLL = 8
-PIECES = 4
 
 
 def order(flags, n_lev):
@@ -485,18 +484,16 @@
 
 def finish(
     n_lev, n_pair, n_rows, pe_ref, pi_ref, far_ref, c_ref, wx_ref, depth_ref, acce_ref, acci_ref,
-    f_ref, a_ref, sens_ref, te_ref, ti_ref,
+    x_ref, sens_ref, te_ref, ti_ref,
 ):
     flags = where_am_i(n_pair)
     halves = n_pair // 8
-    stride = n_lev * n_rows
     ps = [(pe_ref, 0), (pi_ref, 0), (pi_ref, 1), (pe_ref, 1)]
     e_in, e_out = tallies(False, acce_ref, te_ref, n_lev)
     i_in, i_out = tallies(False, acci_ref, ti_ref, n_lev)
 
     def put(lev, i, kind, g, v):
-        to = f_ref if kind == 0 else a_ref
-        to[pl.ds(g * 8 * stride + lev * n_rows + i, 8, stride=stride), :] = v
+        x_ref[lev * n_rows + i, pl.ds((kind * halves + g) * 8, 8), :] = v
 
     back(
         flags, n_lev, n_pair, range(4), wx_ref, far_ref, c_ref,
@@ -518,12 +515,11 @@
     lax.fori_loop(0, n_lev, reduce, 0, unroll=UNROLL)
 
 
-def hand_out(pieces, f_ref, a_ref, f_hbm, a_hbm, sems):
-    size = f_ref.shape[0] // pieces
+def hand_out(n_pair, x_ref, f_hbm, a_hbm, sems):
     copies = [
-        pltpu.make_async_copy(ref.at[pl.ds(j * size, size), :], hbm.at[pl.ds(j * size, size), :], sems.at[2 * j + k])
-        for j in range(pieces)
-        for k, (ref, hbm) in enumerate(((f_ref, f_hbm), (a_ref, a_hbm)))
+        pltpu.make_async_copy(x_ref.at[:, kind * n_pair + j, :], hbm.at[j], sems.at[kind * n_pair + j])
+        for j in range(n_pair)
+        for kind, hbm in enumerate((f_hbm, a_hbm))
     ]
     for copy in copies:
         copy.start()
@@ -640,20 +636,20 @@
             work * 9,
             [state],
         )
-    f_flat, a_flat, sens = call(
+    x, sens = call(
         functools.partial(finish, n_lev, n_pair, n_rows),
-        [flat, flat, vmem(n_lev, n_rows, n_x)],
+        [vmem(n_lev * n_rows, n_all, n_x), vmem(n_lev, n_rows, n_x)],
         [pe, pi, far, c, wx, depth, acce, acci],
         work * 4,
         [acc, acc],
     )
-    out = jax.ShapeDtypeStruct(f_flat.shape, F32)
+    out = jax.ShapeDtypeStruct((n_pair, n_lev * n_rows, n_x), F32)
     f_out, a_out = call(
-        functools.partial(hand_out, PIECES),
+        functools.partial(hand_out, n_pair),
         [out, out],
-        [f_flat, a_flat],
+        [x],
         work * 4,
-        [pltpu.SemaphoreType.DMA((2 * PIECES,))],
+        [pltpu.SemaphoreType.DMA((n_all,))],
         hbm_out=2,
     )
     sens = sens + lax.ppermute(sens, "tracer", swap)

time: 87.3 us -> 85.8 us (0.983)
  Pallas kernels: 16.9 us -> 15.5 us
    pallas_call x14, Pallas kernels: 16.9 us -> 15.5 us  [call(): pl.pallas_call(kernel, out_shape=tuple(outs), in_specs=[far if hbm_in els...]
where the time goes in v4:
time: 85.8 us; the launch traced here: 85 us
  starting transfers between devices  34.6 us (40%)
  waiting for transfers between devices  33.3 us (39%)
  Pallas kernels  15.5 us (18%)
    ppermute x4, starting transfers between devices, per_device(): from_odd = lax.ppermute(to_odd, pairs, odd)  17.2 us
    ppermute x4, waiting for transfers between devices, per_device(): from_odd = lax.ppermute(to_odd, pairs, odd)  16.6 us
    pallas_call x14, Pallas kernels, call(): pl.pallas_call(kernel, out_shape=tuple(outs), in_specs=[far if hbm_in els...  15.5 us
    ppermute x4, waiting for transfers between devices, per_device(): far = lax.ppermute(edge, 'level', swap)  13.3 us
    ppermute x1, starting transfers between devices, per_device(): sens = sens + lax.ppermute(sens, 'tracer', swap)  8.65 us
    ppermute x4, starting transfers between devices, per_device(): far = lax.ppermute(edge, 'level', swap)  6.85 us
    ppermute x4, waiting for transfers between devices, per_device(): from_even = lax.ppermute(to_even, pairs, even)  3.44 us
    ppermute x4, starting transfers between devices, per_device(): from_even = lax.ppermute(to_even, pairs, even)  1.97 us
  transfers between devices with their start and end apart: 13, of which 10 were waited for; matrix products, arithmetic and copies ran while one was open for 0% of the time, Pallas kernels for 12%

profile of v4, /device:TPU:3, one launch (start us, length us, event | category | flops | bytes accessed | tf_op | source)
XLA Modules:
  0.0 85.0 jit_solution(3704111238075934)
XLA Ops:
  0.7 2.1 %shard_map.103 = (f32[65,16,128]{2,1,0:T(8,128)S(1)}, f32[65,16,128]{2,1,0:T(8,128)S(1)}, f32[2048,128]{1,0:T(8,128)S(1)}, f32[2048,128]{1,0:T(8,128)S(1)}, f32[...) custom-call(f32[2048,128]{1,0:T(8,128)} %bitcast.10, f32[2048,128]{1,0:T(8,128)} %bitcast.11, f32[32,4,128]{2,1,0:T(4,128)} %nf_hbm.1, ...), custom_call_target="tpu_custom_call" | custom-call | flops 524288 | bytes 65536 | tf_op jit(solution)/shard_map/pallas_call | solution.py:547
  2.7 1.7 %collective-permute-start = (f32[65,16,128]{2,1,0:T(8,128)S(1)}, f32[65,16,128]{2,1,0:T(8,128)S(1)}, u32[]{:S(2)}, u32[]{:S(2)}) collective-permute-start(f32[65,16,128]{2,1,0:T(8,128)S(1)} %get-tuple-element.62), channel_id=1, source_target_pairs={{0,4},{2,6},{4,0},{6,2},{8,12},{10,14},{12,8},{14,10},{16,20},{18,... | collective-permute-start | bytes 1597448 | tf_op jit(solution)/shard_map/ppermute | solution.py:591
  4.5 4.7 %collective-permute-start.1 = (f32[65,16,128]{2,1,0:T(8,128)S(1)}, f32[65,16,128]{2,1,0:T(8,128)S(1)}, u32[]{:S(2)}, u32[]{:S(2)}) collective-permute-start(f32[65,16,128]{2,1,0:T(8,128)S(1)} %get-tuple-element.63), channel_id=1, source_target_pairs={{0,2},{2,0},{4,8},{6,10},{8,4},{10,6},{12,16},{14,18},{16,12},{18,... | collective-permute-start | bytes 1597448 | tf_op jit(solution)/shard_map/ppermute | solution.py:590
  9.1 3.7 %shard_map.104 = (f32[32,2,32,128]{3,2,1,0:T(8,128)S(1)}, f32[32,2,32,128]{3,2,1,0:T(8,128)S(1)}, f32[32,2,32,128]{3,2,1,0:T(8,128)S(1)}, f32[13,32,4,128]{3,2,1...) custom-call(f32[2048,128]{1,0:T(8,128)S(1)} %get-tuple-element.54.f_ref, ...), custom_call_target="tpu_custom_call" | custom-call | flops 5242880 | bytes 655360 | tf_op jit(solution)/shard_map/pallas_call | solution.py:547
  12.9 3.3 %collective-permute-done.even_ref = f32[65,16,128]{2,1,0:T(8,128)S(1)} collective-permute-done((f32[65,16,128]{2,1,0:T(8,128)S(1)}, f32[65,16,128]{2,1,0:T(8,128)S(1)}, u32[]{:S(2)}, u32[]{:S(2)}) %collective-permute-start) | collective-permute-done | bytes 532512 | tf_op jit(solution)/shard_map/ppermute | solution.py:591
  16.2 5.2 %collective-permute-done.1.odd_ref = f32[65,16,128]{2,1,0:T(8,128)S(1)} collective-permute-done((f32[65,16,128]{2,1,0:T(8,128)S(1)}, f32[65,16,128]{2,1,0:T(8,128)S(1)}, u32[]{:S(2)}, u32[]{:S(2)}) %collective-permute-start.1) | collective-permute-done | bytes 532512 | tf_op jit(solution)/shard_map/ppermute | solution.py:590
  22.0 2.0 %collective-permute-start.2 = (f32[4,32,128]{2,1,0:T(8,128)S(1)}, f32[4,32,128]{2,1,0:T(8,128)S(1)}, u32[]{:S(2)}, u32[]{:S(2)}) collective-permute-start(f32[4,32,128]{2,1,0:T(8,128)S(1)} %get-tuple-element.65), channel_id=1, source_target_pairs={{0,1},{1,0},{2,3},{3,2},{4,5},{5,4},{6,7},{7,6},{8,9},{9,8},{10,11... | collective-permute-start | bytes 196616 | tf_op jit(solution)/shard_map/ppermute | solution.py:619
  24.0 2.7 %collective-permute-done.2.far_ref = f32[4,32,128]{2,1,0:T(8,128)S(1)} collective-permute-done((f32[4,32,128]{2,1,0:T(8,128)S(1)}, f32[4,32,128]{2,1,0:T(8,128)S(1)}, u32[]{:S(2)}, u32[]{:S(2)}) %collective-permute-start.2) | collective-permute-done | bytes 65568 | tf_op jit(solution)/shard_map/ppermute | solution.py:619
  27.1 4.7 %collective-permute-start.4 = (f32[32,16,128]{2,1,0:T(8,128)S(1)}, f32[32,16,128]{2,1,0:T(8,128)S(1)}, u32[]{:S(2)}, u32[]{:S(2)}) collective-permute-start(f32[32,16,128]{2,1,0:T(8,128)S(1)} %get-tuple-element.76), channel_id=1, source_target_pairs={{0,2},{2,0},{4,8},{6,10},{8,4},{10,6},{12,16},{14,18},{16,12},{18,... | collective-permute-start | bytes 786440 | tf_op jit(solution)/shard_map/ppermute | solution.py:629
  31.8 1.7 %shard_map.107 = (f32[32,2,32,128]{3,2,1,0:T(8,128)S(1)}, f32[32,2,32,128]{3,2,1,0:T(8,128)S(1)}, f32[32,16,128]{2,1,0:T(8,128)S(1)}, f32[33,2,8,128]{3,2,1,0:T(8,128)S(1)}) custom-call(f32[32,2,32,128]{3,2,1,0:T(8,128)S(1)} %get-tuple-element.58.pi_ref, f32[4,32,128]{2,1,0:T(8,128)S(1)} %collective-permute-done.2.far_ref, ...), custom_call_target="tpu_custom_call" | custom-call | flops 4718592 | bytes 589824 | tf_op jit(solution)/shard_map/pallas_call | solution.py:547
  33.5 3.1 %collective-permute-done.4.odd_ref = f32[32,16,128]{2,1,0:T(8,128)S(1)} collective-permute-done((f32[32,16,128]{2,1,0:T(8,128)S(1)}, f32[32,16,128]{2,1,0:T(8,128)S(1)}, u32[]{:S(2)}, u32[]{:S(2)}) %collective-permute-start.4) | collective-permute-done | bytes 262176 | tf_op jit(solution)/shard_map/ppermute | solution.py:629
  36.9 2.0 %collective-permute-start.5 = (f32[4,32,128]{2,1,0:T(8,128)S(1)}, f32[4,32,128]{2,1,0:T(8,128)S(1)}, u32[]{:S(2)}, u32[]{:S(2)}) collective-permute-start(f32[4,32,128]{2,1,0:T(8,128)S(1)} %get-tuple-element.77), channel_id=1, source_target_pairs={{0,1},{1,0},{2,3},{3,2},{4,5},{5,4},{6,7},{7,6},{8,9},{9,8},{10,11... | collective-permute-start | bytes 196616 | tf_op jit(solution)/shard_map/ppermute | solution.py:619
  38.9 3.1 %collective-permute-done.5.far_ref = f32[4,32,128]{2,1,0:T(8,128)S(1)} collective-permute-done((f32[4,32,128]{2,1,0:T(8,128)S(1)}, f32[4,32,128]{2,1,0:T(8,128)S(1)}, u32[]{:S(2)}, u32[]{:S(2)}) %collective-permute-start.5) | collective-permute-done | bytes 65568 | tf_op jit(solution)/shard_map/ppermute | solution.py:619
  42.3 4.4 %collective-permute-start.7 = (f32[32,16,128]{2,1,0:T(8,128)S(1)}, f32[32,16,128]{2,1,0:T(8,128)S(1)}, u32[]{:S(2)}, u32[]{:S(2)}) collective-permute-start(f32[32,16,128]{2,1,0:T(8,128)S(1)} %get-tuple-element.86), channel_id=1, source_target_pairs={{0,2},{2,0},{4,8},{6,10},{8,4},{10,6},{12,16},{14,18},{16,12},{18,... | collective-permute-start | bytes 786440 | tf_op jit(solution)/shard_map/ppermute | solution.py:629
  46.8 1.7 %shard_map.110 = (f32[32,2,32,128]{3,2,1,0:T(8,128)S(1)}, f32[32,2,32,128]{3,2,1,0:T(8,128)S(1)}, f32[32,16,128]{2,1,0:T(8,128)S(1)}, f32[33,2,8,128]{3,2,1,0:T(8,128)S(1)}) custom-call(f32[32,2,32,128]{3,2,1,0:T(8,128)S(1)} %get-tuple-element.72.pi_ref, f32[4,32,128]{2,1,0:T(8,128)S(1)} %collective-permute-done.5.far_ref, ...), custom_call_target="tpu_custom_call" | custom-call | flops 4718592 | bytes 589824 | tf_op jit(solution)/shard_map/pallas_call | solution.py:547
  48.5 4.1 %collective-permute-done.7.odd_ref = f32[32,16,128]{2,1,0:T(8,128)S(1)} collective-permute-done((f32[32,16,128]{2,1,0:T(8,128)S(1)}, f32[32,16,128]{2,1,0:T(8,128)S(1)}, u32[]{:S(2)}, u32[]{:S(2)}) %collective-permute-start.7) | collective-permute-done | bytes 262176 | tf_op jit(solution)/shard_map/ppermute | solution.py:629
  53.8 4.4 %collective-permute-done.8.far_ref = f32[4,32,128]{2,1,0:T(8,128)S(1)} collective-permute-done((f32[4,32,128]{2,1,0:T(8,128)S(1)}, f32[4,32,128]{2,1,0:T(8,128)S(1)}, u32[]{:S(2)}, u32[]{:S(2)}) %collective-permute-start.8) | collective-permute-done | bytes 65568 | tf_op jit(solution)/shard_map/ppermute | solution.py:619
  58.7 3.3 %collective-permute-start.10 = (f32[32,16,128]{2,1,0:T(8,128)S(1)}, f32[32,16,128]{2,1,0:T(8,128)S(1)}, u32[]{:S(2)}, u32[]{:S(2)}) collective-permute-start(f32[32,16,128]{2,1,0:T(8,128)S(1)} %get-tuple-element.96), channel_id=1, source_target_pairs={{0,2},{2,0},{4,8},{6,10},{8,4},{10,6},{12,16},{14,18},{16,12},{18,... | collective-permute-start | bytes 786440 | tf_op jit(solution)/shard_map/ppermute | solution.py:629
  62.0 1.7 %shard_map.113 = (f32[32,2,32,128]{3,2,1,0:T(8,128)S(1)}, f32[32,2,32,128]{3,2,1,0:T(8,128)S(1)}, f32[32,16,128]{2,1,0:T(8,128)S(1)}, f32[33,2,8,128]{3,2,1,0:T(8,128)S(1)}) custom-call(f32[32,2,32,128]{3,2,1,0:T(8,128)S(1)} %get-tuple-element.82.pi_ref, f32[4,32,128]{2,1,0:T(8,128)S(1)} %collective-permute-done.8.far_ref, ...), custom_call_target="tpu_custom_call" | custom-call | flops 4718592 | bytes 589824 | tf_op jit(solution)/shard_map/pallas_call | solution.py:547
  63.9 4.3 %collective-permute-done.10.odd_ref = f32[32,16,128]{2,1,0:T(8,128)S(1)} collective-permute-done((f32[32,16,128]{2,1,0:T(8,128)S(1)}, f32[32,16,128]{2,1,0:T(8,128)S(1)}, u32[]{:S(2)}, u32[]{:S(2)}) %collective-permute-start.10) | collective-permute-done | bytes 262176 | tf_op jit(solution)/shard_map/ppermute | solution.py:629
  68.5 2.0 %collective-permute-start.11 = (f32[4,32,128]{2,1,0:T(8,128)S(1)}, f32[4,32,128]{2,1,0:T(8,128)S(1)}, u32[]{:S(2)}, u32[]{:S(2)}) collective-permute-start(f32[4,32,128]{2,1,0:T(8,128)S(1)} %get-tuple-element.98), channel_id=1, source_target_pairs={{0,1},{1,0},{2,3},{3,2},{4,5},{5,4},{6,7},{7,6},{8,9},{9,8},{10,11... | collective-permute-start | bytes 196616 | tf_op jit(solution)/shard_map/ppermute | solution.py:619
  70.5 3.0 %collective-permute-done.11.far_ref = f32[4,32,128]{2,1,0:T(8,128)S(1)} collective-permute-done((f32[4,32,128]{2,1,0:T(8,128)S(1)}, f32[4,32,128]{2,1,0:T(8,128)S(1)}, u32[]{:S(2)}, u32[]{:S(2)}) %collective-permute-start.11) | collective-permute-done | bytes 65568 | tf_op jit(solution)/shard_map/ppermute | solution.py:619
  74.1 8.7 %collective-permute-start.12 = (f32[32,4,128]{2,1,0:T(4,128)S(1)}, f32[32,4,128]{2,1,0:T(4,128)S(1)}, u32[]{:S(2)}, u32[]{:S(2)}) collective-permute-start(f32[32,4,128]{2,1,0:T(4,128)S(1)} %get-tuple-element.104), channel_id=1, source_target_pairs={{0,2},{2,0},{1,3},{3,1},{4,6},{6,4},{5,7},{7,5},{8,10},{10,8},{9,1... | collective-permute-start | bytes 196616 | tf_op jit(solution)/shard_map/ppermute | solution.py:655
  82.7 1.6 %shard_map.116 = (f32[16,128,128]{2,1,0:T(8,128)}, f32[16,128,128]{2,1,0:T(8,128)}) custom-call(f32[128,32,128]{2,1,0:T(8,128)S(1)} %get-tuple-element.101.x_ref), custom_call_target="tpu_custom_call" | custom-call | flops 2097152 | bytes 262144 | tf_op jit(solution)/shard_map/pallas_call | solution.py:547
  (25 shorter events, 5.1 us)
Async XLA Ops:
  0.6 8.5 %copy-start.2 = (s32[128]{0:T(128)S(1)}, s32[128]{0:T(128)}, u32[]{:S(2)}) copy-start(s32[128]{0:T(128)} %param.15) | copy-start | bytes 1540
  0.6 8.5 %copy-start.3 = (s32[4,128]{1,0:T(4,128)S(1)}, s32[4,128]{1,0:T(4,128)}, u32[]{:S(2)}) copy-start(s32[4,128]{1,0:T(4,128)} %color_ref.1) | copy-start | bytes 6148
  0.7 8.5 %copy-start = (f32[63,4,128]{2,1,0:T(4,128)S(1)}, f32[63,4,128]{2,1,0:T(4,128)}, u32[]{:S(2)}) copy-start(f32[63,4,128]{2,1,0:T(4,128)} %mix_ref.1) | copy-start | bytes 387076
  0.7 8.5 %copy-start.1 = (f32[32,4,128]{2,1,0:T(4,128)S(1)}, f32[32,4,128]{2,1,0:T(4,128)}, u32[]{:S(2)}) copy-start(f32[32,4,128]{2,1,0:T(4,128)} %ef_ref.1) | copy-start | bytes 196612
  2.7 13.4 %collective-permute-start = (f32[65,16,128]{2,1,0:T(8,128)S(1)}, f32[65,16,128]{2,1,0:T(8,128)S(1)}, u32[]{:S(2)}, u32[]{:S(2)}) collective-permute-start(f32[65,16,128]{2,1,0:T(8,128)S(1)} %get-tuple-element.62), channel_id=1, source_target_pairs={{0,4},{2,6},{4,0},{6,2},{8,12},{10,14},{12,8},{14,10},{16,20},{18,... | collective-permute-start | bytes 1597448 | tf_op jit(solution)/shard_map/ppermute | solution.py:591
  4.5 16.9 %collective-permute-start.1 = (f32[65,16,128]{2,1,0:T(8,128)S(1)}, f32[65,16,128]{2,1,0:T(8,128)S(1)}, u32[]{:S(2)}, u32[]{:S(2)}) collective-permute-start(f32[65,16,128]{2,1,0:T(8,128)S(1)} %get-tuple-element.63), channel_id=1, source_target_pairs={{0,2},{2,0},{4,8},{6,10},{8,4},{10,6},{12,16},{14,18},{16,12},{18,... | collective-permute-start | bytes 1597448 | tf_op jit(solution)/shard_map/ppermute | solution.py:590
  22.0 4.7 %collective-permute-start.2 = (f32[4,32,128]{2,1,0:T(8,128)S(1)}, f32[4,32,128]{2,1,0:T(8,128)S(1)}, u32[]{:S(2)}, u32[]{:S(2)}) collective-permute-start(f32[4,32,128]{2,1,0:T(8,128)S(1)} %get-tuple-element.65), channel_id=1, source_target_pairs={{0,1},{1,0},{2,3},{3,2},{4,5},{5,4},{6,7},{7,6},{8,9},{9,8},{10,11... | collective-permute-start | bytes 196616 | tf_op jit(solution)/shard_map/ppermute | solution.py:619
  27.0 6.5 %collective-permute-start.3 = (f32[32,16,128]{2,1,0:T(8,128)S(1)}, f32[32,16,128]{2,1,0:T(8,128)S(1)}, u32[]{:S(2)}, u32[]{:S(2)}) collective-permute-start(f32[32,16,128]{2,1,0:T(8,128)S(1)} %get-tuple-element.75), channel_id=1, source_target_pairs={{0,4},{2,6},{4,0},{6,2},{8,12},{10,14},{12,8},{14,10},{16,20},{18,... | collective-permute-start | bytes 786440 | tf_op jit(solution)/shard_map/ppermute | solution.py:630
  27.1 9.5 %collective-permute-start.4 = (f32[32,16,128]{2,1,0:T(8,128)S(1)}, f32[32,16,128]{2,1,0:T(8,128)S(1)}, u32[]{:S(2)}, u32[]{:S(2)}) collective-permute-start(f32[32,16,128]{2,1,0:T(8,128)S(1)} %get-tuple-element.76), channel_id=1, source_target_pairs={{0,2},{2,0},{4,8},{6,10},{8,4},{10,6},{12,16},{14,18},{16,12},{18,... | collective-permute-start | bytes 786440 | tf_op jit(solution)/shard_map/ppermute | solution.py:629
  36.9 5.0 %collective-permute-start.5 = (f32[4,32,128]{2,1,0:T(8,128)S(1)}, f32[4,32,128]{2,1,0:T(8,128)S(1)}, u32[]{:S(2)}, u32[]{:S(2)}) collective-permute-start(f32[4,32,128]{2,1,0:T(8,128)S(1)} %get-tuple-element.77), channel_id=1, source_target_pairs={{0,1},{1,0},{2,3},{3,2},{4,5},{5,4},{6,7},{7,6},{8,9},{9,8},{10,11... | collective-permute-start | bytes 196616 | tf_op jit(solution)/shard_map/ppermute | solution.py:619
  42.2 6.2 %collective-permute-start.6 = (f32[32,16,128]{2,1,0:T(8,128)S(1)}, f32[32,16,128]{2,1,0:T(8,128)S(1)}, u32[]{:S(2)}, u32[]{:S(2)}) collective-permute-start(f32[32,16,128]{2,1,0:T(8,128)S(1)} %get-tuple-element.85), channel_id=1, source_target_pairs={{0,4},{2,6},{4,0},{6,2},{8,12},{10,14},{12,8},{14,10},{16,20},{18,... | collective-permute-start | bytes 786440 | tf_op jit(solution)/shard_map/ppermute | solution.py:630
  42.3 10.2 %collective-permute-start.7 = (f32[32,16,128]{2,1,0:T(8,128)S(1)}, f32[32,16,128]{2,1,0:T(8,128)S(1)}, u32[]{:S(2)}, u32[]{:S(2)}) collective-permute-start(f32[32,16,128]{2,1,0:T(8,128)S(1)} %get-tuple-element.86), channel_id=1, source_target_pairs={{0,2},{2,0},{4,8},{6,10},{8,4},{10,6},{12,16},{14,18},{16,12},{18,... | collective-permute-start | bytes 786440 | tf_op jit(solution)/shard_map/ppermute | solution.py:629
  52.9 5.4 %collective-permute-start.8 = (f32[4,32,128]{2,1,0:T(8,128)S(1)}, f32[4,32,128]{2,1,0:T(8,128)S(1)}, u32[]{:S(2)}, u32[]{:S(2)}) collective-permute-start(f32[4,32,128]{2,1,0:T(8,128)S(1)} %get-tuple-element.87), channel_id=1, source_target_pairs={{0,1},{1,0},{2,3},{3,2},{4,5},{5,4},{6,7},{7,6},{8,9},{9,8},{10,11... | collective-permute-start | bytes 196616 | tf_op jit(solution)/shard_map/ppermute | solution.py:619
  58.6 5.3 %collective-permute-start.9 = (f32[32,16,128]{2,1,0:T(8,128)S(1)}, f32[32,16,128]{2,1,0:T(8,128)S(1)}, u32[]{:S(2)}, u32[]{:S(2)}) collective-permute-start(f32[32,16,128]{2,1,0:T(8,128)S(1)} %get-tuple-element.95), channel_id=1, source_target_pairs={{0,4},{2,6},{4,0},{6,2},{8,12},{10,14},{12,8},{14,10},{16,20},{18,... | collective-permute-start | bytes 786440 | tf_op jit(solution)/shard_map/ppermute | solution.py:630
  58.7 9.5 %collective-permute-start.10 = (f32[32,16,128]{2,1,0:T(8,128)S(1)}, f32[32,16,128]{2,1,0:T(8,128)S(1)}, u32[]{:S(2)}, u32[]{:S(2)}) collective-permute-start(f32[32,16,128]{2,1,0:T(8,128)S(1)} %get-tuple-element.96), channel_id=1, source_target_pairs={{0,2},{2,0},{4,8},{6,10},{8,4},{10,6},{12,16},{14,18},{16,12},{18,... | collective-permute-start | bytes 786440 | tf_op jit(solution)/shard_map/ppermute | solution.py:629
  68.5 5.0 %collective-permute-start.11 = (f32[4,32,128]{2,1,0:T(8,128)S(1)}, f32[4,32,128]{2,1,0:T(8,128)S(1)}, u32[]{:S(2)}, u32[]{:S(2)}) collective-permute-start(f32[4,32,128]{2,1,0:T(8,128)S(1)} %get-tuple-element.98), channel_id=1, source_target_pairs={{0,1},{1,0},{2,3},{3,2},{4,5},{5,4},{6,7},{7,6},{8,9},{9,8},{10,11... | collective-permute-start | bytes 196616 | tf_op jit(solution)/shard_map/ppermute | solution.py:619
  74.1 10.2 %collective-permute-start.12 = (f32[32,4,128]{2,1,0:T(4,128)S(1)}, f32[32,4,128]{2,1,0:T(4,128)S(1)}, u32[]{:S(2)}, u32[]{:S(2)}) collective-permute-start(f32[32,4,128]{2,1,0:T(4,128)S(1)} %get-tuple-element.104), channel_id=1, source_target_pairs={{0,2},{2,0},{1,3},{3,1},{4,6},{6,4},{5,7},{7,5},{8,10},{10,8},{9,1... | collective-permute-start | bytes 196616 | tf_op jit(solution)/shard_map/ppermute | solution.py:655

commit v5 on v4

--- a/solution.py
+++ b/solution.py
@@ -84,20 +84,20 @@
     return explicit
 
 
-def back(flags, n_lev, n_pair, rows, wx_ref, far_ref, c_ref, part, put, acc_in, acc_out):
+def back(flags, n_lev, n_pair, rows, wx_ref, far, c_ref, part, put, acc_in, acc_out):
     bottom = flags[0]
     k0, dk = order(flags, n_lev)
     halves = n_pair // 8
     mid = k0 + dk * (n_lev - 1)
-    own, far = [], []
+    own, beyond = [], []
     for i, row in enumerate(rows):
         wa, wb, ff = (spread(wx_ref[j, row : row + 1, :]) for j in range(3))
         for kind in range(2):
             for g in range(halves):
-                p_far = far_ref[row, pl.ds((kind * halves + g) * 8, 8), :]
+                p_far = far(i, row, pl.ds((kind * halves + g) * 8, 8))
                 x = wa * part(mid, i, kind, g) + wb * p_far
                 own.append(x)
-                far.append(p_far + ff * x)
+                beyond.append(p_far + ff * x)
 
     def tally(s, now, nxt):
         at = jnp.where(bottom == 0, s + 1, n_lev - 1 - s)
@@ -117,7 +117,7 @@
                     put(lev, i, kind, g, xs[at])
                     at += 1
 
-    tally(n_lev - 1, own, far)
+    tally(n_lev - 1, own, beyond)
     store(mid, own)
 
     def body(q, nxt):
@@ -158,74 +158,54 @@
     return ref[lev, row, pl.ds((kind * halves + g) * 8, 8), :]
 
 
-def send_first(
-    n_lev, n_pair, n_rows, f_hbm, a_hbm, nf_hbm, depth_hbm, even_ref, odd_ref, f_ref, a_ref, nf_ref, depth_ref, sems
-):
-    stride = n_lev * n_rows
-    part = 4 * stride
-    first = lax.axis_index("level") * n_lev
-    small = [
+def load(n_pair, f_hbm, a_hbm, nf_hbm, depth_hbm, f_ref, a_ref, nf_ref, depth_ref, sems):
+    part = f_ref.shape[0] // 4
+    copies = [
         pltpu.make_async_copy(nf_hbm, nf_ref, sems.at[0]),
         pltpu.make_async_copy(depth_hbm, depth_ref, sems.at[1]),
     ]
-    large = [
-        [
-            pltpu.make_async_copy(
-                hbm.at[pl.ds(j * part, part), :], to.at[pl.ds(j * part, part), :], sems.at[2 + 2 * j + i]
-            )
-            for i, (hbm, to) in enumerate(((f_hbm, f_ref), (a_hbm, a_ref)))
-        ]
-        for j in range(n_pair // 4)
-    ]
-    for copy in small:
+    for j in range(4):
+        for i, (hbm, to) in enumerate(((f_hbm, f_ref), (a_hbm, a_ref))):
+            at = pl.ds(j * part, part)
+            copies.append(pltpu.make_async_copy(hbm.at[at, :], to.at[at, :], sems.at[2 + 2 * j + i]))
+    for copy in copies:
         copy.start()
-    for pair in large:
-        for copy in pair:
-            copy.start()
-    for copy in small:
+    for copy in copies:
         copy.wait()
+
+
+def send_first(n_lev, n_pair, n_rows, f_ref, a_ref, nf_ref, depth_ref, flow_ref, even_ref, odd_ref):
+    stride = n_lev * n_rows
+    first = lax.axis_index("level") * n_lev
+    up_even = lax.rem(lax.axis_index("horiz"), 2) == 0
     depth = depth_ref[...]
-    up_even = lax.rem(lax.axis_index("horiz"), 2) == 0
-    high = depth[n_rows - 1 : n_rows].astype(F32)
-    low = depth[0:1].astype(F32)
-    even_ref[2 * n_lev] = jnp.broadcast_to(jnp.where(up_even, high, low), (n_pair, LANES))
-    odd_ref[2 * n_lev] = jnp.broadcast_to(jnp.where(up_even, low, high), (n_pair, LANES))
+    low, high = spread(depth[0:1]), spread(depth[n_rows - 1 : n_rows])
     for g in range(n_pair // 8):
-        for pair in large[2 * g : 2 * g + 2]:
-            for copy in pair:
-                copy.wait()
-
-        def body(lev, _, g=g):
-            wet = jnp.where(first + lev < depth, 1.0, 0.0)
-            w0 = spread(wet[0:1])
-            w3 = spread(wet[n_rows - 1 : n_rows])
-            n3 = spread(nf_ref[lev, n_rows - 1 : n_rows, :])
+        to = pl.ds(g * 8, 8)
+        even_ref[n_lev, to, :] = jnp.where(up_even, high, low).astype(F32)
+        odd_ref[n_lev, to, :] = jnp.where(up_even, low, high).astype(F32)
+
+    def body(lev, _):
+        w0 = jnp.where(first + lev < low, 1.0, 0.0)
+        w3 = jnp.where(first + lev < high, 1.0, 0.0)
+        n3 = spread(nf_ref[lev, n_rows - 1 : n_rows, :])
+        s0 = spread(flow_ref[lev, n_rows - 1 : n_rows, :])
+        for g in range(n_pair // 8):
             at = g * 8 * stride + lev * n_rows
-            low, high = pl.ds(at, 8, stride=stride), pl.ds(at + n_rows - 1, 8, stride=stride)
+            at0, at3 = pl.ds(at, 8, stride=stride), pl.ds(at + n_rows - 1, 8, stride=stride)
             to = pl.ds(g * 8, 8)
-            north = jnp.where(n3 > 0.0, f_ref[high, :], a_ref[high, :]) * w3
-            south = f_ref[low, :] * w0
+            north = jnp.where(n3 > 0.0, f_ref[at3, :], a_ref[at3, :]) * w3
+            south = jnp.where(s0 < 0.0, f_ref[at0, :], a_ref[at0, :]) * w0
             even_ref[lev, to, :] = jnp.where(up_even, north, south)
             odd_ref[lev, to, :] = jnp.where(up_even, south, north)
-            south = a_ref[low, :] * w0
-            even_ref[n_lev + lev, to, :] = south
-            odd_ref[n_lev + lev, to, :] = south
-            return 0
-
-        lax.fori_loop(0, n_lev, body, 0, unroll=UNROLL)
-
-    def flow(ref):
-        for lev in range(n_lev):
-            page, line = n_lev + lev // n_pair, lev % n_pair
-            ref[page, line : line + 1, :] = nf_ref[lev, n_rows - 1 : n_rows, :]
-
-    pl.when(up_even)(lambda: flow(even_ref))
-    pl.when(jnp.logical_not(up_even))(lambda: flow(odd_ref))
+        return 0
+
+    lax.fori_loop(0, n_lev, body, 0, unroll=UNROLL)
 
 
 def prepare(
     n_lev, n_pair, n_rows, f_ref, a_ref, ef_ref, nf_ref, mix_ref, depth_ref, color_ref, fold_ref,
-    xe_ref, pi_ref, be_ref, c_ref, wx_ref, hot_ref, mf_ref, inv_ref, xi_ref,
+    mid_ref, xe_ref, pi_ref, be_ref, c_ref, wx_ref, hot_ref, mf_ref, inv_ref, xi_ref,
 ):
     flags = where_am_i(n_pair)
     halves = n_pair // 8
@@ -303,13 +283,13 @@
     for row in range(n_rows):
         hot_ref[row] = jnp.where(color_ref[row : row + 1, :] == ids, 1.0, 0.0)
 
-    inner_sweep(n_lev, n_pair, flags, xe_ref, xi_ref, c_ref, None, hot_ref, pi_ref, be_ref)
+    inner_sweep(n_lev, n_pair, flags, xe_ref, xi_ref, c_ref, None, hot_ref, pi_ref, be_ref, mid_ref)
     fold_rows(
         flags, fold_ref, nf_ref, lambda lev, kind, g: rows_at(xe_ref, 1, lev, kind, g, halves), mf_ref, n_lev, n_pair
     )
 
 
-def inner_sweep(n_lev, n_pair, flags, xe_ref, xi_ref, c_ref, ec_ref, hot_ref, pi_ref, be_ref):
+def inner_sweep(n_lev, n_pair, flags, xe_ref, xi_ref, c_ref, ec_ref, hot_ref, pi_ref, be_ref, mid_ref):
     halves = n_pair // 8
 
     def at(ref, line):
@@ -335,10 +315,13 @@
         to, line = (pi_ref, i) if i < 2 else (be_ref, i - 2)
         to[lev, line, pl.ds((kind * halves + g) * 8, 8), :] = v
 
-    sweep(flags, n_lev, n_pair, [row(1), row(2), row(0), row(3)], put, lambda *_: None)
-
-
-def edge_sweep(is_first, n_lev, n_pair, be_ref, pi_ref, c_ref, mf_ref, even_ref, odd_ref, *rest):
+    def last(i, kind, g, v):
+        mid_ref[i, pl.ds((kind * halves + g) * 8, 8), :] = v
+
+    sweep(flags, n_lev, n_pair, [row(1), row(2), row(0), row(3)], put, last)
+
+
+def edge_sweep(is_first, n_lev, n_pair, inner_ref, be_ref, c_ref, mf_ref, even_ref, odd_ref, *rest):
     flags = where_am_i(n_pair)
     halves = n_pair // 8
     is_top = flags[1] == 1
@@ -351,19 +334,18 @@
         return jnp.where(up_even, even_ref[at], odd_ref[at])
 
     if is_first:
-        xe_ref, nf_ref, depth_ref, fold_ref, pe_ref, edge_ref, ec_ref, fs_ref = rest
+        xe_ref, nf_ref, depth_ref, fold_ref, flow_ref, pe_ref, edge_ref, ec_ref, fs_ref = rest
         first = flags[0] * n_lev
         depth = depth_ref[...]
         own3 = depth[3:4]
-        south_depth = from_south(2 * n_lev, slice(0, 1), slice(None))
+        south_depth = from_south(n_lev, slice(0, 1), slice(None))
         folded = jnp.take_along_axis(spread(own3.astype(F32)), spread(fold_ref[0:1, :]), axis=1)[0:1]
-        north_depth = jnp.where(is_top, folded, from_north(2 * n_lev, slice(0, 1), slice(None)))
+        north_depth = jnp.where(is_top, folded, from_north(n_lev, slice(0, 1), slice(None)))
         open_south = jnp.where(flags[2] == 1, 0.0, 1.0)
         for lev in range(n_lev):
             k = first + lev
             kf = k.astype(F32)
-            line = lev % n_pair
-            raw = from_south(n_lev + lev // n_pair, slice(line, line + 1), slice(None))
+            raw = flow_ref[lev, 3:4, :]
             fs_ref[lev] = spread(raw)
             wi0, wi3 = c_ref[WI, lev, 0:1, :], c_ref[WI, lev, 3:4, :]
             s = raw * jnp.where(kf < south_depth, 1.0, 0.0) * open_south * wi0
@@ -382,11 +364,7 @@
 
     def come_north(lev, g):
         to = pl.ds(g * 8, 8)
-        if is_first:
-            n3 = spread(nf_ref[lev, 3:4, :])
-            come = jnp.where(n3 < 0.0, from_north(lev, to, slice(None)), from_north(n_lev + lev, to, slice(None)))
-        else:
-            come = from_north(lev, to, slice(None))
+        come = from_north(lev, to, slice(None))
         return jnp.where(is_top, mf_ref[lev, to, :], come)
 
     def row(i, number, inflow, come):
@@ -410,14 +388,12 @@
         pe_ref[lev, i, pl.ds((kind * halves + g) * 8, 8), :] = v
 
     def last(i, kind, g, v):
-        edge_ref[3 * i, pl.ds((kind * halves + g) * 8, 8), :] = v
+        edge_ref[i, pl.ds((kind * halves + g) * 8, 8), :] = v
 
     rows = [row(0, 0, ESF, lambda lev, g: from_south(lev, pl.ds(g * 8, 8), slice(None))), row(1, 3, TNF, come_north)]
     sweep(flags, n_lev, n_pair, rows, put, last)
-    k0, dk = order(flags, n_lev)
-    mid = k0 + dk * (n_lev - 1)
-    edge_ref[1] = pi_ref[mid, 0]
-    edge_ref[2] = pi_ref[mid, 1]
+    if is_first:
+        edge_ref[2:4] = inner_ref[...]
 
 
 def tallies(is_first, in_ref, out_ref, n_lev):
@@ -456,7 +432,7 @@
             odd_ref[lev, pl.ds(g * 8, 8), :] = jnp.where(up_even, south[g], north)
 
     back(
-        flags, n_lev, n_pair, (0, 3), wx_ref, far_ref, c_ref,
+        flags, n_lev, n_pair, (0, 3), wx_ref, lambda i, row, at: far_ref[i, at, :], c_ref,
         lambda lev, i, kind, g: rows_at(pe_ref, i, lev, kind, g, halves), put, acc_in, acc_out,
     )
 
@@ -466,28 +442,31 @@
 ):
     flags = where_am_i(n_pair)
     halves = n_pair // 8
-    acc_ref, (pn_ref, be_ref, mf_ref, out_ref, xi_ref) = (None, rest) if is_first else (rest[0], rest[1:])
+    acc_ref, (mid_ref, pn_ref, be_ref, mf_ref, out_ref, xi_ref) = (None, rest) if is_first else (rest[0], rest[1:])
     acc_in, acc_out = tallies(is_first, acc_ref, out_ref, n_lev)
 
     def put(lev, i, kind, g, v):
         xi_ref[lev, i, pl.ds((kind * halves + g) * 8, 8), :] = v
 
     back(
-        flags, n_lev, n_pair, (1, 2), wx_ref, far_ref, c_ref,
+        flags, n_lev, n_pair, (1, 2), wx_ref, lambda i, row, at: far_ref[2 * is_first + i, at, :], c_ref,
         lambda lev, i, kind, g: rows_at(pi_ref, i, lev, kind, g, halves), put, acc_in, acc_out,
     )
-    inner_sweep(n_lev, n_pair, flags, xe_ref, xi_ref, c_ref, ec_ref, hot_ref, pn_ref, be_ref)
+    inner_sweep(n_lev, n_pair, flags, xe_ref, xi_ref, c_ref, ec_ref, hot_ref, pn_ref, be_ref, mid_ref)
     fold_rows(
         flags, fold_ref, nf_ref, lambda lev, kind, g: rows_at(xe_ref, 1, lev, kind, g, halves), mf_ref, n_lev, n_pair
     )
 
 
 def finish(
-    n_lev, n_pair, n_rows, pe_ref, pi_ref, far_ref, c_ref, wx_ref, depth_ref, acce_ref, acci_ref,
+    n_lev, n_pair, n_rows, pe_ref, pi_ref, fare_ref, fari_ref, c_ref, wx_ref, depth_ref, acce_ref, acci_ref,
     x_ref, sens_ref, te_ref, ti_ref,
 ):
     flags = where_am_i(n_pair)
     halves = n_pair // 8
+    def far_of(i, row, at):
+        return (fare_ref[i // 3] if i in (0, 3) else fari_ref[i - 1])[at.start : at.start + at.size]
+
     ps = [(pe_ref, 0), (pi_ref, 0), (pi_ref, 1), (pe_ref, 1)]
     e_in, e_out = tallies(False, acce_ref, te_ref, n_lev)
     i_in, i_out = tallies(False, acci_ref, ti_ref, n_lev)
@@ -496,7 +475,7 @@
         x_ref[lev * n_rows + i, pl.ds((kind * halves + g) * 8, 8), :] = v
 
     back(
-        flags, n_lev, n_pair, range(4), wx_ref, far_ref, c_ref,
+        flags, n_lev, n_pair, range(4), wx_ref, far_of, c_ref,
         lambda lev, i, kind, g: rows_at(ps[i][0], ps[i][1], lev, kind, g, halves), put,
         lambda at, i: e_in(at, i // 3) if i in (0, 3) else i_in(at, i - 1),
         lambda at, i, v: e_out(at, i // 3, v) if i in (0, 3) else i_out(at, i - 1, v),
@@ -572,74 +551,75 @@
     work = n_lev * n_rows * n_all * n_x
 
     flat = vmem(n_pair * n_lev * n_rows, n_x)
-    to_even, to_odd, f2, a2, north_flow, depth = call(
-        functools.partial(send_first, n_lev, n_pair, n_rows),
-        [
-            vmem(2 * n_lev + 1, n_pair, n_x),
-            vmem(2 * n_lev + 1, n_pair, n_x),
-            flat,
-            flat,
-            vmem(n_lev, n_rows, n_x),
-            pltpu.VMEM((n_rows, n_x), jnp.int32),
-        ],
+    flow = lax.ppermute(north_flow, "horiz", [(i, (i + 1) % count) for i in range(count)])
+    f2, a2, north_flow, depth = call(
+        functools.partial(load, n_pair),
+        [flat, flat, vmem(n_lev, n_rows, n_x), pltpu.VMEM((n_rows, n_x), jnp.int32)],
         [f2, a2, north_flow, depth],
         work,
-        [pltpu.SemaphoreType.DMA((2 + n_pair // 2,))],
+        [pltpu.SemaphoreType.DMA((10,))],
         hbm_in=True,
+    )
+    message = vmem(n_lev + 1, n_pair, n_x)
+    to_even, to_odd = call(
+        functools.partial(send_first, n_lev, n_pair, n_rows), [message, message], [f2, a2, north_flow, depth, flow], work
     )
     from_odd = lax.ppermute(to_odd, pairs, odd)
     from_even = lax.ppermute(to_even, pairs, even)
     state = vmem(n_lev, 2, n_all, n_x)
     halo = vmem(n_lev, n_pair, n_x)
     acc = vmem(n_lev + 1, 2, 8, n_x)
-    xe, pi, be, c, wx, hot, mf = call(
+    edges = vmem(2, n_all, n_x)
+    mid, xe, pi, be, c, wx, hot, mf = call(
         functools.partial(prepare, n_lev, n_pair, n_rows),
-        [state] * 3 + [vmem(13, n_lev, n_rows, n_x), vmem(3, n_rows, n_x), vmem(n_rows, n_pair, n_x), halo],
+        [edges] + [state] * 3 + [vmem(13, n_lev, n_rows, n_x), vmem(3, n_rows, n_x), vmem(n_rows, n_pair, n_x), halo],
         [f2, a2, east_flow, north_flow, mixing, depth, color, fold2],
         work * 10,
         [vmem(n_lev, n_rows, n_x), state],
     )
-    edges = vmem(n_rows, n_all, n_x)
     acce = acci = None
     for step in range(STEPS):
         if step == 0:
             pe, edge, ec, fs = call(
                 functools.partial(edge_sweep, True, n_lev, n_pair),
-                [state, edges, vmem(8, n_lev, 8, n_x), vmem(n_lev, 8, n_x)],
-                [be, pi, c, mf, from_even, from_odd, xe, north_flow, depth, fold2],
+                [state, vmem(n_rows, n_all, n_x), vmem(8, n_lev, 8, n_x), vmem(n_lev, 8, n_x)],
+                [mid, be, c, mf, from_even, from_odd, xe, north_flow, depth, fold2, flow],
                 work * 3,
             )
         else:
             pe, edge = call(
                 functools.partial(edge_sweep, False, n_lev, n_pair),
                 [state, edges],
-                [be, pi, c, mf, from_even, from_odd, ec],
+                [fari, be, c, mf, from_even, from_odd, ec],
                 work * 2,
             )
-        far = lax.ppermute(edge, "level", swap)
+        fare = lax.ppermute(edge, "level", swap)
+        if step == 0:
+            fari = fare
         if step == STEPS - 1:
             break
         more = [] if step == 0 else [acce]
         xe, to_even, to_odd, acce = call(
             functools.partial(edge_back, step == 0, n_lev, n_pair),
             [state, halo, halo, acc],
-            [pe, far, c, wx, north_flow, fs] + more,
+            [pe, fare, c, wx, north_flow, fs] + more,
             work * 2,
         )
         from_odd = lax.ppermute(to_odd, pairs, odd)
         from_even = lax.ppermute(to_even, pairs, even)
         more = [] if step == 0 else [acci]
-        pi, be, mf, acci = call(
+        mid, pi, be, mf, acci = call(
             functools.partial(inner, step == 0, n_lev, n_pair),
-            [state, state, halo, acc],
-            [pi, far, c, ec, wx, north_flow, fold2, hot, xe] + more,
+            [edges, state, state, halo, acc],
+            [pi, fari, c, ec, wx, north_flow, fold2, hot, xe] + more,
             work * 9,
             [state],
         )
+        fari = lax.ppermute(mid, "level", swap)
     x, sens = call(
         functools.partial(finish, n_lev, n_pair, n_rows),
         [vmem(n_lev * n_rows, n_all, n_x), vmem(n_lev, n_rows, n_x)],
-        [pe, pi, far, c, wx, depth, acce, acci],
+        [pe, pi, fare, fari, c, wx, depth, acce, acci],
         work * 4,
         [acc, acc],
     )

time: 85.8 us -> 83.8 us (0.977)
  starting transfers between devices: 34.6 us -> 33.7 us
    ppermute x4 -> x8, waiting for transfers between devices: 13.3 us -> 24 us  [the longest x4 10.7 us: per_device(): fare = lax.ppermute(edge, 'level', swap)]
    ppermute x4, waiting for transfers between devices: 16.6 us -> 7.7 us  [per_device(): from_odd = lax.ppermute(to_odd, pairs, odd)]
    ppermute x4, starting transfers between devices: 17.2 us -> 9.05 us  [per_device(): from_odd = lax.ppermute(to_odd, pairs, odd)]
    ppermute x4 -> x8, starting transfers between devices: 6.85 us -> 14.3 us  [the longest x4 7.96 us: per_device(): fare = lax.ppermute(edge, 'level', swap)]
    ppermute x4, waiting for transfers between devices: 3.44 us -> 1.07 us  [per_device(): from_even = lax.ppermute(to_even, pairs, even)]
    ppermute x4, starting transfers between devices: 1.97 us -> 0.34 us  [per_device(): from_even = lax.ppermute(to_even, pairs, even)]
    ppermute x1, starting transfers between devices: 8.65 us -> 10.1 us  [per_device(): sens = sens + lax.ppermute(sens, 'tracer', swap)]
    pallas_call x14 -> x15, Pallas kernels: 15.5 us -> 15.6 us  [call(): pl.pallas_call(kernel, out_shape=tuple(outs), in_specs=[far if hbm_in els...]
  transfers between devices with their start and end apart: 13 -> 17, of which waited for: 10 -> 13; matrix products, arithmetic and copies ran while one was open for 0% -> 0% of each run, Pallas kernels for 12% -> 14%
where the time goes in v5:
time: 83.8 us; the launch traced here: 83.7 us
  starting transfers between devices  33.7 us (40%)
  waiting for transfers between devices  32.8 us (39%)
  Pallas kernels  15.6 us (19%)
    pallas_call x15, Pallas kernels, call(): pl.pallas_call(kernel, out_shape=tuple(outs), in_specs=[far if hbm_in els...  15.6 us
    ppermute x4, waiting for transfers between devices, per_device(): fare = lax.ppermute(edge, 'level', swap)  10.7 us
    ppermute x1, starting transfers between devices, per_device(): sens = sens + lax.ppermute(sens, 'tracer', swap)  10.1 us
    ppermute x4, starting transfers between devices, per_device(): from_odd = lax.ppermute(to_odd, pairs, odd)  9.05 us
    ppermute x3, waiting for transfers between devices, per_device(): fari = lax.ppermute(mid, 'level', swap)  8.63 us
    ppermute x4, starting transfers between devices, per_device(): fare = lax.ppermute(edge, 'level', swap)  7.96 us
    ppermute x4, waiting for transfers between devices, per_device(): from_odd = lax.ppermute(to_odd, pairs, odd)  7.7 us
    ppermute x1, waiting for transfers between devices, per_device(): lax.ppermute(north_flow, 'horiz', [(i, (i + 1) % count) for i in range(co...  4.71 us
  transfers between devices with their start and end apart: 17, of which 13 were waited for; matrix products, arithmetic and copies ran while one was open for 0% of the time, Pallas kernels for 14%

profile of v5, /device:TPU:3, one launch (start us, length us, event | category | flops | bytes accessed | tf_op | source)
XLA Modules:
  0.0 83.7 jit_solution(16695344896955675731)
XLA Ops:
  0.6 1.7 %collective-permute-start = (f32[32,4,128]{2,1,0:T(4,128)}, f32[32,4,128]{2,1,0:T(4,128)S(1)}, u32[]{:S(2)}, u32[]{:S(2)}) collective-permute-start(f32[32,4,128]{2,1,0:T(4,128)} %nf_hbm.1), channel_id=1, source_target_pairs={{0,4},{4,8},{8,12},{12,16},{16,20},{20,24},{24,28},{28,32},{32,36}... | collective-permute-start | bytes 196616 | tf_op jit(solution)/shard_map/ppermute | solution.py:554
  2.4 1.7 %shard_map.103 = (f32[2048,128]{1,0:T(8,128)S(1)}, f32[2048,128]{1,0:T(8,128)S(1)}, f32[32,4,128]{2,1,0:T(4,128)S(1)}, s32[4,128]{1,0:T(4,128)S(1)}) custom-call(f32[2048,128]{1,0:T(8,128)} %bitcast.10, f32[2048,128]{1,0:T(8,128)} %bitcast.11, f32[32,4,128]{2,1,0:T(4,128)} %nf_hbm.1, s32[4,128]{1,0:T(4,128)} %depth_hbm.1), custom_call_target="tpu_custom_call" | custom-call | flops 524288 | bytes 65536 | tf_op jit(solution)/shard_map/pallas_call | solution.py:526
  4.0 4.7 %collective-permute-done.flow_ref.rest_4_ = f32[32,4,128]{2,1,0:T(4,128)S(1)} collective-permute-done((f32[32,4,128]{2,1,0:T(4,128)}, f32[32,4,128]{2,1,0:T(4,128)S(1)}, u32[]{:S(2)}, u32[]{:S(2)}) %collective-permute-start) | collective-permute-done | bytes 65568 | tf_op jit(solution)/shard_map/ppermute | solution.py:554
  11.1 3.8 %shard_map.104 = (f32[2,32,128]{2,1,0:T(8,128)S(1)}, f32[32,2,32,128]{3,2,1,0:T(8,128)S(1)}, f32[32,2,32,128]{3,2,1,0:T(8,128)S(1)}, f32[32,2,32,128]{3,2,1,0:T(...) custom-call(f32[2048,128]{1,0:T(8,128)S(1)} %get-tuple-element.58.f_, ...), custom_call_target="tpu_custom_call" | custom-call | flops 5242880 | bytes 655360 | tf_op jit(solution)/shard_map/pallas_call | solution.py:526
  15.9 4.3 %collective-permute-done.2.odd_ref = f32[33,16,128]{2,1,0:T(8,128)S(1)} collective-permute-done((f32[33,16,128]{2,1,0:T(8,128)S(1)}, f32[33,16,128]{2,1,0:T(8,128)S(1)}, u32[]{:S(2)}, u32[]{:S(2)}) %collective-permute-start.2) | collective-permute-done | bytes 270368 | tf_op jit(solution)/shard_map/ppermute | solution.py:567
  20.8 2.2 %collective-permute-start.3 = (f32[4,32,128]{2,1,0:T(8,128)S(1)}, f32[4,32,128]{2,1,0:T(8,128)S(1)}, u32[]{:S(2)}, u32[]{:S(2)}) collective-permute-start(f32[4,32,128]{2,1,0:T(8,128)S(1)} %get-tuple-element.70), channel_id=1, source_target_pairs={{0,1},{1,0},{2,3},{3,2},{4,5},{5,4},{6,7},{7,6},{8,9},{9,8},{10,11... | collective-permute-start | bytes 196616 | tf_op jit(solution)/shard_map/ppermute | solution.py:596
  23.0 2.5 %collective-permute-done.3.far_ref = f32[4,32,128]{2,1,0:T(8,128)S(1)} collective-permute-done((f32[4,32,128]{2,1,0:T(8,128)S(1)}, f32[4,32,128]{2,1,0:T(8,128)S(1)}, u32[]{:S(2)}, u32[]{:S(2)}) %collective-permute-start.3) | collective-permute-done | bytes 65568 | tf_op jit(solution)/shard_map/ppermute | solution.py:596
  26.9 1.7 %shard_map.108 = (f32[2,32,128]{2,1,0:T(8,128)S(1)}, f32[32,2,32,128]{3,2,1,0:T(8,128)S(1)}, f32[32,2,32,128]{3,2,1,0:T(8,128)S(1)}, f32[32,16,128]{2,1,0:T(8,128)S(1)}, f32[33,2,8,128]{3,2,1,0:T(8,128)S(1)}) custom-call(f32[32,2,32,128]{3,2,1,0:T(8,128)S(1)} %get-tuple-element.62.pi_ref, f32[4,32,128]{2,1,0:T(8,128)S(1)} %collective-permute-done.3.far_ref, ...), custom_call_target="tpu_custom_call" | custom-call | flops 4718592 | bytes 589824 | tf_op jit(solution)/shard_map/pallas_call | solution.py:526
  28.6 2.2 %collective-permute-start.4 = (f32[2,32,128]{2,1,0:T(8,128)S(1)}, f32[2,32,128]{2,1,0:T(8,128)S(1)}, u32[]{:S(2)}, u32[]{:S(2)}) collective-permute-start(f32[2,32,128]{2,1,0:T(8,128)S(1)} %get-tuple-element.78), channel_id=1, source_target_pairs={{0,1},{1,0},{2,3},{3,2},{4,5},{5,4},{6,7},{7,6},{8,9},{9,8},{10,11... | collective-permute-start | bytes 98312 | tf_op jit(solution)/shard_map/ppermute | solution.py:618
  30.8 2.3 %collective-permute-done.4.inner_ref.far_ref = f32[2,32,128]{2,1,0:T(8,128)S(1)} collective-permute-done((f32[2,32,128]{2,1,0:T(8,128)S(1)}, f32[2,32,128]{2,1,0:T(8,128)S(1)}, u32[]{:S(2)}, u32[]{:S(2)}) %collective-permute-start.4) | collective-permute-done | bytes 32800 | tf_op jit(solution)/shard_map/ppermute | solution.py:618
  33.1 2.3 %collective-permute-done.6.odd_ref = f32[32,16,128]{2,1,0:T(8,128)S(1)} collective-permute-done((f32[32,16,128]{2,1,0:T(8,128)S(1)}, f32[32,16,128]{2,1,0:T(8,128)S(1)}, u32[]{:S(2)}, u32[]{:S(2)}) %collective-permute-start.6) | collective-permute-done | bytes 262176 | tf_op jit(solution)/shard_map/ppermute | solution.py:608
  35.7 2.2 %collective-permute-start.7 = (f32[2,32,128]{2,1,0:T(8,128)S(1)}, f32[2,32,128]{2,1,0:T(8,128)S(1)}, u32[]{:S(2)}, u32[]{:S(2)}) collective-permute-start(f32[2,32,128]{2,1,0:T(8,128)S(1)} %get-tuple-element.84), channel_id=1, source_target_pairs={{0,1},{1,0},{2,3},{3,2},{4,5},{5,4},{6,7},{7,6},{8,9},{9,8},{10,11... | collective-permute-start | bytes 98312 | tf_op jit(solution)/shard_map/ppermute | solution.py:596
  37.9 2.2 %collective-permute-done.7.far_ref = f32[2,32,128]{2,1,0:T(8,128)S(1)} collective-permute-done((f32[2,32,128]{2,1,0:T(8,128)S(1)}, f32[2,32,128]{2,1,0:T(8,128)S(1)}, u32[]{:S(2)}, u32[]{:S(2)}) %collective-permute-start.7) | collective-permute-done | bytes 32800 | tf_op jit(solution)/shard_map/ppermute | solution.py:596
  40.5 3.4 %collective-permute-start.10 = (f32[32,16,128]{2,1,0:T(8,128)S(1)}, f32[32,16,128]{2,1,0:T(8,128)S(1)}, u32[]{:S(2)}, u32[]{:S(2)}) collective-permute-start(f32[32,16,128]{2,1,0:T(8,128)S(1)} %get-tuple-element.93), channel_id=1, source_target_pairs={{0,2},{2,0},{4,8},{6,10},{8,4},{10,6},{12,16},{14,18},{16,12},{18,... | collective-permute-start | bytes 786440 | tf_op jit(solution)/shard_map/ppermute | solution.py:608
  43.9 1.7 %shard_map.111 = (f32[2,32,128]{2,1,0:T(8,128)S(1)}, f32[32,2,32,128]{3,2,1,0:T(8,128)S(1)}, f32[32,2,32,128]{3,2,1,0:T(8,128)S(1)}, f32[32,16,128]{2,1,0:T(8,128)S(1)}, f32[33,2,8,128]{3,2,1,0:T(8,128)S(1)}) custom-call(f32[32,2,32,128]{3,2,1,0:T(8,128)S(1)} %get-tuple-element.77.pi_ref, f32[2,32,128]{2,1,0:T(8,128)S(1)} %collective-permute-done.4.inner_ref.far_ref, ...), custom_call_target="tpu_custom_call" | custom-call | flops 4718592 | bytes 589824 | tf_op jit(solution)/shard_map/pallas_call | solution.py:526
  47.0 3.0 %collective-permute-done.8.inner_ref.far_ref = f32[2,32,128]{2,1,0:T(8,128)S(1)} collective-permute-done((f32[2,32,128]{2,1,0:T(8,128)S(1)}, f32[2,32,128]{2,1,0:T(8,128)S(1)}, u32[]{:S(2)}, u32[]{:S(2)}) %collective-permute-start.8) | collective-permute-done | bytes 32800 | tf_op jit(solution)/shard_map/ppermute | solution.py:618
  50.7 1.8 %collective-permute-start.11 = (f32[2,32,128]{2,1,0:T(8,128)S(1)}, f32[2,32,128]{2,1,0:T(8,128)S(1)}, u32[]{:S(2)}, u32[]{:S(2)}) collective-permute-start(f32[2,32,128]{2,1,0:T(8,128)S(1)} %get-tuple-element.95), channel_id=1, source_target_pairs={{0,1},{1,0},{2,3},{3,2},{4,5},{5,4},{6,7},{7,6},{8,9},{9,8},{10,11... | collective-permute-start | bytes 98312 | tf_op jit(solution)/shard_map/ppermute | solution.py:596
  52.5 3.3 %collective-permute-done.11.far_ref = f32[2,32,128]{2,1,0:T(8,128)S(1)} collective-permute-done((f32[2,32,128]{2,1,0:T(8,128)S(1)}, f32[2,32,128]{2,1,0:T(8,128)S(1)}, u32[]{:S(2)}, u32[]{:S(2)}) %collective-permute-start.11) | collective-permute-done | bytes 32800 | tf_op jit(solution)/shard_map/ppermute | solution.py:596
  56.1 3.1 %collective-permute-start.14 = (f32[32,16,128]{2,1,0:T(8,128)S(1)}, f32[32,16,128]{2,1,0:T(8,128)S(1)}, u32[]{:S(2)}, u32[]{:S(2)}) collective-permute-start(f32[32,16,128]{2,1,0:T(8,128)S(1)} %get-tuple-element.103), channel_id=1, source_target_pairs={{0,2},{2,0},{4,8},{6,10},{8,4},{10,6},{12,16},{14,18},{16,12},{18,... | collective-permute-start | bytes 786440 | tf_op jit(solution)/shard_map/ppermute | solution.py:608
  59.2 1.7 %shard_map.114 = (f32[2,32,128]{2,1,0:T(8,128)S(1)}, f32[32,2,32,128]{3,2,1,0:T(8,128)S(1)}, f32[32,2,32,128]{3,2,1,0:T(8,128)S(1)}, f32[32,16,128]{2,1,0:T(8,128)S(1)}, f32[33,2,8,128]{3,2,1,0:T(8,128)S(1)}) custom-call(f32[32,2,32,128]{3,2,1,0:T(8,128)S(1)} %get-tuple-element.88.pi_ref, f32[2,32,128]{2,1,0:T(8,128)S(1)} %collective-permute-done.8.inner_ref.far_ref, ...), custom_call_target="tpu_custom_call" | custom-call | flops 4718592 | bytes 589824 | tf_op jit(solution)/shard_map/pallas_call | solution.py:526
  61.9 3.3 %collective-permute-done.12.inner_ref.fari_ref = f32[2,32,128]{2,1,0:T(8,128)S(1)} collective-permute-done((f32[2,32,128]{2,1,0:T(8,128)S(1)}, f32[2,32,128]{2,1,0:T(8,128)S(1)}, u32[]{:S(2)}, u32[]{:S(2)}) %collective-permute-start.12) | collective-permute-done | bytes 32800 | tf_op jit(solution)/shard_map/ppermute | solution.py:618
  66.3 1.7 %collective-permute-start.15 = (f32[2,32,128]{2,1,0:T(8,128)S(1)}, f32[2,32,128]{2,1,0:T(8,128)S(1)}, u32[]{:S(2)}, u32[]{:S(2)}) collective-permute-start(f32[2,32,128]{2,1,0:T(8,128)S(1)} %get-tuple-element.106), channel_id=1, source_target_pairs={{0,1},{1,0},{2,3},{3,2},{4,5},{5,4},{6,7},{7,6},{8,9},{9,8},{10,11... | collective-permute-start | bytes 98312 | tf_op jit(solution)/shard_map/ppermute | solution.py:596
  68.0 2.8 %collective-permute-done.15.fare_ref = f32[2,32,128]{2,1,0:T(8,128)S(1)} collective-permute-done((f32[2,32,128]{2,1,0:T(8,128)S(1)}, f32[2,32,128]{2,1,0:T(8,128)S(1)}, u32[]{:S(2)}, u32[]{:S(2)}) %collective-permute-start.15) | collective-permute-done | bytes 32800 | tf_op jit(solution)/shard_map/ppermute | solution.py:596
  71.4 10.1 %collective-permute-start.16 = (f32[32,4,128]{2,1,0:T(4,128)S(1)}, f32[32,4,128]{2,1,0:T(4,128)S(1)}, u32[]{:S(2)}, u32[]{:S(2)}) collective-permute-start(f32[32,4,128]{2,1,0:T(4,128)S(1)} %get-tuple-element.112), channel_id=1, source_target_pairs={{0,2},{2,0},{1,3},{3,1},{4,6},{6,4},{5,7},{7,5},{8,10},{10,8},{9,1... | collective-permute-start | bytes 196616 | tf_op jit(solution)/shard_map/ppermute | solution.py:635
  (34 shorter events, 13.3 us)
Async XLA Ops:
  0.6 8.1 %collective-permute-start = (f32[32,4,128]{2,1,0:T(4,128)}, f32[32,4,128]{2,1,0:T(4,128)S(1)}, u32[]{:S(2)}, u32[]{:S(2)}) collective-permute-start(f32[32,4,128]{2,1,0:T(4,128)} %nf_hbm.1), channel_id=1, source_target_pairs={{0,4},{4,8},{8,12},{12,16},{16,20},{20,24},{24,28},{28,32},{32,36}... | collective-permute-start | bytes 196616 | tf_op jit(solution)/shard_map/ppermute | solution.py:554
  2.3 8.7 %copy-start = (f32[63,4,128]{2,1,0:T(4,128)S(1)}, f32[63,4,128]{2,1,0:T(4,128)}, u32[]{:S(2)}) copy-start(f32[63,4,128]{2,1,0:T(4,128)} %mix_ref.1) | copy-start | bytes 387076
  2.3 8.7 %copy-start.1 = (f32[32,4,128]{2,1,0:T(4,128)S(1)}, f32[32,4,128]{2,1,0:T(4,128)}, u32[]{:S(2)}) copy-start(f32[32,4,128]{2,1,0:T(4,128)} %ef_ref.1) | copy-start | bytes 196612
  2.3 8.7 %copy-start.2 = (s32[128]{0:T(128)S(1)}, s32[128]{0:T(128)}, u32[]{:S(2)}) copy-start(s32[128]{0:T(128)} %param.15) | copy-start | bytes 1540
  2.3 8.7 %copy-start.3 = (s32[4,128]{1,0:T(4,128)S(1)}, s32[4,128]{1,0:T(4,128)}, u32[]{:S(2)}) copy-start(s32[4,128]{1,0:T(4,128)} %color_ref.1) | copy-start | bytes 6148
  9.4 6.5 %collective-permute-start.1 = (f32[33,16,128]{2,1,0:T(8,128)S(1)}, f32[33,16,128]{2,1,0:T(8,128)S(1)}, u32[]{:S(2)}, u32[]{:S(2)}) collective-permute-start(f32[33,16,128]{2,1,0:T(8,128)S(1)} %get-tuple-element.67), channel_id=1, source_target_pairs={{0,4},{2,6},{4,0},{6,2},{8,12},{10,14},{12,8},{14,10},{16,20},{18,... | collective-permute-start | bytes 811016 | tf_op jit(solution)/shard_map/ppermute | solution.py:568
  9.5 10.7 %collective-permute-start.2 = (f32[33,16,128]{2,1,0:T(8,128)S(1)}, f32[33,16,128]{2,1,0:T(8,128)S(1)}, u32[]{:S(2)}, u32[]{:S(2)}) collective-permute-start(f32[33,16,128]{2,1,0:T(8,128)S(1)} %get-tuple-element.68), channel_id=1, source_target_pairs={{0,2},{2,0},{4,8},{6,10},{8,4},{10,6},{12,16},{14,18},{16,12},{18,... | collective-permute-start | bytes 811016 | tf_op jit(solution)/shard_map/ppermute | solution.py:567
  20.8 4.7 %collective-permute-start.3 = (f32[4,32,128]{2,1,0:T(8,128)S(1)}, f32[4,32,128]{2,1,0:T(8,128)S(1)}, u32[]{:S(2)}, u32[]{:S(2)}) collective-permute-start(f32[4,32,128]{2,1,0:T(8,128)S(1)} %get-tuple-element.70), channel_id=1, source_target_pairs={{0,1},{1,0},{2,3},{3,2},{4,5},{5,4},{6,7},{7,6},{8,9},{9,8},{10,11... | collective-permute-start | bytes 196616 | tf_op jit(solution)/shard_map/ppermute | solution.py:596
  25.8 7.4 %collective-permute-start.5 = (f32[32,16,128]{2,1,0:T(8,128)S(1)}, f32[32,16,128]{2,1,0:T(8,128)S(1)}, u32[]{:S(2)}, u32[]{:S(2)}) collective-permute-start(f32[32,16,128]{2,1,0:T(8,128)S(1)} %get-tuple-element.81), channel_id=1, source_target_pairs={{0,4},{2,6},{4,0},{6,2},{8,12},{10,14},{12,8},{14,10},{16,20},{18,... | collective-permute-start | bytes 786440 | tf_op jit(solution)/shard_map/ppermute | solution.py:609
  25.9 9.5 %collective-permute-start.6 = (f32[32,16,128]{2,1,0:T(8,128)S(1)}, f32[32,16,128]{2,1,0:T(8,128)S(1)}, u32[]{:S(2)}, u32[]{:S(2)}) collective-permute-start(f32[32,16,128]{2,1,0:T(8,128)S(1)} %get-tuple-element.82), channel_id=1, source_target_pairs={{0,2},{2,0},{4,8},{6,10},{8,4},{10,6},{12,16},{14,18},{16,12},{18,... | collective-permute-start | bytes 786440 | tf_op jit(solution)/shard_map/ppermute | solution.py:608
  28.6 4.6 %collective-permute-start.4 = (f32[2,32,128]{2,1,0:T(8,128)S(1)}, f32[2,32,128]{2,1,0:T(8,128)S(1)}, u32[]{:S(2)}, u32[]{:S(2)}) collective-permute-start(f32[2,32,128]{2,1,0:T(8,128)S(1)} %get-tuple-element.78), channel_id=1, source_target_pairs={{0,1},{1,0},{2,3},{3,2},{4,5},{5,4},{6,7},{7,6},{8,9},{9,8},{10,11... | collective-permute-start | bytes 98312 | tf_op jit(solution)/shard_map/ppermute | solution.py:618
  35.7 4.4 %collective-permute-start.7 = (f32[2,32,128]{2,1,0:T(8,128)S(1)}, f32[2,32,128]{2,1,0:T(8,128)S(1)}, u32[]{:S(2)}, u32[]{:S(2)}) collective-permute-start(f32[2,32,128]{2,1,0:T(8,128)S(1)} %get-tuple-element.84), channel_id=1, source_target_pairs={{0,1},{1,0},{2,3},{3,2},{4,5},{5,4},{6,7},{7,6},{8,9},{9,8},{10,11... | collective-permute-start | bytes 98312 | tf_op jit(solution)/shard_map/ppermute | solution.py:596
  40.4 9.6 %collective-permute-start.9 = (f32[32,16,128]{2,1,0:T(8,128)S(1)}, f32[32,16,128]{2,1,0:T(8,128)S(1)}, u32[]{:S(2)}, u32[]{:S(2)}) collective-permute-start(f32[32,16,128]{2,1,0:T(8,128)S(1)} %get-tuple-element.92), channel_id=1, source_target_pairs={{0,4},{2,6},{4,0},{6,2},{8,12},{10,14},{12,8},{14,10},{16,20},{18,... | collective-permute-start | bytes 786440 | tf_op jit(solution)/shard_map/ppermute | solution.py:609
  40.5 9.9 %collective-permute-start.10 = (f32[32,16,128]{2,1,0:T(8,128)S(1)}, f32[32,16,128]{2,1,0:T(8,128)S(1)}, u32[]{:S(2)}, u32[]{:S(2)}) collective-permute-start(f32[32,16,128]{2,1,0:T(8,128)S(1)} %get-tuple-element.93), channel_id=1, source_target_pairs={{0,2},{2,0},{4,8},{6,10},{8,4},{10,6},{12,16},{14,18},{16,12},{18,... | collective-permute-start | bytes 786440 | tf_op jit(solution)/shard_map/ppermute | solution.py:608
  45.6 4.3 %collective-permute-start.8 = (f32[2,32,128]{2,1,0:T(8,128)S(1)}, f32[2,32,128]{2,1,0:T(8,128)S(1)}, u32[]{:S(2)}, u32[]{:S(2)}) collective-permute-start(f32[2,32,128]{2,1,0:T(8,128)S(1)} %get-tuple-element.89), channel_id=1, source_target_pairs={{0,1},{1,0},{2,3},{3,2},{4,5},{5,4},{6,7},{7,6},{8,9},{9,8},{10,11... | collective-permute-start | bytes 98312 | tf_op jit(solution)/shard_map/ppermute | solution.py:618
  50.7 5.1 %collective-permute-start.11 = (f32[2,32,128]{2,1,0:T(8,128)S(1)}, f32[2,32,128]{2,1,0:T(8,128)S(1)}, u32[]{:S(2)}, u32[]{:S(2)}) collective-permute-start(f32[2,32,128]{2,1,0:T(8,128)S(1)} %get-tuple-element.95), channel_id=1, source_target_pairs={{0,1},{1,0},{2,3},{3,2},{4,5},{5,4},{6,7},{7,6},{8,9},{9,8},{10,11... | collective-permute-start | bytes 98312 | tf_op jit(solution)/shard_map/ppermute | solution.py:596
  56.0 9.2 %collective-permute-start.13 = (f32[32,16,128]{2,1,0:T(8,128)S(1)}, f32[32,16,128]{2,1,0:T(8,128)S(1)}, u32[]{:S(2)}, u32[]{:S(2)}) collective-permute-start(f32[32,16,128]{2,1,0:T(8,128)S(1)} %get-tuple-element.102), channel_id=1, source_target_pairs={{0,4},{2,6},{4,0},{6,2},{8,12},{10,14},{12,8},{14,10},{16,20},{18,... | collective-permute-start | bytes 786440 | tf_op jit(solution)/shard_map/ppermute | solution.py:609
  56.1 9.9 %collective-permute-start.14 = (f32[32,16,128]{2,1,0:T(8,128)S(1)}, f32[32,16,128]{2,1,0:T(8,128)S(1)}, u32[]{:S(2)}, u32[]{:S(2)}) collective-permute-start(f32[32,16,128]{2,1,0:T(8,128)S(1)} %get-tuple-element.103), channel_id=1, source_target_pairs={{0,2},{2,0},{4,8},{6,10},{8,4},{10,6},{12,16},{14,18},{16,12},{18,... | collective-permute-start | bytes 786440 | tf_op jit(solution)/shard_map/ppermute | solution.py:608
  60.9 4.3 %collective-permute-start.12 = (f32[2,32,128]{2,1,0:T(8,128)S(1)}, f32[2,32,128]{2,1,0:T(8,128)S(1)}, u32[]{:S(2)}, u32[]{:S(2)}) collective-permute-start(f32[2,32,128]{2,1,0:T(8,128)S(1)} %get-tuple-element.99), channel_id=1, source_target_pairs={{0,1},{1,0},{2,3},{3,2},{4,5},{5,4},{6,7},{7,6},{8,9},{9,8},{10,11... | collective-permute-start | bytes 98312 | tf_op jit(solution)/shard_map/ppermute | solution.py:618
  66.3 4.5 %collective-permute-start.15 = (f32[2,32,128]{2,1,0:T(8,128)S(1)}, f32[2,32,128]{2,1,0:T(8,128)S(1)}, u32[]{:S(2)}, u32[]{:S(2)}) collective-permute-start(f32[2,32,128]{2,1,0:T(8,128)S(1)} %get-tuple-element.106), channel_id=1, source_target_pairs={{0,1},{1,0},{2,3},{3,2},{4,5},{5,4},{6,7},{7,6},{8,9},{9,8},{10,11... | collective-permute-start | bytes 98312 | tf_op jit(solution)/shard_map/ppermute | solution.py:596
  71.4 11.6 %collective-permute-start.16 = (f32[32,4,128]{2,1,0:T(4,128)S(1)}, f32[32,4,128]{2,1,0:T(4,128)S(1)}, u32[]{:S(2)}, u32[]{:S(2)}) collective-permute-start(f32[32,4,128]{2,1,0:T(4,128)S(1)} %get-tuple-element.112), channel_id=1, source_target_pairs={{0,2},{2,0},{1,3},{3,1},{4,6},{6,4},{5,7},{7,5},{8,10},{10,8},{9,1... | collective-permute-start | bytes 196616 | tf_op jit(solution)/shard_map/ppermute | solution.py:635

commit v6 on v5

--- a/solution.py
+++ b/solution.py
@@ -189,7 +189,7 @@
         w0 = jnp.where(first + lev < low, 1.0, 0.0)
         w3 = jnp.where(first + lev < high, 1.0, 0.0)
         n3 = spread(nf_ref[lev, n_rows - 1 : n_rows, :])
-        s0 = spread(flow_ref[lev, n_rows - 1 : n_rows, :])
+        s0 = spread(flow_ref[pl.ds(lev, 1), :])
         for g in range(n_pair // 8):
             at = g * 8 * stride + lev * n_rows
             at0, at3 = pl.ds(at, 8, stride=stride), pl.ds(at + n_rows - 1, 8, stride=stride)
@@ -345,7 +345,7 @@
         for lev in range(n_lev):
             k = first + lev
             kf = k.astype(F32)
-            raw = flow_ref[lev, 3:4, :]
+            raw = flow_ref[lev : lev + 1, :]
             fs_ref[lev] = spread(raw)
             wi0, wi3 = c_ref[WI, lev, 0:1, :], c_ref[WI, lev, 3:4, :]
             s = raw * jnp.where(kf < south_depth, 1.0, 0.0) * open_south * wi0
@@ -551,7 +551,7 @@
     work = n_lev * n_rows * n_all * n_x
 
     flat = vmem(n_pair * n_lev * n_rows, n_x)
-    flow = lax.ppermute(north_flow, "horiz", [(i, (i + 1) % count) for i in range(count)])
+    flow = lax.ppermute(north_flow[:, n_rows - 1], "horiz", [(i, (i + 1) % count) for i in range(count)])
     f2, a2, north_flow, depth = call(
         functools.partial(load, n_pair),
         [flat, flat, vmem(n_lev, n_rows, n_x), pltpu.VMEM((n_rows, n_x), jnp.int32)],

time: 83.8 us -> 84 us (level)
  waiting for transfers between devices: 32.8 us -> 30.7 us
  starting transfers between devices: 33.7 us -> 35.2 us
  local copies, waits for them, and re-layouts: 0.01 us -> 0.88 us
    slice x0 -> x1, local copies, waits for them, and re-layouts: none -> 0.86 us  [per_device(): north_flow[:, n_rows - 1]]
where the time goes in v6:
time: 84 us; the launch traced here: 83.8 us
  starting transfers between devices  35.2 us (42%)
  waiting for transfers between devices  30.7 us (37%)
  Pallas kernels  15.7 us (19%)
  local copies, waits for them, and re-layouts  0.88 us (1%)
    pallas_call x15, Pallas kernels, call(): pl.pallas_call(kernel, out_shape=tuple(outs), in_specs=[far if hbm_in els...  15.7 us
    ppermute x4, waiting for transfers between devices, per_device(): fare = lax.ppermute(edge, 'level', swap)  10.7 us
    ppermute x1, starting transfers between devices, per_device(): sens = sens + lax.ppermute(sens, 'tracer', swap)  10.1 us
    ppermute x4, starting transfers between devices, per_device(): from_odd = lax.ppermute(to_odd, pairs, odd)  9.86 us
    ppermute x3, waiting for transfers between devices, per_device(): fari = lax.ppermute(mid, 'level', swap)  7.99 us
    ppermute x4, starting transfers between devices, per_device(): fare = lax.ppermute(edge, 'level', swap)  7.93 us
    ppermute x4, waiting for transfers between devices, per_device(): from_odd = lax.ppermute(to_odd, pairs, odd)  7.39 us
    ppermute x3, starting transfers between devices, per_device(): fari = lax.ppermute(mid, 'level', swap)  5.24 us
  transfers between devices with their start and end apart: 17, of which 13 were waited for; matrix products, arithmetic and copies ran while one was open for 0% of the time, Pallas kernels for 14%

profile of v6, /device:TPU:3, one launch (start us, length us, event | category | flops | bytes accessed | tf_op | source)
XLA Modules:
  0.0 83.8 jit_solution(15001828521470491984)
XLA Ops:
  1.5 1.7 %collective-permute-start = (f32[32,128]{1,0:T(8,128)S(1)}, f32[32,128]{1,0:T(8,128)S(1)}, u32[]{:S(2)}, u32[]{:S(2)}) collective-permute-start(f32[32,128]{1,0:T(8,128)S(1)} %bitcast.15), channel_id=1, source_target_pairs={{0,4},{4,8},{8,12},{12,16},{16,20},{20,24},{24,28},{28,32},{32,36}... | collective-permute-start | bytes 49160 | tf_op jit(solution)/shard_map/ppermute | solution.py:554
  4.9 4.0 %collective-permute-done.flow_ref.rest_4_ = f32[32,128]{1,0:T(8,128)S(1)} collective-permute-done((f32[32,128]{1,0:T(8,128)S(1)}, f32[32,128]{1,0:T(8,128)S(1)}, u32[]{:S(2)}, u32[]{:S(2)}) %collective-permute-start) | collective-permute-done | bytes 16416 | tf_op jit(solution)/shard_map/ppermute | solution.py:554
  9.6 2.1 %collective-permute-start.2 = (f32[33,16,128]{2,1,0:T(8,128)S(1)}, f32[33,16,128]{2,1,0:T(8,128)S(1)}, u32[]{:S(2)}, u32[]{:S(2)}) collective-permute-start(f32[33,16,128]{2,1,0:T(8,128)S(1)} %get-tuple-element.68), channel_id=1, source_target_pairs={{0,2},{2,0},{4,8},{6,10},{8,4},{10,6},{12,16},{14,18},{16,12},{18,... | collective-permute-start | bytes 811016 | tf_op jit(solution)/shard_map/ppermute | solution.py:567
  11.7 3.8 %shard_map.104 = (f32[2,32,128]{2,1,0:T(8,128)S(1)}, f32[32,2,32,128]{3,2,1,0:T(8,128)S(1)}, f32[32,2,32,128]{3,2,1,0:T(8,128)S(1)}, f32[32,2,32,128]{3,2,1,0:T(...) custom-call(f32[2048,128]{1,0:T(8,128)S(1)} %get-tuple-element.58.f_, ...), custom_call_target="tpu_custom_call" | custom-call | flops 5242880 | bytes 655360 | tf_op jit(solution)/shard_map/pallas_call | solution.py:526
  16.0 4.3 %collective-permute-done.2.odd_ref = f32[33,16,128]{2,1,0:T(8,128)S(1)} collective-permute-done((f32[33,16,128]{2,1,0:T(8,128)S(1)}, f32[33,16,128]{2,1,0:T(8,128)S(1)}, u32[]{:S(2)}, u32[]{:S(2)}) %collective-permute-start.2) | collective-permute-done | bytes 270368 | tf_op jit(solution)/shard_map/ppermute | solution.py:567
  20.9 2.2 %collective-permute-start.3 = (f32[4,32,128]{2,1,0:T(8,128)S(1)}, f32[4,32,128]{2,1,0:T(8,128)S(1)}, u32[]{:S(2)}, u32[]{:S(2)}) collective-permute-start(f32[4,32,128]{2,1,0:T(8,128)S(1)} %get-tuple-element.70), channel_id=1, source_target_pairs={{0,1},{1,0},{2,3},{3,2},{4,5},{5,4},{6,7},{7,6},{8,9},{9,8},{10,11... | collective-permute-start | bytes 196616 | tf_op jit(solution)/shard_map/ppermute | solution.py:596
  23.1 2.5 %collective-permute-done.3.far_ref = f32[4,32,128]{2,1,0:T(8,128)S(1)} collective-permute-done((f32[4,32,128]{2,1,0:T(8,128)S(1)}, f32[4,32,128]{2,1,0:T(8,128)S(1)}, u32[]{:S(2)}, u32[]{:S(2)}) %collective-permute-start.3) | collective-permute-done | bytes 65568 | tf_op jit(solution)/shard_map/ppermute | solution.py:596
  26.0 2.0 %collective-permute-start.6 = (f32[32,16,128]{2,1,0:T(8,128)S(1)}, f32[32,16,128]{2,1,0:T(8,128)S(1)}, u32[]{:S(2)}, u32[]{:S(2)}) collective-permute-start(f32[32,16,128]{2,1,0:T(8,128)S(1)} %get-tuple-element.82), channel_id=1, source_target_pairs={{0,2},{2,0},{4,8},{6,10},{8,4},{10,6},{12,16},{14,18},{16,12},{18,... | collective-permute-start | bytes 786440 | tf_op jit(solution)/shard_map/ppermute | solution.py:608
  28.0 1.7 %shard_map.108 = (f32[2,32,128]{2,1,0:T(8,128)S(1)}, f32[32,2,32,128]{3,2,1,0:T(8,128)S(1)}, f32[32,2,32,128]{3,2,1,0:T(8,128)S(1)}, f32[32,16,128]{2,1,0:T(8,128)S(1)}, f32[33,2,8,128]{3,2,1,0:T(8,128)S(1)}) custom-call(f32[32,2,32,128]{3,2,1,0:T(8,128)S(1)} %get-tuple-element.62.pi_ref, f32[4,32,128]{2,1,0:T(8,128)S(1)} %collective-permute-done.3.far_ref, ...), custom_call_target="tpu_custom_call" | custom-call | flops 4718592 | bytes 589824 | tf_op jit(solution)/shard_map/pallas_call | solution.py:526
  29.7 2.2 %collective-permute-start.4 = (f32[2,32,128]{2,1,0:T(8,128)S(1)}, f32[2,32,128]{2,1,0:T(8,128)S(1)}, u32[]{:S(2)}, u32[]{:S(2)}) collective-permute-start(f32[2,32,128]{2,1,0:T(8,128)S(1)} %get-tuple-element.78), channel_id=1, source_target_pairs={{0,1},{1,0},{2,3},{3,2},{4,5},{5,4},{6,7},{7,6},{8,9},{9,8},{10,11... | collective-permute-start | bytes 98312 | tf_op jit(solution)/shard_map/ppermute | solution.py:618
  31.9 2.3 %collective-permute-done.4.inner_ref.far_ref = f32[2,32,128]{2,1,0:T(8,128)S(1)} collective-permute-done((f32[2,32,128]{2,1,0:T(8,128)S(1)}, f32[2,32,128]{2,1,0:T(8,128)S(1)}, u32[]{:S(2)}, u32[]{:S(2)}) %collective-permute-start.4) | collective-permute-done | bytes 32800 | tf_op jit(solution)/shard_map/ppermute | solution.py:618
  35.8 2.2 %collective-permute-start.7 = (f32[2,32,128]{2,1,0:T(8,128)S(1)}, f32[2,32,128]{2,1,0:T(8,128)S(1)}, u32[]{:S(2)}, u32[]{:S(2)}) collective-permute-start(f32[2,32,128]{2,1,0:T(8,128)S(1)} %get-tuple-element.84), channel_id=1, source_target_pairs={{0,1},{1,0},{2,3},{3,2},{4,5},{5,4},{6,7},{7,6},{8,9},{9,8},{10,11... | collective-permute-start | bytes 98312 | tf_op jit(solution)/shard_map/ppermute | solution.py:596
  38.0 2.2 %collective-permute-done.7.far_ref = f32[2,32,128]{2,1,0:T(8,128)S(1)} collective-permute-done((f32[2,32,128]{2,1,0:T(8,128)S(1)}, f32[2,32,128]{2,1,0:T(8,128)S(1)}, u32[]{:S(2)}, u32[]{:S(2)}) %collective-permute-start.7) | collective-permute-done | bytes 32800 | tf_op jit(solution)/shard_map/ppermute | solution.py:596
  40.6 3.1 %collective-permute-start.10 = (f32[32,16,128]{2,1,0:T(8,128)S(1)}, f32[32,16,128]{2,1,0:T(8,128)S(1)}, u32[]{:S(2)}, u32[]{:S(2)}) collective-permute-start(f32[32,16,128]{2,1,0:T(8,128)S(1)} %get-tuple-element.93), channel_id=1, source_target_pairs={{0,2},{2,0},{4,8},{6,10},{8,4},{10,6},{12,16},{14,18},{16,12},{18,... | collective-permute-start | bytes 786440 | tf_op jit(solution)/shard_map/ppermute | solution.py:608
  43.7 1.7 %shard_map.111 = (f32[2,32,128]{2,1,0:T(8,128)S(1)}, f32[32,2,32,128]{3,2,1,0:T(8,128)S(1)}, f32[32,2,32,128]{3,2,1,0:T(8,128)S(1)}, f32[32,16,128]{2,1,0:T(8,128)S(1)}, f32[33,2,8,128]{3,2,1,0:T(8,128)S(1)}) custom-call(f32[32,2,32,128]{3,2,1,0:T(8,128)S(1)} %get-tuple-element.77.pi_ref, f32[2,32,128]{2,1,0:T(8,128)S(1)} %collective-permute-done.4.inner_ref.far_ref, ...), custom_call_target="tpu_custom_call" | custom-call | flops 4718592 | bytes 589824 | tf_op jit(solution)/shard_map/pallas_call | solution.py:526
  47.1 2.7 %collective-permute-done.8.inner_ref.far_ref = f32[2,32,128]{2,1,0:T(8,128)S(1)} collective-permute-done((f32[2,32,128]{2,1,0:T(8,128)S(1)}, f32[2,32,128]{2,1,0:T(8,128)S(1)}, u32[]{:S(2)}, u32[]{:S(2)}) %collective-permute-start.8) | collective-permute-done | bytes 32800 | tf_op jit(solution)/shard_map/ppermute | solution.py:618
  50.8 1.8 %collective-permute-start.11 = (f32[2,32,128]{2,1,0:T(8,128)S(1)}, f32[2,32,128]{2,1,0:T(8,128)S(1)}, u32[]{:S(2)}, u32[]{:S(2)}) collective-permute-start(f32[2,32,128]{2,1,0:T(8,128)S(1)} %get-tuple-element.95), channel_id=1, source_target_pairs={{0,1},{1,0},{2,3},{3,2},{4,5},{5,4},{6,7},{7,6},{8,9},{9,8},{10,11... | collective-permute-start | bytes 98312 | tf_op jit(solution)/shard_map/ppermute | solution.py:596
  52.6 3.3 %collective-permute-done.11.far_ref = f32[2,32,128]{2,1,0:T(8,128)S(1)} collective-permute-done((f32[2,32,128]{2,1,0:T(8,128)S(1)}, f32[2,32,128]{2,1,0:T(8,128)S(1)}, u32[]{:S(2)}, u32[]{:S(2)}) %collective-permute-start.11) | collective-permute-done | bytes 32800 | tf_op jit(solution)/shard_map/ppermute | solution.py:596
  56.3 2.7 %collective-permute-start.14 = (f32[32,16,128]{2,1,0:T(8,128)S(1)}, f32[32,16,128]{2,1,0:T(8,128)S(1)}, u32[]{:S(2)}, u32[]{:S(2)}) collective-permute-start(f32[32,16,128]{2,1,0:T(8,128)S(1)} %get-tuple-element.103), channel_id=1, source_target_pairs={{0,2},{2,0},{4,8},{6,10},{8,4},{10,6},{12,16},{14,18},{16,12},{18,... | collective-permute-start | bytes 786440 | tf_op jit(solution)/shard_map/ppermute | solution.py:608
  59.0 1.7 %shard_map.114 = (f32[2,32,128]{2,1,0:T(8,128)S(1)}, f32[32,2,32,128]{3,2,1,0:T(8,128)S(1)}, f32[32,2,32,128]{3,2,1,0:T(8,128)S(1)}, f32[32,16,128]{2,1,0:T(8,128)S(1)}, f32[33,2,8,128]{3,2,1,0:T(8,128)S(1)}) custom-call(f32[32,2,32,128]{3,2,1,0:T(8,128)S(1)} %get-tuple-element.88.pi_ref, f32[2,32,128]{2,1,0:T(8,128)S(1)} %collective-permute-done.8.inner_ref.far_ref, ...), custom_call_target="tpu_custom_call" | custom-call | flops 4718592 | bytes 589824 | tf_op jit(solution)/shard_map/pallas_call | solution.py:526
  62.1 3.0 %collective-permute-done.12.inner_ref.fari_ref = f32[2,32,128]{2,1,0:T(8,128)S(1)} collective-permute-done((f32[2,32,128]{2,1,0:T(8,128)S(1)}, f32[2,32,128]{2,1,0:T(8,128)S(1)}, u32[]{:S(2)}, u32[]{:S(2)}) %collective-permute-start.12) | collective-permute-done | bytes 32800 | tf_op jit(solution)/shard_map/ppermute | solution.py:618
  66.4 1.7 %collective-permute-start.15 = (f32[2,32,128]{2,1,0:T(8,128)S(1)}, f32[2,32,128]{2,1,0:T(8,128)S(1)}, u32[]{:S(2)}, u32[]{:S(2)}) collective-permute-start(f32[2,32,128]{2,1,0:T(8,128)S(1)} %get-tuple-element.106), channel_id=1, source_target_pairs={{0,1},{1,0},{2,3},{3,2},{4,5},{5,4},{6,7},{7,6},{8,9},{9,8},{10,11... | collective-permute-start | bytes 98312 | tf_op jit(solution)/shard_map/ppermute | solution.py:596
  68.2 2.8 %collective-permute-done.15.fare_ref = f32[2,32,128]{2,1,0:T(8,128)S(1)} collective-permute-done((f32[2,32,128]{2,1,0:T(8,128)S(1)}, f32[2,32,128]{2,1,0:T(8,128)S(1)}, u32[]{:S(2)}, u32[]{:S(2)}) %collective-permute-start.15) | collective-permute-done | bytes 32800 | tf_op jit(solution)/shard_map/ppermute | solution.py:596
  71.5 10.1 %collective-permute-start.16 = (f32[32,4,128]{2,1,0:T(4,128)S(1)}, f32[32,4,128]{2,1,0:T(4,128)S(1)}, u32[]{:S(2)}, u32[]{:S(2)}) collective-permute-start(f32[32,4,128]{2,1,0:T(4,128)S(1)} %get-tuple-element.112), channel_id=1, source_target_pairs={{0,2},{2,0},{1,3},{3,1},{4,6},{6,4},{5,7},{7,5},{8,10},{10,8},{9,1... | collective-permute-start | bytes 196616 | tf_op jit(solution)/shard_map/ppermute | solution.py:635
  (35 shorter events, 15.4 us)
Async XLA Ops:
  1.5 7.4 %collective-permute-start = (f32[32,128]{1,0:T(8,128)S(1)}, f32[32,128]{1,0:T(8,128)S(1)}, u32[]{:S(2)}, u32[]{:S(2)}) collective-permute-start(f32[32,128]{1,0:T(8,128)S(1)} %bitcast.15), channel_id=1, source_target_pairs={{0,4},{4,8},{8,12},{12,16},{16,20},{20,24},{24,28},{28,32},{32,36}... | collective-permute-start | bytes 49160 | tf_op jit(solution)/shard_map/ppermute | solution.py:554
  3.2 8.4 %copy-start = (f32[63,4,128]{2,1,0:T(4,128)S(1)}, f32[63,4,128]{2,1,0:T(4,128)}, u32[]{:S(2)}) copy-start(f32[63,4,128]{2,1,0:T(4,128)} %mix_ref.1) | copy-start | bytes 387076
  3.2 8.4 %copy-start.1 = (f32[32,4,128]{2,1,0:T(4,128)S(1)}, f32[32,4,128]{2,1,0:T(4,128)}, u32[]{:S(2)}) copy-start(f32[32,4,128]{2,1,0:T(4,128)} %ef_ref.1) | copy-start | bytes 196612
  3.2 8.4 %copy-start.2 = (s32[128]{0:T(128)S(1)}, s32[128]{0:T(128)}, u32[]{:S(2)}) copy-start(s32[128]{0:T(128)} %param.15) | copy-start | bytes 1540
  3.2 8.4 %copy-start.3 = (s32[4,128]{1,0:T(4,128)S(1)}, s32[4,128]{1,0:T(4,128)}, u32[]{:S(2)}) copy-start(s32[4,128]{1,0:T(4,128)} %color_ref.1) | copy-start | bytes 6148
  9.5 6.5 %collective-permute-start.1 = (f32[33,16,128]{2,1,0:T(8,128)S(1)}, f32[33,16,128]{2,1,0:T(8,128)S(1)}, u32[]{:S(2)}, u32[]{:S(2)}) collective-permute-start(f32[33,16,128]{2,1,0:T(8,128)S(1)} %get-tuple-element.67), channel_id=1, source_target_pairs={{0,4},{2,6},{4,0},{6,2},{8,12},{10,14},{12,8},{14,10},{16,20},{18,... | collective-permute-start | bytes 811016 | tf_op jit(solution)/shard_map/ppermute | solution.py:568
  9.6 10.7 %collective-permute-start.2 = (f32[33,16,128]{2,1,0:T(8,128)S(1)}, f32[33,16,128]{2,1,0:T(8,128)S(1)}, u32[]{:S(2)}, u32[]{:S(2)}) collective-permute-start(f32[33,16,128]{2,1,0:T(8,128)S(1)} %get-tuple-element.68), channel_id=1, source_target_pairs={{0,2},{2,0},{4,8},{6,10},{8,4},{10,6},{12,16},{14,18},{16,12},{18,... | collective-permute-start | bytes 811016 | tf_op jit(solution)/shard_map/ppermute | solution.py:567
  20.9 4.7 %collective-permute-start.3 = (f32[4,32,128]{2,1,0:T(8,128)S(1)}, f32[4,32,128]{2,1,0:T(8,128)S(1)}, u32[]{:S(2)}, u32[]{:S(2)}) collective-permute-start(f32[4,32,128]{2,1,0:T(8,128)S(1)} %get-tuple-element.70), channel_id=1, source_target_pairs={{0,1},{1,0},{2,3},{3,2},{4,5},{5,4},{6,7},{7,6},{8,9},{9,8},{10,11... | collective-permute-start | bytes 196616 | tf_op jit(solution)/shard_map/ppermute | solution.py:596
  25.9 8.3 %collective-permute-start.5 = (f32[32,16,128]{2,1,0:T(8,128)S(1)}, f32[32,16,128]{2,1,0:T(8,128)S(1)}, u32[]{:S(2)}, u32[]{:S(2)}) collective-permute-start(f32[32,16,128]{2,1,0:T(8,128)S(1)} %get-tuple-element.81), channel_id=1, source_target_pairs={{0,4},{2,6},{4,0},{6,2},{8,12},{10,14},{12,8},{14,10},{16,20},{18,... | collective-permute-start | bytes 786440 | tf_op jit(solution)/shard_map/ppermute | solution.py:609
  26.0 9.5 %collective-permute-start.6 = (f32[32,16,128]{2,1,0:T(8,128)S(1)}, f32[32,16,128]{2,1,0:T(8,128)S(1)}, u32[]{:S(2)}, u32[]{:S(2)}) collective-permute-start(f32[32,16,128]{2,1,0:T(8,128)S(1)} %get-tuple-element.82), channel_id=1, source_target_pairs={{0,2},{2,0},{4,8},{6,10},{8,4},{10,6},{12,16},{14,18},{16,12},{18,... | collective-permute-start | bytes 786440 | tf_op jit(solution)/shard_map/ppermute | solution.py:608
  29.7 4.5 %collective-permute-start.4 = (f32[2,32,128]{2,1,0:T(8,128)S(1)}, f32[2,32,128]{2,1,0:T(8,128)S(1)}, u32[]{:S(2)}, u32[]{:S(2)}) collective-permute-start(f32[2,32,128]{2,1,0:T(8,128)S(1)} %get-tuple-element.78), channel_id=1, source_target_pairs={{0,1},{1,0},{2,3},{3,2},{4,5},{5,4},{6,7},{7,6},{8,9},{9,8},{10,11... | collective-permute-start | bytes 98312 | tf_op jit(solution)/shard_map/ppermute | solution.py:618
  35.8 4.4 %collective-permute-start.7 = (f32[2,32,128]{2,1,0:T(8,128)S(1)}, f32[2,32,128]{2,1,0:T(8,128)S(1)}, u32[]{:S(2)}, u32[]{:S(2)}) collective-permute-start(f32[2,32,128]{2,1,0:T(8,128)S(1)} %get-tuple-element.84), channel_id=1, source_target_pairs={{0,1},{1,0},{2,3},{3,2},{4,5},{5,4},{6,7},{7,6},{8,9},{9,8},{10,11... | collective-permute-start | bytes 98312 | tf_op jit(solution)/shard_map/ppermute | solution.py:596
  40.5 9.3 %collective-permute-start.9 = (f32[32,16,128]{2,1,0:T(8,128)S(1)}, f32[32,16,128]{2,1,0:T(8,128)S(1)}, u32[]{:S(2)}, u32[]{:S(2)}) collective-permute-start(f32[32,16,128]{2,1,0:T(8,128)S(1)} %get-tuple-element.92), channel_id=1, source_target_pairs={{0,4},{2,6},{4,0},{6,2},{8,12},{10,14},{12,8},{14,10},{16,20},{18,... | collective-permute-start | bytes 786440 | tf_op jit(solution)/shard_map/ppermute | solution.py:609
  40.6 9.9 %collective-permute-start.10 = (f32[32,16,128]{2,1,0:T(8,128)S(1)}, f32[32,16,128]{2,1,0:T(8,128)S(1)}, u32[]{:S(2)}, u32[]{:S(2)}) collective-permute-start(f32[32,16,128]{2,1,0:T(8,128)S(1)} %get-tuple-element.93), channel_id=1, source_target_pairs={{0,2},{2,0},{4,8},{6,10},{8,4},{10,6},{12,16},{14,18},{16,12},{18,... | collective-permute-start | bytes 786440 | tf_op jit(solution)/shard_map/ppermute | solution.py:608
  45.5 4.3 %collective-permute-start.8 = (f32[2,32,128]{2,1,0:T(8,128)S(1)}, f32[2,32,128]{2,1,0:T(8,128)S(1)}, u32[]{:S(2)}, u32[]{:S(2)}) collective-permute-start(f32[2,32,128]{2,1,0:T(8,128)S(1)} %get-tuple-element.89), channel_id=1, source_target_pairs={{0,1},{1,0},{2,3},{3,2},{4,5},{5,4},{6,7},{7,6},{8,9},{9,8},{10,11... | collective-permute-start | bytes 98312 | tf_op jit(solution)/shard_map/ppermute | solution.py:618
  50.8 5.1 %collective-permute-start.11 = (f32[2,32,128]{2,1,0:T(8,128)S(1)}, f32[2,32,128]{2,1,0:T(8,128)S(1)}, u32[]{:S(2)}, u32[]{:S(2)}) collective-permute-start(f32[2,32,128]{2,1,0:T(8,128)S(1)} %get-tuple-element.95), channel_id=1, source_target_pairs={{0,1},{1,0},{2,3},{3,2},{4,5},{5,4},{6,7},{7,6},{8,9},{9,8},{10,11... | collective-permute-start | bytes 98312 | tf_op jit(solution)/shard_map/ppermute | solution.py:596
  56.2 8.9 %collective-permute-start.13 = (f32[32,16,128]{2,1,0:T(8,128)S(1)}, f32[32,16,128]{2,1,0:T(8,128)S(1)}, u32[]{:S(2)}, u32[]{:S(2)}) collective-permute-start(f32[32,16,128]{2,1,0:T(8,128)S(1)} %get-tuple-element.102), channel_id=1, source_target_pairs={{0,4},{2,6},{4,0},{6,2},{8,12},{10,14},{12,8},{14,10},{16,20},{18,... | collective-permute-start | bytes 786440 | tf_op jit(solution)/shard_map/ppermute | solution.py:609
  56.3 9.9 %collective-permute-start.14 = (f32[32,16,128]{2,1,0:T(8,128)S(1)}, f32[32,16,128]{2,1,0:T(8,128)S(1)}, u32[]{:S(2)}, u32[]{:S(2)}) collective-permute-start(f32[32,16,128]{2,1,0:T(8,128)S(1)} %get-tuple-element.103), channel_id=1, source_target_pairs={{0,2},{2,0},{4,8},{6,10},{8,4},{10,6},{12,16},{14,18},{16,12},{18,... | collective-permute-start | bytes 786440 | tf_op jit(solution)/shard_map/ppermute | solution.py:608
  60.7 4.3 %collective-permute-start.12 = (f32[2,32,128]{2,1,0:T(8,128)S(1)}, f32[2,32,128]{2,1,0:T(8,128)S(1)}, u32[]{:S(2)}, u32[]{:S(2)}) collective-permute-start(f32[2,32,128]{2,1,0:T(8,128)S(1)} %get-tuple-element.99), channel_id=1, source_target_pairs={{0,1},{1,0},{2,3},{3,2},{4,5},{5,4},{6,7},{7,6},{8,9},{9,8},{10,11... | collective-permute-start | bytes 98312 | tf_op jit(solution)/shard_map/ppermute | solution.py:618
  66.4 4.5 %collective-permute-start.15 = (f32[2,32,128]{2,1,0:T(8,128)S(1)}, f32[2,32,128]{2,1,0:T(8,128)S(1)}, u32[]{:S(2)}, u32[]{:S(2)}) collective-permute-start(f32[2,32,128]{2,1,0:T(8,128)S(1)} %get-tuple-element.106), channel_id=1, source_target_pairs={{0,1},{1,0},{2,3},{3,2},{4,5},{5,4},{6,7},{7,6},{8,9},{9,8},{10,11... | collective-permute-start | bytes 98312 | tf_op jit(solution)/shard_map/ppermute | solution.py:596
  71.5 11.6 %collective-permute-start.16 = (f32[32,4,128]{2,1,0:T(4,128)S(1)}, f32[32,4,128]{2,1,0:T(4,128)S(1)}, u32[]{:S(2)}, u32[]{:S(2)}) collective-permute-start(f32[32,4,128]{2,1,0:T(4,128)S(1)} %get-tuple-element.112), channel_id=1, source_target_pairs={{0,2},{2,0},{1,3},{3,1},{4,6},{6,4},{5,7},{7,5},{8,10},{10,8},{9,1... | collective-permute-start | bytes 196616 | tf_op jit(solution)/shard_map/ppermute | solution.py:635

commit v7 on v5

--- a/solution.py
+++ b/solution.py
@@ -158,7 +158,7 @@
     return ref[lev, row, pl.ds((kind * halves + g) * 8, 8), :]
 
 
-def load(n_pair, f_hbm, a_hbm, nf_hbm, depth_hbm, f_ref, a_ref, nf_ref, depth_ref, sems):
+def load(n_lev, n_pair, n_rows, f_hbm, a_hbm, nf_hbm, depth_hbm, f_ref, a_ref, nf_ref, depth_ref, edge_ref, sems):
     part = f_ref.shape[0] // 4
     copies = [
         pltpu.make_async_copy(nf_hbm, nf_ref, sems.at[0]),
@@ -172,11 +172,28 @@
         copy.start()
     for copy in copies:
         copy.wait()
-
-
-def send_first(n_lev, n_pair, n_rows, f_ref, a_ref, nf_ref, depth_ref, flow_ref, even_ref, odd_ref):
     stride = n_lev * n_rows
     first = lax.axis_index("level") * n_lev
+    depth = depth_ref[...]
+    low, high = spread(depth[0:1]), spread(depth[n_rows - 1 : n_rows])
+
+    def body(lev, _):
+        w0 = jnp.where(first + lev < low, 1.0, 0.0)
+        w3 = jnp.where(first + lev < high, 1.0, 0.0)
+        n3 = spread(nf_ref[lev, n_rows - 1 : n_rows, :])
+        for g in range(n_pair // 8):
+            at = g * 8 * stride + lev * n_rows
+            at0, at3 = pl.ds(at, 8, stride=stride), pl.ds(at + n_rows - 1, 8, stride=stride)
+            to = pl.ds(g * 8, 8)
+            edge_ref[0, lev, to, :] = jnp.where(n3 > 0.0, f_ref[at3, :], a_ref[at3, :]) * w3
+            edge_ref[1, lev, to, :] = f_ref[at0, :] * w0
+            edge_ref[2, lev, to, :] = a_ref[at0, :] * w0
+        return 0
+
+    lax.fori_loop(0, n_lev, body, 0, unroll=UNROLL)
+
+
+def send_first(n_lev, n_pair, n_rows, edge_ref, depth_ref, flow_ref, even_ref, odd_ref):
     up_even = lax.rem(lax.axis_index("horiz"), 2) == 0
     depth = depth_ref[...]
     low, high = spread(depth[0:1]), spread(depth[n_rows - 1 : n_rows])
@@ -186,16 +203,11 @@
         odd_ref[n_lev, to, :] = jnp.where(up_even, low, high).astype(F32)
 
     def body(lev, _):
-        w0 = jnp.where(first + lev < low, 1.0, 0.0)
-        w3 = jnp.where(first + lev < high, 1.0, 0.0)
-        n3 = spread(nf_ref[lev, n_rows - 1 : n_rows, :])
         s0 = spread(flow_ref[lev, n_rows - 1 : n_rows, :])
         for g in range(n_pair // 8):
-            at = g * 8 * stride + lev * n_rows
-            at0, at3 = pl.ds(at, 8, stride=stride), pl.ds(at + n_rows - 1, 8, stride=stride)
             to = pl.ds(g * 8, 8)
-            north = jnp.where(n3 > 0.0, f_ref[at3, :], a_ref[at3, :]) * w3
-            south = jnp.where(s0 < 0.0, f_ref[at0, :], a_ref[at0, :]) * w0
+            north = edge_ref[0, lev, to, :]
+            south = jnp.where(s0 < 0.0, edge_ref[1, lev, to, :], edge_ref[2, lev, to, :])
             even_ref[lev, to, :] = jnp.where(up_even, north, south)
             odd_ref[lev, to, :] = jnp.where(up_even, south, north)
         return 0
@@ -552,9 +564,15 @@
 
     flat = vmem(n_pair * n_lev * n_rows, n_x)
     flow = lax.ppermute(north_flow, "horiz", [(i, (i + 1) % count) for i in range(count)])
-    f2, a2, north_flow, depth = call(
-        functools.partial(load, n_pair),
-        [flat, flat, vmem(n_lev, n_rows, n_x), pltpu.VMEM((n_rows, n_x), jnp.int32)],
+    f2, a2, north_flow, depth, edge_rows = call(
+        functools.partial(load, n_lev, n_pair, n_rows),
+        [
+            flat,
+            flat,
+            vmem(n_lev, n_rows, n_x),
+            pltpu.VMEM((n_rows, n_x), jnp.int32),
+            vmem(3, n_lev, n_pair, n_x),
+        ],
         [f2, a2, north_flow, depth],
         work,
         [pltpu.SemaphoreType.DMA((10,))],
@@ -562,7 +580,7 @@
     )
     message = vmem(n_lev + 1, n_pair, n_x)
     to_even, to_odd = call(
-        functools.partial(send_first, n_lev, n_pair, n_rows), [message, message], [f2, a2, north_flow, depth, flow], work
+        functools.partial(send_first, n_lev, n_pair, n_rows), [message, message], [edge_rows, depth, flow], work
     )
     from_odd = lax.ppermute(to_odd, pairs, odd)
     from_even = lax.ppermute(to_even, pairs, even)

time: 83.8 us -> 83.3 us (level)
  waiting for transfers between devices: 32.8 us -> 31.3 us
  starting transfers between devices: 33.7 us -> 34.6 us
    ppermute x4, starting transfers between devices: 9.05 us -> 9.99 us  [per_device(): from_odd = lax.ppermute(to_odd, pairs, odd)]
  transfers between devices with their start and end apart: 17 -> 17, of which waited for: 13 -> 13; matrix products, arithmetic and copies ran while one was open for 0% -> 0% of each run, Pallas kernels for 14% -> 15%
where the time goes in v7:
time: 83.3 us; the launch traced here: 83.1 us
  starting transfers between devices  34.6 us (42%)
  waiting for transfers between devices  31.3 us (38%)
  Pallas kernels  15.7 us (19%)
    pallas_call x15, Pallas kernels, call(): pl.pallas_call(kernel, out_shape=tuple(outs), in_specs=[far if hbm_in els...  15.7 us
    ppermute x4, waiting for transfers between devices, per_device(): fare = lax.ppermute(edge, 'level', swap)  10.7 us
    ppermute x1, starting transfers between devices, per_device(): sens = sens + lax.ppermute(sens, 'tracer', swap)  10.1 us
    ppermute x4, starting transfers between devices, per_device(): from_odd = lax.ppermute(to_odd, pairs, odd)  9.99 us
    ppermute x3, waiting for transfers between devices, per_device(): fari = lax.ppermute(mid, 'level', swap)  8.66 us
    ppermute x4, starting transfers between devices, per_device(): fare = lax.ppermute(edge, 'level', swap)  7.96 us
    ppermute x4, waiting for transfers between devices, per_device(): from_odd = lax.ppermute(to_odd, pairs, odd)  7.06 us
    ppermute x3, starting transfers between devices, per_device(): fari = lax.ppermute(mid, 'level', swap)  4.58 us
  transfers between devices with their start and end apart: 17, of which 13 were waited for; matrix products, arithmetic and copies ran while one was open for 0% of the time, Pallas kernels for 15%

profile of v7, /device:TPU:3, one launch (start us, length us, event | category | flops | bytes accessed | tf_op | source)
XLA Modules:
  0.0 83.1 jit_solution(12756326474123573613)
XLA Ops:
  0.7 1.7 %collective-permute-start = (f32[32,4,128]{2,1,0:T(4,128)}, f32[32,4,128]{2,1,0:T(4,128)S(1)}, u32[]{:S(2)}, u32[]{:S(2)}) collective-permute-start(f32[32,4,128]{2,1,0:T(4,128)} %nf_hbm.1), channel_id=1, source_target_pairs={{0,4},{4,8},{8,12},{12,16},{16,20},{20,24},{24,28},{28,32},{32,36}... | collective-permute-start | bytes 196616 | tf_op jit(solution)/shard_map/ppermute | solution.py:566
  2.4 2.3 %shard_map.103 = (f32[2048,128]{1,0:T(8,128)S(1)}, f32[2048,128]{1,0:T(8,128)S(1)}, f32[32,4,128]{2,1,0:T(4,128)S(1)}, s32[4,128]{1,0:T(4,128)S(1)}, f32[3,32,16,128]{3,2,1,0:T(8,128)S(1)}) custom-call(f32[2048,128]{1,0:T(8,128)} %bitcast.10, f32[2048,128]{1,0:T(8,128)} %bitcast.11, f32[32,4,128]{2,1,0:T(4,128)} %nf_hbm.1, s32[4,128]{1,0:T(4,128)} %depth_hbm.1), custom_call_target="tpu_custom_call" | custom-call | flops 524288 | bytes 65536 | tf_op jit(solution)/shard_map/pallas_call | solution.py:538
  4.6 4.1 %collective-permute-done.flow_ref.rest_4_ = f32[32,4,128]{2,1,0:T(4,128)S(1)} collective-permute-done((f32[32,4,128]{2,1,0:T(4,128)}, f32[32,4,128]{2,1,0:T(4,128)S(1)}, u32[]{:S(2)}, u32[]{:S(2)}) %collective-permute-start) | collective-permute-done | bytes 65568 | tf_op jit(solution)/shard_map/ppermute | solution.py:566
  9.0 1.9 %collective-permute-start.2 = (f32[33,16,128]{2,1,0:T(8,128)S(1)}, f32[33,16,128]{2,1,0:T(8,128)S(1)}, u32[]{:S(2)}, u32[]{:S(2)}) collective-permute-start(f32[33,16,128]{2,1,0:T(8,128)S(1)} %get-tuple-element.70), channel_id=1, source_target_pairs={{0,2},{2,0},{4,8},{6,10},{8,4},{10,6},{12,16},{14,18},{16,12},{18,... | collective-permute-start | bytes 811016 | tf_op jit(solution)/shard_map/ppermute | solution.py:585
  10.9 3.8 %shard_map.104 = (f32[2,32,128]{2,1,0:T(8,128)S(1)}, f32[32,2,32,128]{3,2,1,0:T(8,128)S(1)}, f32[32,2,32,128]{3,2,1,0:T(8,128)S(1)}, f32[32,2,32,128]{3,2,1,0:T(...) custom-call(f32[2048,128]{1,0:T(8,128)S(1)} %get-tuple-element.59.f_, ...), custom_call_target="tpu_custom_call" | custom-call | flops 5242880 | bytes 655360 | tf_op jit(solution)/shard_map/pallas_call | solution.py:538
  15.4 4.3 %collective-permute-done.2.odd_ref = f32[33,16,128]{2,1,0:T(8,128)S(1)} collective-permute-done((f32[33,16,128]{2,1,0:T(8,128)S(1)}, f32[33,16,128]{2,1,0:T(8,128)S(1)}, u32[]{:S(2)}, u32[]{:S(2)}) %collective-permute-start.2) | collective-permute-done | bytes 270368 | tf_op jit(solution)/shard_map/ppermute | solution.py:585
  20.2 2.2 %collective-permute-start.3 = (f32[4,32,128]{2,1,0:T(8,128)S(1)}, f32[4,32,128]{2,1,0:T(8,128)S(1)}, u32[]{:S(2)}, u32[]{:S(2)}) collective-permute-start(f32[4,32,128]{2,1,0:T(8,128)S(1)} %get-tuple-element.72), channel_id=1, source_target_pairs={{0,1},{1,0},{2,3},{3,2},{4,5},{5,4},{6,7},{7,6},{8,9},{9,8},{10,11... | collective-permute-start | bytes 196616 | tf_op jit(solution)/shard_map/ppermute | solution.py:614
  22.5 2.5 %collective-permute-done.3.far_ref = f32[4,32,128]{2,1,0:T(8,128)S(1)} collective-permute-done((f32[4,32,128]{2,1,0:T(8,128)S(1)}, f32[4,32,128]{2,1,0:T(8,128)S(1)}, u32[]{:S(2)}, u32[]{:S(2)}) %collective-permute-start.3) | collective-permute-done | bytes 65568 | tf_op jit(solution)/shard_map/ppermute | solution.py:614
  27.0 1.7 %shard_map.108 = (f32[2,32,128]{2,1,0:T(8,128)S(1)}, f32[32,2,32,128]{3,2,1,0:T(8,128)S(1)}, f32[32,2,32,128]{3,2,1,0:T(8,128)S(1)}, f32[32,16,128]{2,1,0:T(8,128)S(1)}, f32[33,2,8,128]{3,2,1,0:T(8,128)S(1)}) custom-call(f32[32,2,32,128]{3,2,1,0:T(8,128)S(1)} %get-tuple-element.63.pi_ref, f32[4,32,128]{2,1,0:T(8,128)S(1)} %collective-permute-done.3.far_ref, ...), custom_call_target="tpu_custom_call" | custom-call | flops 4718592 | bytes 589824 | tf_op jit(solution)/shard_map/pallas_call | solution.py:538
  28.7 2.2 %collective-permute-start.4 = (f32[2,32,128]{2,1,0:T(8,128)S(1)}, f32[2,32,128]{2,1,0:T(8,128)S(1)}, u32[]{:S(2)}, u32[]{:S(2)}) collective-permute-start(f32[2,32,128]{2,1,0:T(8,128)S(1)} %get-tuple-element.80), channel_id=1, source_target_pairs={{0,1},{1,0},{2,3},{3,2},{4,5},{5,4},{6,7},{7,6},{8,9},{9,8},{10,11... | collective-permute-start | bytes 98312 | tf_op jit(solution)/shard_map/ppermute | solution.py:636
  30.9 2.3 %collective-permute-done.4.inner_ref.far_ref = f32[2,32,128]{2,1,0:T(8,128)S(1)} collective-permute-done((f32[2,32,128]{2,1,0:T(8,128)S(1)}, f32[2,32,128]{2,1,0:T(8,128)S(1)}, u32[]{:S(2)}, u32[]{:S(2)}) %collective-permute-start.4) | collective-permute-done | bytes 32800 | tf_op jit(solution)/shard_map/ppermute | solution.py:636
  35.1 2.2 %collective-permute-start.7 = (f32[2,32,128]{2,1,0:T(8,128)S(1)}, f32[2,32,128]{2,1,0:T(8,128)S(1)}, u32[]{:S(2)}, u32[]{:S(2)}) collective-permute-start(f32[2,32,128]{2,1,0:T(8,128)S(1)} %get-tuple-element.86), channel_id=1, source_target_pairs={{0,1},{1,0},{2,3},{3,2},{4,5},{5,4},{6,7},{7,6},{8,9},{9,8},{10,11... | collective-permute-start | bytes 98312 | tf_op jit(solution)/shard_map/ppermute | solution.py:614
  37.4 2.2 %collective-permute-done.7.far_ref = f32[2,32,128]{2,1,0:T(8,128)S(1)} collective-permute-done((f32[2,32,128]{2,1,0:T(8,128)S(1)}, f32[2,32,128]{2,1,0:T(8,128)S(1)}, u32[]{:S(2)}, u32[]{:S(2)}) %collective-permute-start.7) | collective-permute-done | bytes 32800 | tf_op jit(solution)/shard_map/ppermute | solution.py:614
  40.0 3.4 %collective-permute-start.10 = (f32[32,16,128]{2,1,0:T(8,128)S(1)}, f32[32,16,128]{2,1,0:T(8,128)S(1)}, u32[]{:S(2)}, u32[]{:S(2)}) collective-permute-start(f32[32,16,128]{2,1,0:T(8,128)S(1)} %get-tuple-element.95), channel_id=1, source_target_pairs={{0,2},{2,0},{4,8},{6,10},{8,4},{10,6},{12,16},{14,18},{16,12},{18,... | collective-permute-start | bytes 786440 | tf_op jit(solution)/shard_map/ppermute | solution.py:626
  43.4 1.7 %shard_map.111 = (f32[2,32,128]{2,1,0:T(8,128)S(1)}, f32[32,2,32,128]{3,2,1,0:T(8,128)S(1)}, f32[32,2,32,128]{3,2,1,0:T(8,128)S(1)}, f32[32,16,128]{2,1,0:T(8,128)S(1)}, f32[33,2,8,128]{3,2,1,0:T(8,128)S(1)}) custom-call(f32[32,2,32,128]{3,2,1,0:T(8,128)S(1)} %get-tuple-element.79.pi_ref, f32[2,32,128]{2,1,0:T(8,128)S(1)} %collective-permute-done.4.inner_ref.far_ref, ...), custom_call_target="tpu_custom_call" | custom-call | flops 4718592 | bytes 589824 | tf_op jit(solution)/shard_map/pallas_call | solution.py:538
  46.5 3.0 %collective-permute-done.8.inner_ref.far_ref = f32[2,32,128]{2,1,0:T(8,128)S(1)} collective-permute-done((f32[2,32,128]{2,1,0:T(8,128)S(1)}, f32[2,32,128]{2,1,0:T(8,128)S(1)}, u32[]{:S(2)}, u32[]{:S(2)}) %collective-permute-start.8) | collective-permute-done | bytes 32800 | tf_op jit(solution)/shard_map/ppermute | solution.py:636
  50.1 1.8 %collective-permute-start.11 = (f32[2,32,128]{2,1,0:T(8,128)S(1)}, f32[2,32,128]{2,1,0:T(8,128)S(1)}, u32[]{:S(2)}, u32[]{:S(2)}) collective-permute-start(f32[2,32,128]{2,1,0:T(8,128)S(1)} %get-tuple-element.97), channel_id=1, source_target_pairs={{0,1},{1,0},{2,3},{3,2},{4,5},{5,4},{6,7},{7,6},{8,9},{9,8},{10,11... | collective-permute-start | bytes 98312 | tf_op jit(solution)/shard_map/ppermute | solution.py:614
  51.9 3.3 %collective-permute-done.11.far_ref = f32[2,32,128]{2,1,0:T(8,128)S(1)} collective-permute-done((f32[2,32,128]{2,1,0:T(8,128)S(1)}, f32[2,32,128]{2,1,0:T(8,128)S(1)}, u32[]{:S(2)}, u32[]{:S(2)}) %collective-permute-start.11) | collective-permute-done | bytes 32800 | tf_op jit(solution)/shard_map/ppermute | solution.py:614
  55.6 3.1 %collective-permute-start.14 = (f32[32,16,128]{2,1,0:T(8,128)S(1)}, f32[32,16,128]{2,1,0:T(8,128)S(1)}, u32[]{:S(2)}, u32[]{:S(2)}) collective-permute-start(f32[32,16,128]{2,1,0:T(8,128)S(1)} %get-tuple-element.105), channel_id=1, source_target_pairs={{0,2},{2,0},{4,8},{6,10},{8,4},{10,6},{12,16},{14,18},{16,12},{18,... | collective-permute-start | bytes 786440 | tf_op jit(solution)/shard_map/ppermute | solution.py:626
  58.7 1.7 %shard_map.114 = (f32[2,32,128]{2,1,0:T(8,128)S(1)}, f32[32,2,32,128]{3,2,1,0:T(8,128)S(1)}, f32[32,2,32,128]{3,2,1,0:T(8,128)S(1)}, f32[32,16,128]{2,1,0:T(8,128)S(1)}, f32[33,2,8,128]{3,2,1,0:T(8,128)S(1)}) custom-call(f32[32,2,32,128]{3,2,1,0:T(8,128)S(1)} %get-tuple-element.90.pi_ref, f32[2,32,128]{2,1,0:T(8,128)S(1)} %collective-permute-done.8.inner_ref.far_ref, ...), custom_call_target="tpu_custom_call" | custom-call | flops 4718592 | bytes 589824 | tf_op jit(solution)/shard_map/pallas_call | solution.py:538
  61.4 3.3 %collective-permute-done.12.inner_ref.fari_ref = f32[2,32,128]{2,1,0:T(8,128)S(1)} collective-permute-done((f32[2,32,128]{2,1,0:T(8,128)S(1)}, f32[2,32,128]{2,1,0:T(8,128)S(1)}, u32[]{:S(2)}, u32[]{:S(2)}) %collective-permute-start.12) | collective-permute-done | bytes 32800 | tf_op jit(solution)/shard_map/ppermute | solution.py:636
  65.8 1.7 %collective-permute-start.15 = (f32[2,32,128]{2,1,0:T(8,128)S(1)}, f32[2,32,128]{2,1,0:T(8,128)S(1)}, u32[]{:S(2)}, u32[]{:S(2)}) collective-permute-start(f32[2,32,128]{2,1,0:T(8,128)S(1)} %get-tuple-element.108), channel_id=1, source_target_pairs={{0,1},{1,0},{2,3},{3,2},{4,5},{5,4},{6,7},{7,6},{8,9},{9,8},{10,11... | collective-permute-start | bytes 98312 | tf_op jit(solution)/shard_map/ppermute | solution.py:614
  67.5 2.8 %collective-permute-done.15.fare_ref = f32[2,32,128]{2,1,0:T(8,128)S(1)} collective-permute-done((f32[2,32,128]{2,1,0:T(8,128)S(1)}, f32[2,32,128]{2,1,0:T(8,128)S(1)}, u32[]{:S(2)}, u32[]{:S(2)}) %collective-permute-start.15) | collective-permute-done | bytes 32800 | tf_op jit(solution)/shard_map/ppermute | solution.py:614
  70.8 10.1 %collective-permute-start.16 = (f32[32,4,128]{2,1,0:T(4,128)S(1)}, f32[32,4,128]{2,1,0:T(4,128)S(1)}, u32[]{:S(2)}, u32[]{:S(2)}) collective-permute-start(f32[32,4,128]{2,1,0:T(4,128)S(1)} %get-tuple-element.114), channel_id=1, source_target_pairs={{0,2},{2,0},{1,3},{3,1},{4,6},{6,4},{5,7},{7,5},{8,10},{10,8},{9,1... | collective-permute-start | bytes 196616 | tf_op jit(solution)/shard_map/ppermute | solution.py:653
  (34 shorter events, 13.1 us)
Async XLA Ops:
  0.6 10.2 %copy-start.2 = (s32[128]{0:T(128)S(1)}, s32[128]{0:T(128)}, u32[]{:S(2)}) copy-start(s32[128]{0:T(128)} %param.15) | copy-start | bytes 1540
  0.6 10.2 %copy-start.3 = (s32[4,128]{1,0:T(4,128)S(1)}, s32[4,128]{1,0:T(4,128)}, u32[]{:S(2)}) copy-start(s32[4,128]{1,0:T(4,128)} %color_ref.1) | copy-start | bytes 6148
  0.7 10.2 %copy-start = (f32[63,4,128]{2,1,0:T(4,128)S(1)}, f32[63,4,128]{2,1,0:T(4,128)}, u32[]{:S(2)}) copy-start(f32[63,4,128]{2,1,0:T(4,128)} %mix_ref.1) | copy-start | bytes 387076
  0.7 10.2 %copy-start.1 = (f32[32,4,128]{2,1,0:T(4,128)S(1)}, f32[32,4,128]{2,1,0:T(4,128)}, u32[]{:S(2)}) copy-start(f32[32,4,128]{2,1,0:T(4,128)} %ef_ref.1) | copy-start | bytes 196612
  0.7 8.1 %collective-permute-start = (f32[32,4,128]{2,1,0:T(4,128)}, f32[32,4,128]{2,1,0:T(4,128)S(1)}, u32[]{:S(2)}, u32[]{:S(2)}) collective-permute-start(f32[32,4,128]{2,1,0:T(4,128)} %nf_hbm.1), channel_id=1, source_target_pairs={{0,4},{4,8},{8,12},{12,16},{16,20},{20,24},{24,28},{28,32},{32,36}... | collective-permute-start | bytes 196616 | tf_op jit(solution)/shard_map/ppermute | solution.py:566
  8.9 6.5 %collective-permute-start.1 = (f32[33,16,128]{2,1,0:T(8,128)S(1)}, f32[33,16,128]{2,1,0:T(8,128)S(1)}, u32[]{:S(2)}, u32[]{:S(2)}) collective-permute-start(f32[33,16,128]{2,1,0:T(8,128)S(1)} %get-tuple-element.69), channel_id=1, source_target_pairs={{0,4},{2,6},{4,0},{6,2},{8,12},{10,14},{12,8},{14,10},{16,20},{18,... | collective-permute-start | bytes 811016 | tf_op jit(solution)/shard_map/ppermute | solution.py:586
  9.0 10.7 %collective-permute-start.2 = (f32[33,16,128]{2,1,0:T(8,128)S(1)}, f32[33,16,128]{2,1,0:T(8,128)S(1)}, u32[]{:S(2)}, u32[]{:S(2)}) collective-permute-start(f32[33,16,128]{2,1,0:T(8,128)S(1)} %get-tuple-element.70), channel_id=1, source_target_pairs={{0,2},{2,0},{4,8},{6,10},{8,4},{10,6},{12,16},{14,18},{16,12},{18,... | collective-permute-start | bytes 811016 | tf_op jit(solution)/shard_map/ppermute | solution.py:585
  20.2 4.7 %collective-permute-start.3 = (f32[4,32,128]{2,1,0:T(8,128)S(1)}, f32[4,32,128]{2,1,0:T(8,128)S(1)}, u32[]{:S(2)}, u32[]{:S(2)}) collective-permute-start(f32[4,32,128]{2,1,0:T(8,128)S(1)} %get-tuple-element.72), channel_id=1, source_target_pairs={{0,1},{1,0},{2,3},{3,2},{4,5},{5,4},{6,7},{7,6},{8,9},{9,8},{10,11... | collective-permute-start | bytes 196616 | tf_op jit(solution)/shard_map/ppermute | solution.py:614
  25.2 8.0 %collective-permute-start.5 = (f32[32,16,128]{2,1,0:T(8,128)S(1)}, f32[32,16,128]{2,1,0:T(8,128)S(1)}, u32[]{:S(2)}, u32[]{:S(2)}) collective-permute-start(f32[32,16,128]{2,1,0:T(8,128)S(1)} %get-tuple-element.83), channel_id=1, source_target_pairs={{0,4},{2,6},{4,0},{6,2},{8,12},{10,14},{12,8},{14,10},{16,20},{18,... | collective-permute-start | bytes 786440 | tf_op jit(solution)/shard_map/ppermute | solution.py:627
  25.3 9.5 %collective-permute-start.6 = (f32[32,16,128]{2,1,0:T(8,128)S(1)}, f32[32,16,128]{2,1,0:T(8,128)S(1)}, u32[]{:S(2)}, u32[]{:S(2)}) collective-permute-start(f32[32,16,128]{2,1,0:T(8,128)S(1)} %get-tuple-element.84), channel_id=1, source_target_pairs={{0,2},{2,0},{4,8},{6,10},{8,4},{10,6},{12,16},{14,18},{16,12},{18,... | collective-permute-start | bytes 786440 | tf_op jit(solution)/shard_map/ppermute | solution.py:626
  28.7 4.5 %collective-permute-start.4 = (f32[2,32,128]{2,1,0:T(8,128)S(1)}, f32[2,32,128]{2,1,0:T(8,128)S(1)}, u32[]{:S(2)}, u32[]{:S(2)}) collective-permute-start(f32[2,32,128]{2,1,0:T(8,128)S(1)} %get-tuple-element.80), channel_id=1, source_target_pairs={{0,1},{1,0},{2,3},{3,2},{4,5},{5,4},{6,7},{7,6},{8,9},{9,8},{10,11... | collective-permute-start | bytes 98312 | tf_op jit(solution)/shard_map/ppermute | solution.py:636
  35.1 4.4 %collective-permute-start.7 = (f32[2,32,128]{2,1,0:T(8,128)S(1)}, f32[2,32,128]{2,1,0:T(8,128)S(1)}, u32[]{:S(2)}, u32[]{:S(2)}) collective-permute-start(f32[2,32,128]{2,1,0:T(8,128)S(1)} %get-tuple-element.86), channel_id=1, source_target_pairs={{0,1},{1,0},{2,3},{3,2},{4,5},{5,4},{6,7},{7,6},{8,9},{9,8},{10,11... | collective-permute-start | bytes 98312 | tf_op jit(solution)/shard_map/ppermute | solution.py:614
  39.9 9.6 %collective-permute-start.9 = (f32[32,16,128]{2,1,0:T(8,128)S(1)}, f32[32,16,128]{2,1,0:T(8,128)S(1)}, u32[]{:S(2)}, u32[]{:S(2)}) collective-permute-start(f32[32,16,128]{2,1,0:T(8,128)S(1)} %get-tuple-element.94), channel_id=1, source_target_pairs={{0,4},{2,6},{4,0},{6,2},{8,12},{10,14},{12,8},{14,10},{16,20},{18,... | collective-permute-start | bytes 786440 | tf_op jit(solution)/shard_map/ppermute | solution.py:627
  40.0 9.9 %collective-permute-start.10 = (f32[32,16,128]{2,1,0:T(8,128)S(1)}, f32[32,16,128]{2,1,0:T(8,128)S(1)}, u32[]{:S(2)}, u32[]{:S(2)}) collective-permute-start(f32[32,16,128]{2,1,0:T(8,128)S(1)} %get-tuple-element.95), channel_id=1, source_target_pairs={{0,2},{2,0},{4,8},{6,10},{8,4},{10,6},{12,16},{14,18},{16,12},{18,... | collective-permute-start | bytes 786440 | tf_op jit(solution)/shard_map/ppermute | solution.py:626
  45.1 4.3 %collective-permute-start.8 = (f32[2,32,128]{2,1,0:T(8,128)S(1)}, f32[2,32,128]{2,1,0:T(8,128)S(1)}, u32[]{:S(2)}, u32[]{:S(2)}) collective-permute-start(f32[2,32,128]{2,1,0:T(8,128)S(1)} %get-tuple-element.91), channel_id=1, source_target_pairs={{0,1},{1,0},{2,3},{3,2},{4,5},{5,4},{6,7},{7,6},{8,9},{9,8},{10,11... | collective-permute-start | bytes 98312 | tf_op jit(solution)/shard_map/ppermute | solution.py:636
  50.1 5.1 %collective-permute-start.11 = (f32[2,32,128]{2,1,0:T(8,128)S(1)}, f32[2,32,128]{2,1,0:T(8,128)S(1)}, u32[]{:S(2)}, u32[]{:S(2)}) collective-permute-start(f32[2,32,128]{2,1,0:T(8,128)S(1)} %get-tuple-element.97), channel_id=1, source_target_pairs={{0,1},{1,0},{2,3},{3,2},{4,5},{5,4},{6,7},{7,6},{8,9},{9,8},{10,11... | collective-permute-start | bytes 98312 | tf_op jit(solution)/shard_map/ppermute | solution.py:614
  55.5 9.2 %collective-permute-start.13 = (f32[32,16,128]{2,1,0:T(8,128)S(1)}, f32[32,16,128]{2,1,0:T(8,128)S(1)}, u32[]{:S(2)}, u32[]{:S(2)}) collective-permute-start(f32[32,16,128]{2,1,0:T(8,128)S(1)} %get-tuple-element.104), channel_id=1, source_target_pairs={{0,4},{2,6},{4,0},{6,2},{8,12},{10,14},{12,8},{14,10},{16,20},{18,... | collective-permute-start | bytes 786440 | tf_op jit(solution)/shard_map/ppermute | solution.py:627
  55.6 9.9 %collective-permute-start.14 = (f32[32,16,128]{2,1,0:T(8,128)S(1)}, f32[32,16,128]{2,1,0:T(8,128)S(1)}, u32[]{:S(2)}, u32[]{:S(2)}) collective-permute-start(f32[32,16,128]{2,1,0:T(8,128)S(1)} %get-tuple-element.105), channel_id=1, source_target_pairs={{0,2},{2,0},{4,8},{6,10},{8,4},{10,6},{12,16},{14,18},{16,12},{18,... | collective-permute-start | bytes 786440 | tf_op jit(solution)/shard_map/ppermute | solution.py:626
  60.4 4.3 %collective-permute-start.12 = (f32[2,32,128]{2,1,0:T(8,128)S(1)}, f32[2,32,128]{2,1,0:T(8,128)S(1)}, u32[]{:S(2)}, u32[]{:S(2)}) collective-permute-start(f32[2,32,128]{2,1,0:T(8,128)S(1)} %get-tuple-element.101), channel_id=1, source_target_pairs={{0,1},{1,0},{2,3},{3,2},{4,5},{5,4},{6,7},{7,6},{8,9},{9,8},{10,11... | collective-permute-start | bytes 98312 | tf_op jit(solution)/shard_map/ppermute | solution.py:636
  65.8 4.5 %collective-permute-start.15 = (f32[2,32,128]{2,1,0:T(8,128)S(1)}, f32[2,32,128]{2,1,0:T(8,128)S(1)}, u32[]{:S(2)}, u32[]{:S(2)}) collective-permute-start(f32[2,32,128]{2,1,0:T(8,128)S(1)} %get-tuple-element.108), channel_id=1, source_target_pairs={{0,1},{1,0},{2,3},{3,2},{4,5},{5,4},{6,7},{7,6},{8,9},{9,8},{10,11... | collective-permute-start | bytes 98312 | tf_op jit(solution)/shard_map/ppermute | solution.py:614
  70.8 11.6 %collective-permute-start.16 = (f32[32,4,128]{2,1,0:T(4,128)S(1)}, f32[32,4,128]{2,1,0:T(4,128)S(1)}, u32[]{:S(2)}, u32[]{:S(2)}) collective-permute-start(f32[32,4,128]{2,1,0:T(4,128)S(1)} %get-tuple-element.114), channel_id=1, source_target_pairs={{0,2},{2,0},{1,3},{3,1},{4,6},{6,4},{5,7},{7,5},{8,10},{10,8},{9,1... | collective-permute-start | bytes 196616 | tf_op jit(solution)/shard_map/ppermute | solution.py:653
